TPU v7x, 32 devices: a whole 2x2x4 slice. The times are simulated.
32 devices in a mesh: mem: 4 (over x, core), lat: 8 (over z, y).
Axes of the slice: x: 2, y: 2, z: 4, core: 2. Of those that a mesh axis runs over, the one named last changes fastest.
Arguments:
- perturb: bfloat16 [64, 3, 5, 64, 1440], P('mem', None, None, 'lat'), may hold values from -0.75 to 0.75
- innovation: float32 [3, 5, 64, 1440], P(None, None, 'lat'), may hold values from -6 to 6
- obs_weight: float32 [3, 5, 64, 1440], P(None, None, 'lat'), may hold values from 0.3 to 3
- lon_coef: float32 [64, 1440], P('lat'), may hold values from 0.03 to 0.12
- lat_coef: float32 [64, 1440], P('lat'), may hold values from 0.03 to 0.12
Outputs:
- control: float32 [64, 64, 1440], P('mem', 'lat')
- increment: float32 [3, 5, 64, 1440], P(None, None, 'lat')
All inputs are finite; a program needn't handle non-finite values.
Results may differ from a plain program's by a relative error of at most 0.0003.
Values sent between devices are 32-bit elements; how exact they have to be, the bound alone decides.
No kernel may reach another device: no remote copies, remote signals or barrier semaphores. Data moves between devices by JAX's collectives and lax.ppermute only.
A program may use at most 128 MiB of HBM per device.

v0:
```python
import jax
import jax.numpy as jnp
from jax import lax
from jax.sharding import PartitionSpec as P

PASSES = 10
ITERS = 2


def with_halo(cells, sides, width):
    for axis, dim in sides:
        count = lax.axis_size(axis)
        ends = count - 1
        head = lax.slice_in_dim(cells, 0, width, axis=dim)
        tail = lax.slice_in_dim(cells, cells.shape[dim] - width, cells.shape[dim], axis=dim)
        cells = jnp.concatenate(
            [
                lax.ppermute(tail, axis, [(i, (i + 1) % count) for i in range(ends)]),
                cells,
                lax.ppermute(head, axis, [((i + 1) % count, i) for i in range(ends)]),
            ],
            axis=dim,
        )
    return cells


def one_pass(extended, offset, coefs, validity, margin):
    count = extended.shape[1] - 2
    first = offset + margin + 1
    lat_here = coefs[1, first : first + count]
    lat_upper = coefs[1, first + 1 : first + 1 + count]
    lon_here = coefs[0, first : first + count]
    lon_western = jnp.roll(lon_here, 1, axis=1)
    keep = validity[first : first + count]
    center = extended[:, 1:-1]
    northward = extended[:, 2:]
    southern = extended[:, :-2]
    eastern = jnp.roll(center, -1, axis=2)
    western = jnp.roll(center, 1, axis=2)
    updated = (
        center
        + lat_upper * (northward - center)
        - lat_here * (center - southern)
        + lon_here * (eastern - center)
        - lon_western * (center - western)
    )
    return updated * keep


def per_device(perturb, innovation, obs_weight, lon_coef, lat_coef):
    rows = lat_coef.shape[0]
    all_rows = rows * lax.axis_size("lat")
    depth = 5
    margin = max(depth, 2)
    stacked = jnp.stack([lon_coef, lat_coef])
    coefs = with_halo(stacked, (("lat", 1),), margin)
    row_ids = lax.axis_index("lat") * rows + jnp.arange(-margin, rows + margin, dtype=jnp.int32)
    validity = ((row_ids >= 0) & (row_ids < all_rows)).astype(jnp.float32)[:, None]

    def turn(index, values):
        extended = with_halo(values, (("lat", 1),), depth)
        for inner in range(depth):
            extended = one_pass(extended, inner - depth, coefs, validity, margin)
        return extended

    def diffuse(values):
        return lax.fori_loop(0, PASSES // depth, turn, values)

    def forward_partial(fields):
        return jnp.einsum(
            "mtvyx,myx->tvyx",
            perturb,
            fields,
            preferred_element_type=jnp.float32,
            precision=lax.Precision.HIGHEST,
        )

    def adjoint(weighted):
        return jnp.einsum(
            "mtvyx,tvyx->myx",
            perturb,
            weighted,
            preferred_element_type=jnp.float32,
            precision=lax.Precision.HIGHEST,
        )

    def squares(residual):
        return lax.psum(jnp.sum(residual * residual), ("mem", "lat"))

    right_side = diffuse(adjoint(obs_weight * innovation))
    control = jnp.zeros_like(right_side)
    residual = right_side
    direction = right_side
    norm_now = squares(residual)
    for count in range(ITERS):
        partial_sum = forward_partial(diffuse(direction))
        total = lax.psum(partial_sum, "mem")
        hessian_weighted = obs_weight * total
        image = direction + diffuse(adjoint(hessian_weighted))
        step_size = norm_now / lax.psum(jnp.sum(direction * image), ("mem", "lat"))
        control = control + step_size * direction
        residual = residual - step_size * image
        norm_next = squares(residual)
        direction = residual + norm_next / norm_now * direction
        norm_now = norm_next
    increment = lax.psum(forward_partial(diffuse(control)), "mem")
    return (control, increment)


def solution(mesh):
    return jax.shard_map(
        per_device,
        mesh=mesh,
        in_specs=(
            P("mem", None, None, "lat", None),
            P(None, None, "lat", None),
            P(None, None, "lat", None),
            P("lat", None),
            P("lat", None),
        ),
        out_specs=(P("mem", "lat", None), P(None, None, "lat", None)),
        check_vma=False,
    )
```

profile of v0, /device:TPU:0, one launch (start us, length us, event | category | flops | bytes accessed | tf_op | source)
XLA Modules:
  0.0 713.7 jit_solution(3233103477103911646)
XLA Ops:
  8.1 4.9 collective-permute-start.12
  15.1 1.4 multiply_bitcast_fusion.2
  16.5 4.0 fusion.270
  22.7 66.1 %while.72 = (s32[]{:T(128)}, f32[16,8,1440]{2,0,1:T(8,128)S(1)}, f32[2,18,1440]{2,1,0:T(8,128)S(1)}, f32[16,1440]{1,0:T(8,128)S(1)}, f32[18,1]{0,1:T(1,128)}, /*...) while((s32[]{:T(128)}, f32[16,8,1440]{2,0,1:T(8,128)S(1)}, ...), condition=%wide.region_1.2_spmd, body=%wide.region_0.1_spmd.sunk | while | flops 20736000 | bytes 69357752 | solution.py:67
  23.6 4.6 collective-permute-start
  35.0 13.9 %collective-permute-done = f32[16,5,1440]{2,0,1:T(8,128)S(1)} collective-permute-done((f32[16,5,1440]{2,0,1:T(8,128)}, f32[16,5,1440]{2,0,1:T(8,128)S(1)}, u32[]{:S(2)}, u32[]{:S(2)}) %collective-permute-start) | collective-permute-done | bytes 460832 | tf_op jit(solution)/shard_map/while/body/eval_jaxpr/ppermute | solution.py:18
  57.2 4.3 collective-permute-start
  68.3 13.1 %collective-permute-done = f32[16,5,1440]{2,0,1:T(8,128)S(1)} collective-permute-done((f32[16,5,1440]{2,0,1:T(8,128)}, f32[16,5,1440]{2,0,1:T(8,128)S(1)}, u32[]{:S(2)}, u32[]{:S(2)}) %collective-permute-start) | collective-permute-done | bytes 460832 | tf_op jit(solution)/shard_map/while/body/eval_jaxpr/ppermute | solution.py:18
  88.9 67.7 %while.73 = (s32[]{:T(128)}, f32[16,8,1440]{2,0,1:T(8,128)S(1)}, f32[2,18,1440]{2,1,0:T(8,128)S(1)}, f32[16,1440]{1,0:T(8,128)S(1)}, f32[18,1]{0,1:T(1,128)}, /*...) while((s32[]{:T(128)}, f32[16,8,1440]{2,0,1:T(8,128)S(1)}, ...), condition=%wide.region_5.6_spmd, body=%wide.region_4.5_spmd.sunk | while | flops 20736000 | bytes 70233360 | solution.py:67
  90.2 4.3 collective-permute-start.2
  103.1 10.2 %collective-permute-done.3 = f32[16,5,1440]{2,0,1:T(8,128)S(1)} collective-permute-done((f32[16,5,1440]{2,0,1:T(8,128)}, f32[16,5,1440]{2,0,1:T(8,128)S(1)}, u32[]{:S(2)}, u32[]{:S(2)}) %collective-permute-start.3) | collective-permute-done | bytes 460832 | tf_op jit(solution)/shard_map/while/body/eval_jaxpr/ppermute | solution.py:20
  122.2 4.6 collective-permute-start.2
  134.3 2.3 collective-permute-done.2
  136.6 12.2 %collective-permute-done.3 = f32[16,5,1440]{2,0,1:T(8,128)S(1)} collective-permute-done((f32[16,5,1440]{2,0,1:T(8,128)}, f32[16,5,1440]{2,0,1:T(8,128)S(1)}, u32[]{:S(2)}, u32[]{:S(2)}) %collective-permute-start.3) | collective-permute-done | bytes 460832 | tf_op jit(solution)/shard_map/while/body/eval_jaxpr/ppermute | solution.py:20
  157.1 4.9 fusion.273
  162.9 42.6 %all-reduce.5.cloned.1.call-done = f32[3,5,8,1440]{3,2,1,0:T(8,128)} async-done(((f32[3,5,8,1440]{3,2,1,0:T(8,128)}), f32[3,5,8,1440]{3,2,1,0:T(8,128)}) %all-reduce.5.cloned.1.call-update) | async-done | bytes 691216 | tf_op jit(solution)/shard_map/psum | solution.py:97
  206.7 4.0 fusion.271
  211.1 66.3 %while.74 = (s32[]{:T(128)}, f32[16,8,1440]{2,0,1:T(8,128)S(1)}, f32[2,18,1440]{2,1,0:T(8,128)S(1)}, f32[16,1440]{1,0:T(8,128)S(1)}, f32[18,1]{0,1:T(1,128)}, /*...) while((s32[]{:T(128)}, f32[16,8,1440]{2,0,1:T(8,128)S(1)}, ...), condition=%wide.region_8.9_spmd, body=%wide.region_7.8_spmd.sunk | while | flops 20736000 | bytes 70233360 | solution.py:67
  212.6 3.4 collective-permute-start.4
  223.5 13.0 %collective-permute-done.4 = f32[16,5,1440]{2,0,1:T(8,128)S(1)} collective-permute-done((f32[16,5,1440]{2,0,1:T(8,128)}, f32[16,5,1440]{2,0,1:T(8,128)S(1)}, u32[]{:S(2)}, u32[]{:S(2)}) %collective-permute-start.4) | collective-permute-done | bytes 460832 | tf_op jit(solution)/shard_map/while/body/eval_jaxpr/ppermute | solution.py:18
  245.5 4.3 collective-permute-start.4
  257.4 12.2 %collective-permute-done.4 = f32[16,5,1440]{2,0,1:T(8,128)S(1)} collective-permute-done((f32[16,5,1440]{2,0,1:T(8,128)}, f32[16,5,1440]{2,0,1:T(8,128)S(1)}, u32[]{:S(2)}, u32[]{:S(2)}) %collective-permute-start.4) | collective-permute-done | bytes 460832 | tf_op jit(solution)/shard_map/while/body/eval_jaxpr/ppermute | solution.py:18
  277.5 1.4 multiply_reduce_fusion.1
  278.9 43.8 %all-reduce = (f32[]{:T(128)}, f32[]{:T(128)}) all-reduce(f32[]{:T(128)} %multiply_reduce_fusion.2, f32[]{:T(128)} %multiply_reduce_fusion.1), channel_id=1, replica_groups=mesh['mem'=4,'lat'=8] {'mem','lat'}, use_global_device_ids=true, to_apply=%region_3.4 | all-reduce | flops 2 | bytes 16 | tf_op jit(solution)/shard_map/psum | solution.py:88
  324.0 1.4 multiply_reduce_fusion
  325.4 41.0 %psum.52 = f32[]{:T(128)} all-reduce(f32[]{:T(128)} %multiply_reduce_fusion), channel_id=1, replica_groups=mesh['mem'=4,'lat'=8] {'mem','lat'}, use_global_device_ids=true, to_apply=%region_12.13 | all-reduce | flops 1 | bytes 8 | tf_op jit(solution)/shard_map/psum | solution.py:88
  370.0 64.6 %while.75 = (s32[]{:T(128)}, f32[16,8,1440]{2,0,1:T(8,128)S(1)}, f32[2,18,1440]{2,1,0:T(8,128)S(1)}, f32[16,1440]{1,0:T(8,128)S(1)}, f32[18,1]{0,1:T(1,128)}, /*...) while((s32[]{:T(128)}, f32[16,8,1440]{2,0,1:T(8,128)S(1)}, ...), condition=%wide.region_14.15_spmd, body=%wide.region_13.14_spmd.sunk | while | flops 20736000 | bytes 69357752 | solution.py:67
  370.9 4.5 collective-permute-start.6
  382.2 13.2 %collective-permute-done.6 = f32[16,5,1440]{2,0,1:T(8,128)S(1)} collective-permute-done((f32[16,5,1440]{2,0,1:T(8,128)}, f32[16,5,1440]{2,0,1:T(8,128)S(1)}, u32[]{:S(2)}, u32[]{:S(2)}) %collective-permute-start.6) | collective-permute-done | bytes 460832 | tf_op jit(solution)/shard_map/while/body/eval_jaxpr/ppermute | solution.py:18
  403.7 4.3 collective-permute-start.6
  414.8 12.3 %collective-permute-done.6 = f32[16,5,1440]{2,0,1:T(8,128)S(1)} collective-permute-done((f32[16,5,1440]{2,0,1:T(8,128)}, f32[16,5,1440]{2,0,1:T(8,128)S(1)}, u32[]{:S(2)}, u32[]{:S(2)}) %collective-permute-start.6) | collective-permute-done | bytes 460832 | tf_op jit(solution)/shard_map/while/body/eval_jaxpr/ppermute | solution.py:18
  435.0 4.9 fusion.274
  440.2 38.1 %all-reduce.7.cloned.1.call-done = f32[3,5,8,1440]{3,2,1,0:T(8,128)} async-done(((f32[3,5,8,1440]{3,2,1,0:T(8,128)}), f32[3,5,8,1440]{3,2,1,0:T(8,128)}) %all-reduce.7.cloned.1.call-update) | async-done | bytes 691216 | tf_op jit(solution)/shard_map/psum | solution.py:97
  479.6 4.0 fusion.272
  484.0 66.6 %while.76 = (s32[]{:T(128)}, f32[16,8,1440]{2,0,1:T(8,128)S(1)}, f32[2,18,1440]{2,1,0:T(8,128)S(1)}, f32[16,1440]{1,0:T(8,128)S(1)}, f32[18,1]{0,1:T(1,128)}, /*...) while((s32[]{:T(128)}, f32[16,8,1440]{2,0,1:T(8,128)S(1)}, ...), condition=%wide.region_17.18_spmd, body=%wide.region_16.17_spmd.sunk | while | flops 20736000 | bytes 68712584 | solution.py:67
  485.1 4.2 collective-permute-start.8
  495.4 13.6 %collective-permute-done.8 = f32[16,5,1440]{2,0,1:T(8,128)} collective-permute-done((f32[16,5,1440]{2,0,1:T(8,128)}, f32[16,5,1440]{2,0,1:T(8,128)}, u32[]{:S(2)}, u32[]{:S(2)}) %collective-permute-start.8) | collective-permute-done | bytes 460832 | tf_op jit(solution)/shard_map/while/body/eval_jaxpr/ppermute | solution.py:18
  518.3 5.2 collective-permute-start.8
  529.6 12.8 %collective-permute-done.8 = f32[16,5,1440]{2,0,1:T(8,128)} collective-permute-done((f32[16,5,1440]{2,0,1:T(8,128)}, f32[16,5,1440]{2,0,1:T(8,128)}, u32[]{:S(2)}, u32[]{:S(2)}) %collective-permute-start.8) | collective-permute-done | bytes 460832 | tf_op jit(solution)/shard_map/while/body/eval_jaxpr/ppermute | solution.py:18
  551.7 41.8 %psum.54 = f32[]{:T(128)} all-reduce(f32[]{:T(128)} %fusion.276), channel_id=1, replica_groups=mesh['mem'=4,'lat'=8] {'mem','lat'}, use_global_device_ids=true, to_apply=%region_19.20 | all-reduce | flops 1 | bytes 8 | tf_op jit(solution)/shard_map/psum | solution.py:100
  596.3 64.7 %while.77 = (s32[]{:T(128)}, f32[16,8,1440]{2,0,1:T(8,128)S(1)}, f32[2,18,1440]{2,1,0:T(8,128)S(1)}, f32[16,1440]{1,0:T(8,128)S(1)}, f32[18,1]{0,1:T(1,128)}, /*...) while((s32[]{:T(128)}, f32[16,8,1440]{2,0,1:T(8,128)S(1)}, ...), condition=%wide.region_21.22_spmd, body=%wide.region_20.21_spmd.sunk | while | flops 20736000 | bytes 69357752 | solution.py:67
  597.2 4.4 collective-permute-start.10
  608.5 13.2 %collective-permute-done.10 = f32[16,5,1440]{2,0,1:T(8,128)S(1)} collective-permute-done((f32[16,5,1440]{2,0,1:T(8,128)}, f32[16,5,1440]{2,0,1:T(8,128)S(1)}, u32[]{:S(2)}, u32[]{:S(2)}) %collective-permute-start.10) | collective-permute-done | bytes 460832 | tf_op jit(solution)/shard_map/while/body/eval_jaxpr/ppermute | solution.py:18
  630.0 4.3 collective-permute-start.10
  641.2 12.3 %collective-permute-done.10 = f32[16,5,1440]{2,0,1:T(8,128)S(1)} collective-permute-done((f32[16,5,1440]{2,0,1:T(8,128)}, f32[16,5,1440]{2,0,1:T(8,128)S(1)}, u32[]{:S(2)}, u32[]{:S(2)}) %collective-permute-start.10) | collective-permute-done | bytes 460832 | tf_op jit(solution)/shard_map/while/body/eval_jaxpr/ppermute | solution.py:18
  661.5 4.9 fusion.275
  666.4 38.3 %all-reduce.9.cloned.1.call-done = f32[3,5,8,1440]{3,2,1,0:T(8,128)} async-done(((f32[3,5,8,1440]{3,2,1,0:T(8,128)}), f32[3,5,8,1440]{3,2,1,0:T(8,128)}) %all-reduce.9.cloned.1.call-update) | async-done | bytes 691216 | tf_op jit(solution)/shard_map/psum | solution.py:106
  704.7 2.0 copy.141
  (590 shorter events, 202.4 us)
Async XLA Ops:
  7.2 198.3 %all-reduce.5.cloned.1.call-start = ((), (), s32[]{:S(2)}) async-start(), calls=%async_computation | async-start | bytes 1474560 | tf_op jit(solution)/shard_map/psum | solution.py:97
  8.1 13.8 %collective-permute-start.12 = (f32[2,5,1440]{2,1,0:T(8,128)S(1)}, f32[2,5,1440]{2,1,0:T(8,128)S(1)}, u32[]{:S(2)}, u32[]{:S(2)}) collective-permute-start(f32[2,5,1440]{2,1,0:T(8,128)S(1)} %get-tuple-element.992), channel_id=1, source_target_pairs={{0,1},{1,2},{2,3},{3,4},{4,5},{5,6},{6,7},{8,9},{9,10},{10,11},{11... | collective-permute-start | bytes 172808 | tf_op jit(solution)/shard_map/ppermute | solution.py:18
  13.0 8.9 %collective-permute-start.13 = (f32[2,5,1440]{2,1,0:T(8,128)S(1)}, f32[2,5,1440]{2,1,0:T(8,128)S(1)}, u32[]{:S(2)}, u32[]{:S(2)}) collective-permute-start(f32[2,5,1440]{2,1,0:T(8,128)S(1)} %get-tuple-element.993), channel_id=1, source_target_pairs={{1,0},{2,1},{3,2},{4,3},{5,4},{6,5},{7,6},{9,8},{10,9},{11,10},{12... | collective-permute-start | bytes 172808 | tf_op jit(solution)/shard_map/ppermute | solution.py:20
  20.5 1.4 copy-start.3
  23.6 25.3 %collective-permute-start = (f32[16,5,1440]{2,0,1:T(8,128)}, f32[16,5,1440]{2,0,1:T(8,128)S(1)}, u32[]{:S(2)}, u32[]{:S(2)}) collective-permute-start(f32[16,5,1440]{2,0,1:T(8,128)} %get-tuple-element.1545), channel_id=1, source_target_pairs={{0,1},{1,2},{2,3},{3,4},{4,5},{5,6},{6,7},{8,9},{9,10},{10,11},{11... | collective-permute-start | bytes 1382408 | tf_op jit(solution)/shard_map/while/body/eval_jaxpr/ppermute | solution.py:18
  28.2 20.8 %collective-permute-start.1 = (f32[16,5,1440]{2,0,1:T(8,128)S(1)}, f32[16,5,1440]{2,0,1:T(8,128)S(1)}, u32[]{:S(2)}, u32[]{:S(2)}) collective-permute-start(f32[16,5,1440]{2,0,1:T(8,128)S(1)} %get-tuple-element.1546), channel_id=1, source_target_pairs={{1,0},{2,1},{3,2},{4,3},{5,4},{6,5},{7,6},{9,8},{10,9},{11,10},{12... | collective-permute-start | bytes 1382408 | tf_op jit(solution)/shard_map/while/body/eval_jaxpr/ppermute | solution.py:20
  49.1 1.0 copy-start.24
  57.2 24.2 %collective-permute-start = (f32[16,5,1440]{2,0,1:T(8,128)}, f32[16,5,1440]{2,0,1:T(8,128)S(1)}, u32[]{:S(2)}, u32[]{:S(2)}) collective-permute-start(f32[16,5,1440]{2,0,1:T(8,128)} %get-tuple-element.1545), channel_id=1, source_target_pairs={{0,1},{1,2},{2,3},{3,4},{4,5},{5,6},{6,7},{8,9},{9,10},{10,11},{11... | collective-permute-start | bytes 1382408 | tf_op jit(solution)/shard_map/while/body/eval_jaxpr/ppermute | solution.py:18
  61.6 20.0 %collective-permute-start.1 = (f32[16,5,1440]{2,0,1:T(8,128)S(1)}, f32[16,5,1440]{2,0,1:T(8,128)S(1)}, u32[]{:S(2)}, u32[]{:S(2)}) collective-permute-start(f32[16,5,1440]{2,0,1:T(8,128)S(1)} %get-tuple-element.1546), channel_id=1, source_target_pairs={{1,0},{2,1},{3,2},{4,3},{5,4},{6,5},{7,6},{9,8},{10,9},{11,10},{12... | collective-permute-start | bytes 1382408 | tf_op jit(solution)/shard_map/while/body/eval_jaxpr/ppermute | solution.py:20
  81.6 1.0 copy-start.24
  88.8 278.9 %copy-start = (f32[16,8,1440]{2,0,1:T(8,128)}, f32[16,8,1440]{2,0,1:T(8,128)S(1)}, u32[]{:S(2)}) copy-start(f32[16,8,1440]{2,0,1:T(8,128)S(1)} %get-tuple-element.1841) | copy-start | bytes 2211844
  90.2 12.8 %collective-permute-start.2 = (f32[16,5,1440]{2,0,1:T(8,128)}, f32[16,5,1440]{2,0,1:T(8,128)S(1)}, u32[]{:S(2)}, u32[]{:S(2)}) collective-permute-start(f32[16,5,1440]{2,0,1:T(8,128)} %get-tuple-element.1590), channel_id=1, source_target_pairs={{0,1},{1,2},{2,3},{3,4},{4,5},{5,6},{6,7},{8,9},{9,10},{10,11},{11... | collective-permute-start | bytes 1382408 | tf_op jit(solution)/shard_map/while/body/eval_jaxpr/ppermute | solution.py:18
  94.5 18.8 %collective-permute-start.3 = (f32[16,5,1440]{2,0,1:T(8,128)}, f32[16,5,1440]{2,0,1:T(8,128)S(1)}, u32[]{:S(2)}, u32[]{:S(2)}) collective-permute-start(f32[16,5,1440]{2,0,1:T(8,128)} %get-tuple-element.1591), channel_id=1, source_target_pairs={{1,0},{2,1},{3,2},{4,3},{5,4},{6,5},{7,6},{9,8},{10,9},{11,10},{12... | collective-permute-start | bytes 1382408 | tf_op jit(solution)/shard_map/while/body/eval_jaxpr/ppermute | solution.py:20
  113.4 1.0 copy-start.27
  115.4 1.0 copy-start.14
  122.2 14.4 %collective-permute-start.2 = (f32[16,5,1440]{2,0,1:T(8,128)}, f32[16,5,1440]{2,0,1:T(8,128)S(1)}, u32[]{:S(2)}, u32[]{:S(2)}) collective-permute-start(f32[16,5,1440]{2,0,1:T(8,128)} %get-tuple-element.1590), channel_id=1, source_target_pairs={{0,1},{1,2},{2,3},{3,4},{4,5},{5,6},{6,7},{8,9},{9,10},{10,11},{11... | collective-permute-start | bytes 1382408 | tf_op jit(solution)/shard_map/while/body/eval_jaxpr/ppermute | solution.py:18
  126.7 22.1 %collective-permute-start.3 = (f32[16,5,1440]{2,0,1:T(8,128)}, f32[16,5,1440]{2,0,1:T(8,128)S(1)}, u32[]{:S(2)}, u32[]{:S(2)}) collective-permute-start(f32[16,5,1440]{2,0,1:T(8,128)} %get-tuple-element.1591), channel_id=1, source_target_pairs={{1,0},{2,1},{3,2},{4,3},{5,4},{6,5},{7,6},{9,8},{10,9},{11,10},{12... | collective-permute-start | bytes 1382408 | tf_op jit(solution)/shard_map/while/body/eval_jaxpr/ppermute | solution.py:20
  148.9 1.0 copy-start.27
  150.9 1.0 copy-start.14
  162.0 43.5 %copy-start.40 = (f32[3,5,8,1440]{3,2,1,0:T(8,128)S(1)}, f32[3,5,8,1440]{3,2,1,0:T(8,128)}, u32[]{:S(2)}) copy-start(f32[3,5,8,1440]{3,2,1,0:T(8,128)} %param.19) | copy-start | bytes 2073604
  162.0 316.3 %all-reduce.7.cloned.1.call-start = ((), (), s32[]{:S(2)}) async-start(), calls=%async_computation.1 | async-start | bytes 1474560 | tf_op jit(solution)/shard_map/psum | solution.py:97
  212.6 24.0 %collective-permute-start.4 = (f32[16,5,1440]{2,0,1:T(8,128)}, f32[16,5,1440]{2,0,1:T(8,128)S(1)}, u32[]{:S(2)}, u32[]{:S(2)}) collective-permute-start(f32[16,5,1440]{2,0,1:T(8,128)} %get-tuple-element.1635), channel_id=1, source_target_pairs={{0,1},{1,2},{2,3},{3,4},{4,5},{5,6},{6,7},{8,9},{9,10},{10,11},{11... | collective-permute-start | bytes 1382408 | tf_op jit(solution)/shard_map/while/body/eval_jaxpr/ppermute | solution.py:18
  216.0 20.7 %collective-permute-start.5 = (f32[16,5,1440]{2,0,1:T(8,128)}, f32[16,5,1440]{2,0,1:T(8,128)S(1)}, u32[]{:S(2)}, u32[]{:S(2)}) collective-permute-start(f32[16,5,1440]{2,0,1:T(8,128)} %get-tuple-element.1636), channel_id=1, source_target_pairs={{1,0},{2,1},{3,2},{4,3},{5,4},{6,5},{7,6},{9,8},{10,9},{11,10},{12... | collective-permute-start | bytes 1382408 | tf_op jit(solution)/shard_map/while/body/eval_jaxpr/ppermute | solution.py:20
  236.7 1.0 copy-start.30
  238.8 1.0 copy-start.17
  245.5 24.0 %collective-permute-start.4 = (f32[16,5,1440]{2,0,1:T(8,128)}, f32[16,5,1440]{2,0,1:T(8,128)S(1)}, u32[]{:S(2)}, u32[]{:S(2)}) collective-permute-start(f32[16,5,1440]{2,0,1:T(8,128)} %get-tuple-element.1635), channel_id=1, source_target_pairs={{0,1},{1,2},{2,3},{3,4},{4,5},{5,6},{6,7},{8,9},{9,10},{10,11},{11... | collective-permute-start | bytes 1382408 | tf_op jit(solution)/shard_map/while/body/eval_jaxpr/ppermute | solution.py:18
  249.9 19.8 %collective-permute-start.5 = (f32[16,5,1440]{2,0,1:T(8,128)}, f32[16,5,1440]{2,0,1:T(8,128)S(1)}, u32[]{:S(2)}, u32[]{:S(2)}) collective-permute-start(f32[16,5,1440]{2,0,1:T(8,128)} %get-tuple-element.1636), channel_id=1, source_target_pairs={{1,0},{2,1},{3,2},{4,3},{5,4},{6,5},{7,6},{9,8},{10,9},{11,10},{12... | collective-permute-start | bytes 1382408 | tf_op jit(solution)/shard_map/while/body/eval_jaxpr/ppermute | solution.py:20
  269.7 1.0 copy-start.30
  271.7 1.0 copy-start.17
  370.9 24.5 %collective-permute-start.6 = (f32[16,5,1440]{2,0,1:T(8,128)}, f32[16,5,1440]{2,0,1:T(8,128)S(1)}, u32[]{:S(2)}, u32[]{:S(2)}) collective-permute-start(f32[16,5,1440]{2,0,1:T(8,128)} %get-tuple-element.1680), channel_id=1, source_target_pairs={{0,1},{1,2},{2,3},{3,4},{4,5},{5,6},{6,7},{8,9},{9,10},{10,11},{11... | collective-permute-start | bytes 1382408 | tf_op jit(solution)/shard_map/while/body/eval_jaxpr/ppermute | solution.py:18
  375.3 20.1 %collective-permute-start.7 = (f32[16,5,1440]{2,0,1:T(8,128)S(1)}, f32[16,5,1440]{2,0,1:T(8,128)S(1)}, u32[]{:S(2)}, u32[]{:S(2)}) collective-permute-start(f32[16,5,1440]{2,0,1:T(8,128)S(1)} %get-tuple-element.1681), channel_id=1, source_target_pairs={{1,0},{2,1},{3,2},{4,3},{5,4},{6,5},{7,6},{9,8},{10,9},{11,10},{12... | collective-permute-start | bytes 1382408 | tf_op jit(solution)/shard_map/while/body/eval_jaxpr/ppermute | solution.py:20
  395.5 1.0 copy-start.33
  403.7 23.4 %collective-permute-start.6 = (f32[16,5,1440]{2,0,1:T(8,128)}, f32[16,5,1440]{2,0,1:T(8,128)S(1)}, u32[]{:S(2)}, u32[]{:S(2)}) collective-permute-start(f32[16,5,1440]{2,0,1:T(8,128)} %get-tuple-element.1680), channel_id=1, source_target_pairs={{0,1},{1,2},{2,3},{3,4},{4,5},{5,6},{6,7},{8,9},{9,10},{10,11},{11... | collective-permute-start | bytes 1382408 | tf_op jit(solution)/shard_map/while/body/eval_jaxpr/ppermute | solution.py:18
  408.0 19.2 %collective-permute-start.7 = (f32[16,5,1440]{2,0,1:T(8,128)S(1)}, f32[16,5,1440]{2,0,1:T(8,128)S(1)}, u32[]{:S(2)}, u32[]{:S(2)}) collective-permute-start(f32[16,5,1440]{2,0,1:T(8,128)S(1)} %get-tuple-element.1681), channel_id=1, source_target_pairs={{1,0},{2,1},{3,2},{4,3},{5,4},{6,5},{7,6},{9,8},{10,9},{11,10},{12... | collective-permute-start | bytes 1382408 | tf_op jit(solution)/shard_map/while/body/eval_jaxpr/ppermute | solution.py:20
  427.3 1.0 copy-start.33
  435.0 43.3 %copy-start.41 = (f32[3,5,8,1440]{3,2,1,0:T(8,128)S(1)}, f32[3,5,8,1440]{3,2,1,0:T(8,128)}, u32[]{:S(2)}) copy-start(f32[3,5,8,1440]{3,2,1,0:T(8,128)} %param.19) | copy-start | bytes 2073604
  439.9 264.8 %all-reduce.9.cloned.1.call-start = ((), (), s32[]{:S(2)}) async-start(), calls=%async_computation.2 | async-start | bytes 1474560 | tf_op jit(solution)/shard_map/psum | solution.py:106
  484.0 66.6 %copy-start.5 = (f32[16,8,1440]{2,1,0:T(8,128)S(1)}, f32[16,8,1440]{2,1,0:T(8,128)}, u32[]{:S(2)}) copy-start(f32[16,8,1440]{2,1,0:T(8,128)} %copy-done.4) | copy-start | bytes 2211844
  485.1 24.0 %collective-permute-start.8 = (f32[16,5,1440]{2,0,1:T(8,128)}, f32[16,5,1440]{2,0,1:T(8,128)}, u32[]{:S(2)}, u32[]{:S(2)}) collective-permute-start(f32[16,5,1440]{2,0,1:T(8,128)} %get-tuple-element.1725), channel_id=1, source_target_pairs={{0,1},{1,2},{2,3},{3,4},{4,5},{5,6},{6,7},{8,9},{9,10},{10,11},{11... | collective-permute-start | bytes 1382408 | tf_op jit(solution)/shard_map/while/body/eval_jaxpr/ppermute | solution.py:18
  489.2 20.9 %collective-permute-start.9 = (f32[16,5,1440]{2,0,1:T(8,128)}, f32[16,5,1440]{2,0,1:T(8,128)S(1)}, u32[]{:S(2)}, u32[]{:S(2)}) collective-permute-start(f32[16,5,1440]{2,0,1:T(8,128)} %get-tuple-element.1726), channel_id=1, source_target_pairs={{1,0},{2,1},{3,2},{4,3},{5,4},{6,5},{7,6},{9,8},{10,9},{11,10},{12... | collective-permute-start | bytes 1382408 | tf_op jit(solution)/shard_map/while/body/eval_jaxpr/ppermute | solution.py:20
  510.2 1.0 copy-start.36
  518.3 24.1 %collective-permute-start.8 = (f32[16,5,1440]{2,0,1:T(8,128)}, f32[16,5,1440]{2,0,1:T(8,128)}, u32[]{:S(2)}, u32[]{:S(2)}) collective-permute-start(f32[16,5,1440]{2,0,1:T(8,128)} %get-tuple-element.1725), channel_id=1, source_target_pairs={{0,1},{1,2},{2,3},{3,4},{4,5},{5,6},{6,7},{8,9},{9,10},{10,11},{11... | collective-permute-start | bytes 1382408 | tf_op jit(solution)/shard_map/while/body/eval_jaxpr/ppermute | solution.py:18
  523.4 20.1 %collective-permute-start.9 = (f32[16,5,1440]{2,0,1:T(8,128)}, f32[16,5,1440]{2,0,1:T(8,128)S(1)}, u32[]{:S(2)}, u32[]{:S(2)}) collective-permute-start(f32[16,5,1440]{2,0,1:T(8,128)} %get-tuple-element.1726), channel_id=1, source_target_pairs={{1,0},{2,1},{3,2},{4,3},{5,4},{6,5},{7,6},{9,8},{10,9},{11,10},{12... | collective-permute-start | bytes 1382408 | tf_op jit(solution)/shard_map/while/body/eval_jaxpr/ppermute | solution.py:20
  550.6 44.3 %copy-start.1 = (f32[16,8,1440]{2,0,1:T(8,128)S(1)}, f32[16,8,1440]{2,0,1:T(8,128)}, u32[]{:S(2)}) copy-start(f32[16,8,1440]{2,0,1:T(8,128)} %copy-done) | copy-start | bytes 2211844
  597.2 24.5 %collective-permute-start.10 = (f32[16,5,1440]{2,0,1:T(8,128)}, f32[16,5,1440]{2,0,1:T(8,128)S(1)}, u32[]{:S(2)}, u32[]{:S(2)}) collective-permute-start(f32[16,5,1440]{2,0,1:T(8,128)} %get-tuple-element.1770), channel_id=1, source_target_pairs={{0,1},{1,2},{2,3},{3,4},{4,5},{5,6},{6,7},{8,9},{9,10},{10,11},{11... | collective-permute-start | bytes 1382408 | tf_op jit(solution)/shard_map/while/body/eval_jaxpr/ppermute | solution.py:18
  601.6 20.2 %collective-permute-start.11 = (f32[16,5,1440]{2,0,1:T(8,128)S(1)}, f32[16,5,1440]{2,0,1:T(8,128)S(1)}, u32[]{:S(2)}, u32[]{:S(2)}) collective-permute-start(f32[16,5,1440]{2,0,1:T(8,128)S(1)} %get-tuple-element.1771), channel_id=1, source_target_pairs={{1,0},{2,1},{3,2},{4,3},{5,4},{6,5},{7,6},{9,8},{10,9},{11,10},{12... | collective-permute-start | bytes 1382408 | tf_op jit(solution)/shard_map/while/body/eval_jaxpr/ppermute | solution.py:20
  630.0 23.5 %collective-permute-start.10 = (f32[16,5,1440]{2,0,1:T(8,128)}, f32[16,5,1440]{2,0,1:T(8,128)S(1)}, u32[]{:S(2)}, u32[]{:S(2)}) collective-permute-start(f32[16,5,1440]{2,0,1:T(8,128)} %get-tuple-element.1770), channel_id=1, source_target_pairs={{0,1},{1,2},{2,3},{3,4},{4,5},{5,6},{6,7},{8,9},{9,10},{10,11},{11... | collective-permute-start | bytes 1382408 | tf_op jit(solution)/shard_map/while/body/eval_jaxpr/ppermute | solution.py:18
  634.3 19.3 %collective-permute-start.11 = (f32[16,5,1440]{2,0,1:T(8,128)S(1)}, f32[16,5,1440]{2,0,1:T(8,128)S(1)}, u32[]{:S(2)}, u32[]{:S(2)}) collective-permute-start(f32[16,5,1440]{2,0,1:T(8,128)S(1)} %get-tuple-element.1771), channel_id=1, source_target_pairs={{1,0},{2,1},{3,2},{4,3},{5,4},{6,5},{7,6},{9,8},{10,9},{11,10},{12... | collective-permute-start | bytes 1382408 | tf_op jit(solution)/shard_map/while/body/eval_jaxpr/ppermute | solution.py:20
  (70 other events, 60.6 us)
Sparse Core Ops, SparseCore 0:
  162.2 43.2 all-reduce.4
  440.1 38.2 all-reduce.6
  666.5 38.1 all-reduce.8
where the time goes:
time: 723 us; the launch traced here: 714 us
  waiting for transfers between devices  274 us (38%)
  local copies, waits for them, and re-layouts  134 us (19%)
  blocking collectives  127 us (18%)
  other arithmetic  83.5 us (12%)
  starting transfers between devices  74.2 us (10%)
  between operations  18.6 us (3%)
    ppermute x13, waiting for transfers between devices, with_halo(): lax.ppermute(tail, axis, [(i, (i + 1) % count) for i in range(ends)])  133 us
    psum x2, blocking collectives, squares(): return lax.psum(jnp.sum(residual * residual), ('mem', 'lat'))  84.7 us
    psum x2, waiting for transfers between devices, per_device(): total = lax.psum(partial_sum, 'mem')  80.7 us
    ppermute x13, starting transfers between devices, with_halo(): lax.ppermute(tail, axis, [(i, (i + 1) % count) for i in range(ends)])  57.1 us
    mul x60, local copies, waits for them, and re-layouts, one_pass(): return updated * keep  48.3 us
    mul x60, other arithmetic, one_pass(): return updated * keep  45 us
    psum x1, blocking collectives, per_device(): step_size = norm_now / lax.psum(jnp.sum(direction * image), ('mem', 'lat'))  41.8 us
    psum x1, waiting for transfers between devices, per_device(): increment = lax.psum(forward_partial(diffuse(control)), 'mem')  38.3 us
  transfers between devices with their start and end apart: 29, of which 17 were waited for; matrix products, arithmetic and copies ran while one was open for 11% of the time, Pallas kernels for 0%

commit v1 on v0

v1 whole, which is shorter than its diff:
```python
import functools

import jax
import jax.numpy as jnp
from jax import lax
from jax.experimental import pallas as pl
from jax.experimental.pallas import tpu as pltpu
from jax.sharding import PartitionSpec as P

PASSES = 10
LANES = 128
SUB = 8


def ceil_to(value, unit):
    return -(-value // unit) * unit


class Plan:
    def __init__(self, perturb, lat_coef, mem, lat):
        self.members, self.slots, self.vars, self.rows, self.nlon = perturb.shape
        self.mem, self.lat = mem, lat
        self.fields = self.slots * self.vars
        self.half = (self.fields + 2) // 2
        self.wide = ceil_to(self.nlon + 16, LANES)
        halo = -(-2 * PASSES // self.rows)
        self.group = max(
            g for g in range(1, lat + 1)
            if lat % g == 0 and self.members % g == 0 and (g == lat or g >= halo)
        )
        self.groups = lat // self.group
        self.halo = 0 if self.groups == 1 else halo
        self.share = self.members // self.group
        self.window = self.group + 2 * self.halo
        self.run = self.window * self.rows
        self.used = self.share * self.run
        self.lanes = ceil_to(self.used, LANES)
        self.tiles = self.lanes // LANES
        self.step = self.nlon // SUB
        self.unroll = max(u for u in range(1, 21) if self.step % u == 0)


def adjoint_kernel(p, second, *refs):
    if second:
        perturb, weight, mine, other, out, total, scal, prod, full = refs
    else:
        perturb, weight, value, lon, lat, out, prod = refs
    step = pl.program_id(0)

    if second:
        @pl.when(step == 0)
        def _():
            core = lax.axis_index("mem") % 2
            for k in range(p.half):
                full[core * p.half + k] = mine[k]
                full[(1 - core) * p.half + k] = other[k]
            acc = jnp.zeros((p.rows, p.nlon), jnp.float32)
            for k in range(p.fields):
                t = full[k]
                wt = weight[k] * t
                prod[k] = wt
                total[k] = t
                acc = acc + wt * t
            scal[0] = full[2 * p.half - 1][:, :LANES]
            scal[1] = jnp.full((p.rows, LANES), jnp.sum(acc))
    else:
        @pl.when(step == 0)
        def _():
            for k in range(p.fields):
                prod[k] = weight[k] * value[k]

    for m in range(p.share):
        acc = perturb[m, 0].astype(jnp.float32) * prod[0]
        for k in range(1, p.fields):
            acc = acc + perturb[m, k].astype(jnp.float32) * prod[k]
        out[0, m, :, : p.nlon] = acc
    if second:
        tail = jnp.broadcast_to(scal[1][:1, :1], (p.rows, p.wide - p.nlon))
        for m in range(p.share):
            out[0, m, :, p.nlon :] = tail
    else:
        for m in range(p.share):
            out[0, m, :, p.nlon :] = jnp.zeros((p.rows, p.wide - p.nlon), jnp.float32)
        out[0, p.share, :, : p.nlon] = lon[...]
        out[0, p.share + 1, :, : p.nlon] = lat[...]
        out[0, p.share, :, p.nlon :] = jnp.zeros((p.rows, p.wide - p.nlon), jnp.float32)
        out[0, p.share + 1, :, p.nlon :] = jnp.zeros((p.rows, p.wide - p.nlon), jnp.float32)


def adjoint(p, perturb, weight, *rest, second):
    whole = lambda *shape: pl.BlockSpec(shape, lambda i: (0,) * len(shape))
    rows, nlon = p.rows, p.nlon
    planes = p.share if second else p.share + 2
    field = whole(p.fields, rows, nlon)
    if second:
        more = [whole(p.half, rows, nlon)] * 2
    else:
        more = [field, whole(rows, nlon), whole(rows, nlon)]
    out_shape = [jax.ShapeDtypeStruct((p.group, planes, rows, p.wide), jnp.float32)]
    out_specs = [pl.BlockSpec((1, planes, rows, p.wide), lambda i: (i, 0, 0, 0))]
    scratch = [pltpu.VMEM((p.fields, rows, nlon), jnp.float32)]
    if second:
        out_shape += [
            jax.ShapeDtypeStruct((p.fields, rows, nlon), jnp.float32),
            jax.ShapeDtypeStruct((2, rows, LANES), jnp.float32),
        ]
        out_specs += [field, whole(2, rows, LANES)]
        scratch += [pltpu.VMEM((2 * p.half, rows, nlon), jnp.float32)]
    return pl.pallas_call(
        functools.partial(adjoint_kernel, p, second),
        grid=(p.group,),
        in_specs=[
            pl.BlockSpec((p.share, p.fields, rows, nlon), lambda i: (i, 0, 0, 0)),
            field,
            *more,
        ],
        out_specs=out_specs,
        out_shape=out_shape,
        scratch_shapes=scratch,
        name="adjoint_second" if second else "adjoint_first",
    )(perturb, weight, *rest)


def forward_kernel(p, perturb, field, keep, send, scr):
    step = pl.program_id(0)
    for v in range(p.vars):
        acc = perturb[0, 0, v].astype(jnp.float32) * field[0, :, : p.nlon]
        for m in range(1, p.members):
            acc = acc + perturb[m, 0, v].astype(jnp.float32) * field[m, :, : p.nlon]
        scr[step * p.vars + v] = acc

    @pl.when(step == p.slots - 1)
    def _():
        core = lax.axis_index("mem") % 2
        one = jnp.zeros((1, 1), jnp.float32)
        two = jnp.zeros((1, 1), jnp.float32)
        for k in range(p.group):
            one = one + field[k * p.share, :1, p.nlon : p.nlon + 1]
            two = two + field[k * p.share, :1, p.nlon + SUB : p.nlon + SUB + 1]
        for k in range(p.fields, 2 * p.half):
            scr[k] = jnp.zeros((p.rows, p.nlon), jnp.float32)
        scr[2 * p.half - 1, :, :LANES] = jnp.broadcast_to(one, (p.rows, LANES))
        scr[2 * p.half - 1, :, LANES : 2 * LANES] = jnp.broadcast_to(two, (p.rows, LANES))
        for k in range(p.half):
            keep[k] = scr[core * p.half + k]
            send[k] = scr[(1 - core) * p.half + k]


def forward(p, perturb, field):
    rows, nlon = p.rows, p.nlon
    shape = (p.half, rows, nlon)
    spec = pl.BlockSpec(shape, lambda i: (0, 0, 0))
    return pl.pallas_call(
        functools.partial(forward_kernel, p),
        grid=(p.slots,),
        in_specs=[
            pl.BlockSpec((p.members, 1, p.vars, rows, nlon), lambda i: (0, i, 0, 0, 0)),
            pl.BlockSpec((p.members, rows, p.wide), lambda i: (0, 0, 0)),
        ],
        out_specs=[spec, spec],
        out_shape=[jax.ShapeDtypeStruct(shape, jnp.float32)] * 2,
        scratch_shapes=[pltpu.VMEM((2 * p.half, rows, nlon), jnp.float32)],
        name="forward",
    )(perturb, field)


def roll(x, shift, axis):
    return pltpu.roll(x, shift % x.shape[axis], axis)


def flip(p, pick, sheet):
    for j in range(p.wide // LANES):
        cols = slice(j * LANES, (j + 1) * LANES)
        tiles = [pick(c, m, cols) for m in range(p.share) for c in range(p.window)]
        if p.used < p.lanes:
            tiles.append(jnp.zeros((p.lanes - p.used, LANES), jnp.float32))
        block = jnp.concatenate(tiles, axis=0)
        for t in range(p.tiles):
            sheet[t, cols, :] = block[t * LANES : (t + 1) * LANES].T


def unflip(p, sheet, out, stop):
    for j in range(-(-stop // LANES)):
        low, high = j * LANES, min((j + 1) * LANES, stop)
        block = [sheet[t, low : low + LANES, :].T for t in range(p.tiles)]
        for m in range(p.share):
            for c in range(p.group):
                at = m * p.run + (p.halo + c) * p.rows
                piece = block[at // LANES][at % LANES : at % LANES + p.rows]
                out[c, m, :, low:high] = piece[:, : high - low]


def lane_row(p):
    lane = lax.broadcasted_iota(jnp.int32, (SUB, p.lanes), 1)
    return lane % p.run, lane


def wrap(p, buf):
    buf[0] = roll(buf[p.step], 1, 0)
    buf[p.step + 1] = roll(buf[1], -1, 0)


def tile(t):
    return slice(t * LANES, (t + 1) * LANES)


def sheet_to(p, sheet, buf):
    def one(i, none):
        for t in range(p.tiles):
            buf[i + 1, :, tile(t)] = sheet[t, pl.ds(i, SUB, stride=p.step), :]
        return none
    lax.fori_loop(0, p.step, one, 0, unroll=p.unroll)


def to_sheet(p, buf, sheet):
    def one(i, none):
        for t in range(p.tiles):
            sheet[t, pl.ds(i, SUB, stride=p.step), :] = buf[i + 1, :, tile(t)]
        return none
    lax.fori_loop(0, p.step, one, 0, unroll=p.unroll)


def one_pass(p, src, dst, east, north, diag):
    def body(c, carry):
        f, west = carry
        for k in range(p.unroll):
            i = 1 + c * p.unroll + k
            fe = src[i + 1]
            flux = east[i] * (fe - f)
            up = north[i] * (roll(f, -1, 1) - f)
            dst[i] = diag[i] * f + ((up - roll(up, 1, 1)) + (flux - west))
            f, west = fe, flux
        return f, west
    f = src[1]
    lax.fori_loop(0, p.step // p.unroll, body, (f, east[0] * (f - src[0])))
    wrap(p, dst)


def ten(p, a, b, east, north, diag):
    def two(_, none):
        one_pass(p, a, b, east, north, diag)
        one_pass(p, b, a, east, north, diag)
        return none
    lax.fori_loop(0, PASSES // 2, two, 0)
    if PASSES % 2:
        one_pass(p, a, b, east, north, diag)
        a[...] = b[...]


def total_of(p, own, term):
    def one(i, acc):
        return acc + term(i + 1)
    acc = lax.fori_loop(0, p.step, one, jnp.zeros((SUB, p.lanes), jnp.float32), unroll=p.unroll)
    return jnp.sum(jnp.where(own, acc, 0.0))


def own_lanes(p):
    row, lane = lane_row(p)
    first = p.halo * p.rows
    return (row >= first) & (row < first + p.group * p.rows) & (lane < p.used)


def first_kernel(p, got, out, right, east, north, diag, sheet, a, b):
    row, lane = lane_row(p)
    low = 0
    high = p.run - 1
    if p.groups > 1:
        here = lax.axis_index("lat") // p.group * p.group - p.halo
        low = jnp.maximum(-here, 0) * p.rows
        high = jnp.minimum(p.lat - here, p.window) * p.rows - 1
    flip(p, lambda c, m, cols: got[c, p.share + 1, :, cols], sheet)
    sheet_to(p, sheet, a)
    inside = (row >= low) & (row <= high) & (lane < p.used)

    def coefs(i, none):
        here = jnp.where(inside, a[i + 1], 0.0)
        north[i + 1] = jnp.where(inside & (row < high), roll(here, -1, 1), 0.0)
        diag[i + 1] = 1.0 - jnp.where(row == low, here, 0.0)
        return none
    lax.fori_loop(0, p.step, coefs, 0, unroll=p.unroll)
    flip(p, lambda c, m, cols: got[c, p.share, :, cols], sheet)
    sheet_to(p, sheet, east)
    wrap(p, east)
    flip(p, lambda c, m, cols: got[c, m, :, cols], sheet)
    sheet_to(p, sheet, a)
    wrap(p, a)
    ten(p, a, b, east, north, diag)

    def keep(i, none):
        right[i + 1] = a[i + 1]
        return none
    lax.fori_loop(0, p.step, keep, 0, unroll=p.unroll)
    rr = total_of(p, own_lanes(p), lambda i: right[i] * right[i])
    ten(p, a, b, east, north, diag)
    to_sheet(p, a, sheet)
    sheet[:, p.nlon :, :] = jnp.full((p.tiles, p.wide - p.nlon, LANES), rr)
    unflip(p, sheet, out, p.wide)


def second_kernel(p, got, right, east, north, diag, scal, out, resid, ahead, sheet, a, b):
    row, lane = lane_row(p)
    flip(p, lambda c, m, cols: got[c, m, :, cols], sheet)
    if p.groups == 1:
        q = 0.0
        for t in range(p.tiles):
            first = (row[:1, tile(t)] % p.rows == 0) & (lane[:1, tile(t)] < p.run)
            q = q + jnp.sum(jnp.where(first, sheet[t, p.nlon : p.nlon + 1, :], 0.0))
        q = jnp.full((SUB, LANES), q)
    else:
        q = scal[1][:SUB]
    rr = scal[0][:SUB]
    alpha = rr / (rr + q)
    ahead[...] = alpha
    sheet_to(p, sheet, a)
    wrap(p, a)
    ten(p, a, b, east, north, diag)
    alpha = jnp.broadcast_to(alpha[:, :1], (SUB, p.lanes))

    def cut(i, none):
        r = right[i + 1]
        r = r - alpha * (r + a[i + 1])
        a[i + 1] = r
        resid[i + 1] = r
        return none
    lax.fori_loop(0, p.step, cut, 0, unroll=p.unroll)
    wrap(p, a)
    own = own_lanes(p)
    rr1 = total_of(p, own, lambda i: resid[i] * resid[i])
    rb = total_of(p, own, lambda i: resid[i] * right[i])
    ten(p, a, b, east, north, diag)
    to_sheet(p, a, sheet)
    sheet[:, p.nlon :, :] = jnp.zeros((p.tiles, p.wide - p.nlon, LANES), jnp.float32)
    sheet[:, p.nlon : p.nlon + SUB, :] = jnp.full((p.tiles, SUB, LANES), rr1)
    sheet[:, p.nlon + SUB : p.nlon + 2 * SUB, :] = jnp.full((p.tiles, SUB, LANES), rb)
    unflip(p, sheet, out, p.wide)


def buffers(p):
    buf = (p.step + 2, SUB, p.lanes)
    return [pltpu.VMEM((p.tiles, p.wide, LANES), jnp.float32)] + [pltpu.VMEM(buf, jnp.float32)] * 2


def vmem(n):
    return [pl.BlockSpec(memory_space=pltpu.VMEM)] * n


def first_half(p, got):
    buf = jax.ShapeDtypeStruct((p.step + 2, SUB, p.lanes), jnp.float32)
    back = jax.ShapeDtypeStruct((p.group, p.share, p.rows, p.wide), jnp.float32)
    return pl.pallas_call(
        functools.partial(first_kernel, p),
        in_specs=vmem(1),
        out_specs=vmem(5),
        out_shape=[back, buf, buf, buf, buf],
        scratch_shapes=buffers(p),
        name="smooth_first",
    )(got)


def second_half(p, got, right, east, north, diag, scal):
    buf = jax.ShapeDtypeStruct((p.step + 2, SUB, p.lanes), jnp.float32)
    back = jax.ShapeDtypeStruct((p.group, p.share, p.rows, p.wide), jnp.float32)
    return pl.pallas_call(
        functools.partial(second_kernel, p),
        in_specs=vmem(6),
        out_specs=vmem(3),
        out_shape=[back, buf, jax.ShapeDtypeStruct((SUB, LANES), jnp.float32)],
        scratch_shapes=buffers(p),
        name="smooth_second",
    )(got, right, east, north, diag, scal)


def test_kernel(p, weight, total, mine, other, scal, both, sums, part, full):
    core = lax.axis_index("mem") % 2
    for k in range(p.half):
        full[core * p.half + k] = mine[k]
        full[(1 - core) * p.half + k] = other[k]
    rr1 = full[2 * p.half - 1][:, :LANES]
    rb = full[2 * p.half - 1][:, LANES : 2 * LANES]
    rr = scal[0]
    beta = rr1 / rr
    acc = jnp.zeros((p.rows, p.nlon), jnp.float32)
    for k in range(p.fields):
        t = full[k] + beta[:1, :1] * total[k]
        both[k] = t
        acc = acc + weight[k] * t * t
    sums[0] = rr1
    sums[1] = beta
    sums[2] = rr1 + beta * (2.0 * rb + beta * rr)
    part[...] = jnp.full((p.rows, LANES), jnp.sum(acc))


def test(p, weight, total, mine, other, scal):
    return pl.pallas_call(
        functools.partial(test_kernel, p),
        in_specs=vmem(5),
        out_specs=vmem(3),
        out_shape=[
            jax.ShapeDtypeStruct((p.fields, p.rows, p.nlon), jnp.float32),
            jax.ShapeDtypeStruct((3, p.rows, LANES), jnp.float32),
            jax.ShapeDtypeStruct((p.rows, LANES), jnp.float32),
        ],
        scratch_shapes=[pltpu.VMEM((2 * p.half, p.rows, p.nlon), jnp.float32)],
        name="last_sums",
    )(weight, total, mine, other, scal)


def last_kernel(p, total, both, sums, ahead, q, right, resid, grown, back, sheet):
    step2 = sums[0] / (sums[2] + q[...])
    step1 = ahead[: p.rows]
    for k in range(p.fields):
        grown[k] = step1[:1, :1] * total[k] + step2[:1, :1] * both[k]
    near = step1 + step2 * sums[1]
    near = jnp.broadcast_to(near[:1, :1], (SUB, LANES))
    far = jnp.broadcast_to(step2[:1, :1], (SUB, LANES))

    def one(i, none):
        for t in range(p.tiles):
            at = (i + 1, slice(None), tile(t))
            sheet[t, pl.ds(i, SUB, stride=p.step), :] = near * right[at] + far * resid[at]
        return none
    lax.fori_loop(0, p.step, one, 0, unroll=p.unroll)
    sheet[:, p.nlon :, :] = jnp.zeros((p.tiles, p.wide - p.nlon, LANES), jnp.float32)
    unflip(p, sheet, back, p.nlon)


def last(p, total, both, sums, ahead, q, right, resid):
    return pl.pallas_call(
        functools.partial(last_kernel, p),
        in_specs=vmem(7),
        out_specs=vmem(2),
        out_shape=[
            jax.ShapeDtypeStruct((p.fields, p.rows, p.nlon), jnp.float32),
            jax.ShapeDtypeStruct((p.group, p.share, p.rows, p.nlon), jnp.float32),
        ],
        scratch_shapes=[pltpu.VMEM((p.tiles, p.wide, LANES), jnp.float32)],
        name="last_update",
    )(total, both, sums, ahead, q, right, resid)


def swap(p, x, axis, bit, count):
    return lax.ppermute(x, axis, [(i, i ^ bit) for i in range(count)])


def turn(p, x):
    if p.groups == 1:
        return lax.all_to_all(x, "lat", 0, 0)
    sets = [[g * p.group + i for i in range(p.group)] for g in range(p.groups)]
    return lax.all_to_all(x, "lat", 0, 0, axis_index_groups=sets)


def widen(p, x):
    if p.groups == 1:
        return x
    gap = p.group
    up = [(i, i + gap) for i in range(p.lat - gap)]
    down = [(i + gap, i) for i in range(p.lat - gap)]
    before = lax.ppermute(x[-p.halo :], "lat", up)
    after = lax.ppermute(x[: p.halo], "lat", down)
    return jnp.concatenate([before, x, after], axis=0)


def member_sum(p, keep, send):
    mine = keep + swap(p, send, "mem", 1, p.mem)
    bit = 2
    while bit < p.mem:
        mine = mine + swap(p, mine, "mem", bit, p.mem)
        bit *= 2
    other = swap(p, mine, "mem", 1, p.mem)
    if p.groups > 1:
        mine, other = (regroup(p, x) for x in (mine, other))
    return mine, other


def regroup(p, x):
    sums = lax.psum(x[-1:], "lat") / p.group
    return jnp.concatenate([x[:-1], sums], axis=0)


def lat_sum(p, x):
    bit = 1
    while bit < p.lat:
        x = x + swap(p, x, "lat", bit, p.lat)
        bit *= 2
    return x


def per_device(perturb, innovation, obs_weight, lon_coef, lat_coef):
    p = Plan(perturb, lat_coef, lax.axis_size("mem"), lax.axis_size("lat"))
    flat = lambda x: x.reshape(p.fields, p.rows, p.nlon)
    weight = flat(obs_weight)
    by_member = perturb.reshape(p.members, p.fields, p.rows, p.nlon)

    (sent,) = adjoint(p, by_member, weight, flat(innovation), lon_coef, lat_coef, second=False)
    back, right, east, north, diag = first_half(p, widen(p, turn(p, sent)))
    field = turn(p, back).reshape(p.members, p.rows, p.wide)
    mine, other = member_sum(p, *forward(p, perturb, field))
    sent, total, scal = adjoint(p, by_member, weight, mine, other, second=True)
    if p.groups > 1:
        scal = jnp.concatenate([scal[:1], lax.psum(scal[1:], "lat")], axis=0)
    back, resid, ahead = second_half(p, widen(p, turn(p, sent)), right, east, north, diag, scal)
    field = turn(p, back).reshape(p.members, p.rows, p.wide)
    mine, other = member_sum(p, *forward(p, perturb, field))
    both, sums, part = test(p, weight, total, mine, other, scal)
    grown, back = last(p, total, both, sums, ahead, lat_sum(p, part), right, resid)
    control = turn(p, back).reshape(p.members, p.rows, p.nlon)
    return control, grown.reshape(p.slots, p.vars, p.rows, p.nlon)


def solution(mesh):
    return jax.shard_map(
        per_device,
        mesh=mesh,
        in_specs=(
            P("mem", None, None, "lat", None),
            P(None, None, "lat", None),
            P(None, None, "lat", None),
            P("lat", None),
            P("lat", None),
        ),
        out_specs=(P("mem", "lat", None), P(None, None, "lat", None)),
        check_vma=False,
    )
```

time: 723 us -> 287 us (0.40); the launches traced: 714 us -> 286 us
  waiting for transfers between devices: 274 us -> 34.9 us
  local copies, waits for them, and re-layouts: 134 us -> 2.38 us
  Pallas kernels: 0 us -> 99.6 us
  other arithmetic: 83.5 us -> 3.48 us
  starting transfers between devices: 74.2 us -> 6.9 us
  between operations: 18.6 us -> 0.69 us
  blocking collectives: 127 us -> 138 us
    all_to_all x0 -> x5, blocking collectives: none -> 138 us  [turn(): return lax.all_to_all(x, 'lat', 0, 0)]
    psum x3 -> x0, blocking collectives: 127 us -> none  [the longest x2 84.7 us: squares(): return lax.psum(jnp.sum(residual * residual), ('mem', 'lat'))]
    ppermute x26 -> x9, waiting for transfers between devices: 155 us -> 34.9 us  [swap(): return lax.ppermute(x, axis, [(i, i ^ bit) for i in range(count)])]
    psum x3 -> x0, waiting for transfers between devices: 119 us -> none  [the longest x2 80.7 us: per_device(): total = lax.psum(partial_sum, 'mem')]
    pallas_call x0 -> x8, Pallas kernels: none -> 99.6 us  [the longest x1 34.9 us: first_half(): pl.pallas_call(functools.partial(first_kernel, p), in_specs=vmem(1), out_...]
    mul x120 -> x0, local copies, waits for them, and re-layouts: 67.8 us -> none  [the longest x60 48.3 us: one_pass(): return updated * keep]
    ppermute x26 -> x9, starting transfers between devices: 73.8 us -> 6.9 us  [swap(): return lax.ppermute(x, axis, [(i, i ^ bit) for i in range(count)])]
    mul x60 -> x0, other arithmetic: 45 us -> none  [one_pass(): return updated * keep]
  transfers between devices with their start and end apart: 29 -> 9, of which waited for: 17 -> 9; matrix products, arithmetic and copies ran while one was open for 11% -> 0% of each run, Pallas kernels for 0% -> 0%
where the time goes in v1:
time: 287 us; the launch traced here: 286 us
  blocking collectives  138 us (48%)
  Pallas kernels  99.6 us (35%)
  waiting for transfers between devices  34.9 us (12%)
  starting transfers between devices  6.9 us (2%)
  other arithmetic  3.48 us (1%)
    all_to_all x5, blocking collectives, turn(): return lax.all_to_all(x, 'lat', 0, 0)  138 us
    ppermute x9, waiting for transfers between devices, swap(): return lax.ppermute(x, axis, [(i, i ^ bit) for i in range(count)])  34.9 us
    pallas_call x1, Pallas kernels, first_half(): pl.pallas_call(functools.partial(first_kernel, p), in_specs=vmem(1), out_...  34.9 us
    pallas_call x1, Pallas kernels, second_half(): pl.pallas_call(functools.partial(second_kernel, p), in_specs=vmem(6), out...  33.9 us
    pallas_call x2, Pallas kernels, adjoint(): pl.pallas_call(functools.partial(adjoint_kernel, p, second), grid=(p.grou...  14.8 us
    pallas_call x2, Pallas kernels, forward(): pl.pallas_call(functools.partial(forward_kernel, p), grid=(p.slots,), in_...  10.1 us
    ppermute x9, starting transfers between devices, swap(): return lax.ppermute(x, axis, [(i, i ^ bit) for i in range(count)])  6.9 us
  transfers between devices with their start and end apart: 9, of which 9 were waited for; matrix products, arithmetic and copies ran while one was open for 0% of the time, Pallas kernels for 0%

profile of v1, /device:TPU:0, one launch (start us, length us, event | category | flops | bytes accessed | tf_op | source)
XLA Modules:
  0.0 285.6 jit_solution(8193469044934855828)
XLA Ops:
  0.6 7.3 %adjoint_first.1 = f32[8,4,8,1536]{3,2,1,0:T(8,128)} custom-call(bf16[16,15,8,1440]{3,2,1,0:T(8,128)(2,1)} %bitcast.7, f32[15,8,1440]{2,1,0:T(8,128)} %bitcast.9, f32[15,8,1440]{2,1,0:T(8,128)} %bitcast.15, f32[8,1440]{1,0:T(8,128)} %refs_3_.1, f32[8,1440]{1,0:T(8,128)} %refs_4_.1), custom_call_target="tpu_custom_call" | custom-call | tf_op jit(solution)/shard_map/adjoint_first/pallas_call | solution.py:109
  7.9 44.4 %all_to_all.25.got = f32[8,4,8,1536]{3,2,1,0:T(8,128)} all-to-all(f32[8,4,8,1536]{3,2,1,0:T(8,128)} %adjoint_first.1), channel_id=1, replica_groups=mesh['mem'=4,'lat'=8] {'lat'}, dimensions={0} | all-to-all | bytes 3145728 | tf_op jit(solution)/shard_map/all_to_all | solution.py:447
  52.4 34.9 %smooth_first.1 = (f32[8,2,8,1536]{3,2,1,0:T(8,128)}, f32[182,8,128]{2,1,0:T(8,128)}, f32[182,8,128]{2,1,0:T(8,128)}, f32[182,8,128]{2,1,0:T(8,128)}, f32[182,8,128]{2,1,0:T(8,128)}) custom-call(f32[8,4,8,1536]{3,2,1,0:T(8,128)} %all_to_all.25.got), custom_call_target="tpu_custom_call" | custom-call | tf_op jit(solution)/shard_map/smooth_first/pallas_call | solution.py:350
  87.2 23.5 %all_to_all.26 = f32[8,2,8,1536]{3,2,1,0:T(8,128)} all-to-all(f32[8,2,8,1536]{3,2,1,0:T(8,128)} %get-tuple-element.22), channel_id=1, replica_groups=mesh['mem'=4,'lat'=8] {'lat'}, dimensions={0} | all-to-all | bytes 1572864 | tf_op jit(solution)/shard_map/all_to_all | solution.py:447
  110.7 5.1 %forward.2 = (f32[8,8,1440]{2,1,0:T(8,128)}, f32[8,8,1440]{2,1,0:T(8,128)}) custom-call(bf16[16,3,5,8,1440]{4,3,2,1,0:T(8,128)(2,1)} %perturb.3, f32[16,8,1536]{2,1,0:T(8,128)} %bitcast.12), custom_call_target="tpu_custom_call" | custom-call | tf_op jit(solution)/shard_map/forward/pallas_call | solution.py:153
  115.8 0.0 collective-permute-start
  115.8 1.9 collective-permute-done
  117.7 1.1 add.21
  118.8 1.6 collective-permute-start.1
  120.4 9.7 %collective-permute-done.1 = f32[8,8,1440]{2,1,0:T(8,128)S(1)} collective-permute-done((f32[8,8,1440]{2,1,0:T(8,128)S(1)}, f32[8,8,1440]{2,1,0:T(8,128)S(1)}, u32[]{:S(2)}, u32[]{:S(2)}) %collective-permute-start.1) | collective-permute-done | bytes 368672 | tf_op jit(solution)/shard_map/ppermute | solution.py:442
  130.1 0.0 copy-start
  130.1 0.1 collective-permute-start.2
  130.2 1.7 collective-permute-done.2.refs_3_
  131.9 0.0 copy-done
  131.9 0.0 copy-start.2
  131.9 0.7 copy-done.2
  132.6 7.5 %adjoint_second.1 = (f32[8,2,8,1536]{3,2,1,0:T(8,128)}, f32[15,8,1440]{2,1,0:T(8,128)}, f32[2,8,128]{2,1,0:T(8,128)}) custom-call(bf16[16,15,8,1440]{3,2,1,0:T(8,128)(2,1)} %bitcast.8, f32[15,8,1440]{2,1,0:T(8,128)} %bitcast.10, f32[8,8,1440]{2,1,0:T(8,128)} %copy-done, f32[8,8,1440]{2,1,0:T(8,128)} %copy-done.2), custom_call_target="tpu_custom_call" | custom-call | tf_op jit(solution)/shard_map/adjoint_second/pallas_call | solution.py:109
  140.1 24.9 %all_to_all.27.got = f32[8,2,8,1536]{3,2,1,0:T(8,128)} all-to-all(f32[8,2,8,1536]{3,2,1,0:T(8,128)} %get-tuple-element.26), channel_id=1, replica_groups=mesh['mem'=4,'lat'=8] {'lat'}, dimensions={0} | all-to-all | bytes 1572864 | tf_op jit(solution)/shard_map/all_to_all | solution.py:447
  165.0 33.9 %smooth_second.1 = (f32[8,2,8,1536]{3,2,1,0:T(8,128)}, f32[182,8,128]{2,1,0:T(8,128)}, f32[8,128]{1,0:T(8,128)}) custom-call(f32[8,2,8,1536]{3,2,1,0:T(8,128)} %all_to_all.27.got, f32[182,8,128]{2,1,0:T(8,128)} %get-tuple-element.27.right, f32[182,8,128]{2,1,0:T(8,128)} %get-tuple-element.28.east, f32[182,8,128]{2,1,0:T(8,128)} %get-tuple-element.29.north, ...), custom_call_target="tpu_custom_call" | custom-call | tf_op jit(solution)/shard_map/smooth_second/pallas_call | solution.py:363
  198.9 24.1 %all_to_all.28 = f32[8,2,8,1536]{3,2,1,0:T(8,128)} all-to-all(f32[8,2,8,1536]{3,2,1,0:T(8,128)} %get-tuple-element.32), channel_id=1, replica_groups=mesh['mem'=4,'lat'=8] {'lat'}, dimensions={0} | all-to-all | bytes 1572864 | tf_op jit(solution)/shard_map/all_to_all | solution.py:447
  223.0 5.1 %forward.3 = (f32[8,8,1440]{2,1,0:T(8,128)}, f32[8,8,1440]{2,1,0:T(8,128)}) custom-call(bf16[16,3,5,8,1440]{4,3,2,1,0:T(8,128)(2,1)} %perturb.3, f32[16,8,1536]{2,1,0:T(8,128)} %bitcast.13), custom_call_target="tpu_custom_call" | custom-call | tf_op jit(solution)/shard_map/forward/pallas_call | solution.py:153
  228.0 0.0 collective-permute-start.3
  228.0 1.9 collective-permute-done.3
  230.0 1.1 add.23
  231.0 1.6 collective-permute-start.4
  232.6 9.7 %collective-permute-done.4 = f32[8,8,1440]{2,1,0:T(8,128)S(1)} collective-permute-done((f32[8,8,1440]{2,1,0:T(8,128)S(1)}, f32[8,8,1440]{2,1,0:T(8,128)S(1)}, u32[]{:S(2)}, u32[]{:S(2)}) %collective-permute-start.4) | collective-permute-done | bytes 368672 | tf_op jit(solution)/shard_map/ppermute | solution.py:442
  242.3 0.0 copy-start.1
  242.3 0.1 collective-permute-start.5
  242.4 1.7 collective-permute-done.5.other
  244.1 0.0 copy-start.3
  244.1 0.0 copy-done.1
  244.1 0.7 copy-done.3
  244.8 2.7 last_sums.1
  247.5 1.5 collective-permute-start.6
  249.0 2.4 collective-permute-done.6
  251.3 0.7 add.25
  252.0 1.1 collective-permute-start.7
  253.1 2.5 collective-permute-done.7
  255.6 1.1 collective-permute-start.8
  256.7 3.4 %collective-permute-done.8 = f32[8,128]{1,0:T(8,128)S(1)} collective-permute-done((f32[8,128]{1,0:T(8,128)S(1)}, f32[8,128]{1,0:T(8,128)S(1)}, u32[]{:S(2)}, u32[]{:S(2)}) %collective-permute-start.8) | collective-permute-done | bytes 4128 | tf_op jit(solution)/shard_map/ppermute | solution.py:442
  260.1 0.6 add.27.q
  260.7 3.2 %last_update.1 = (f32[15,8,1440]{2,1,0:T(8,128)}, f32[8,2,8,1440]{3,2,1,0:T(8,128)}) custom-call(f32[15,8,1440]{2,1,0:T(8,128)} %get-tuple-element.25.total, f32[15,8,1440]{2,1,0:T(8,128)} %get-tuple-element.35.both, f32[3,8,128]{2,1,0:T(8,128)} %get-tuple-element.36.sums, f32[8,128]{1,0:T(8,128)} %get-tuple-element.37.ahead, f32[8,128]{1,0:T(8,128)} %add.27.q, ...), custom_call_target="tpu_custom_call" | custom-call | tf_op jit(solution)/shard_map/last_update/pallas_call | solution.py:428
  264.0 20.7 %all_to_all.29 = f32[8,2,8,1440]{3,2,1,0:T(8,128)S(1)} all-to-all(f32[8,2,8,1440]{3,2,1,0:T(8,128)} %get-tuple-element.40), channel_id=1, replica_groups=mesh['mem'=4,'lat'=8] {'lat'}, dimensions={0} | all-to-all | bytes 1474560 | tf_op jit(solution)/shard_map/all_to_all | solution.py:447
  284.7 0.9 copy.8
  (3 shorter events, 0.1 us)
Async XLA Ops:
  115.8 1.9 collective-permute-start
  118.8 11.2 %collective-permute-start.1 = (f32[8,8,1440]{2,1,0:T(8,128)S(1)}, f32[8,8,1440]{2,1,0:T(8,128)S(1)}, u32[]{:S(2)}, u32[]{:S(2)}) collective-permute-start(f32[8,8,1440]{2,1,0:T(8,128)S(1)} %add.21), channel_id=1, source_target_pairs={{0,16},{8,24},{16,0},{24,8},{1,17},{9,25},{17,1},{25,9},{2,18},{10... | collective-permute-start | bytes 1105928 | tf_op jit(solution)/shard_map/ppermute | solution.py:442
  130.1 1.8 copy-start
  130.1 1.8 collective-permute-start.2
  131.9 0.7 copy-start.2
  228.0 1.9 collective-permute-start.3
  231.0 11.2 %collective-permute-start.4 = (f32[8,8,1440]{2,1,0:T(8,128)S(1)}, f32[8,8,1440]{2,1,0:T(8,128)S(1)}, u32[]{:S(2)}, u32[]{:S(2)}) collective-permute-start(f32[8,8,1440]{2,1,0:T(8,128)S(1)} %add.23), channel_id=1, source_target_pairs={{0,16},{8,24},{16,0},{24,8},{1,17},{9,25},{17,1},{25,9},{2,18},{10... | collective-permute-start | bytes 1105928 | tf_op jit(solution)/shard_map/ppermute | solution.py:442
  242.3 1.8 copy-start.1
  242.3 1.8 collective-permute-start.5
  244.1 0.7 copy-start.3
  247.5 3.8 %collective-permute-start.6 = (f32[8,128]{1,0:T(8,128)}, f32[8,128]{1,0:T(8,128)S(1)}, u32[]{:S(2)}, u32[]{:S(2)}) collective-permute-start(f32[8,128]{1,0:T(8,128)} %get-tuple-element.38), channel_id=1, source_target_pairs={{0,1},{1,0},{2,3},{3,2},{4,5},{5,4},{6,7},{7,6},{8,9},{9,8},{10,11... | collective-permute-start | bytes 12296 | tf_op jit(solution)/shard_map/ppermute | solution.py:442
  252.0 3.6 %collective-permute-start.7 = (f32[8,128]{1,0:T(8,128)S(1)}, f32[8,128]{1,0:T(8,128)S(1)}, u32[]{:S(2)}, u32[]{:S(2)}) collective-permute-start(f32[8,128]{1,0:T(8,128)S(1)} %add.25), channel_id=1, source_target_pairs={{0,2},{1,3},{2,0},{3,1},{4,6},{5,7},{6,4},{7,5},{8,10},{9,11},{10,... | collective-permute-start | bytes 12296 | tf_op jit(solution)/shard_map/ppermute | solution.py:442
  255.6 4.5 %collective-permute-start.8 = (f32[8,128]{1,0:T(8,128)S(1)}, f32[8,128]{1,0:T(8,128)S(1)}, u32[]{:S(2)}, u32[]{:S(2)}) collective-permute-start(f32[8,128]{1,0:T(8,128)S(1)} %add.26), channel_id=1, source_target_pairs={{0,4},{1,5},{2,6},{3,7},{4,0},{5,1},{6,2},{7,3},{8,12},{9,13},{10,... | collective-permute-start | bytes 12296 | tf_op jit(solution)/shard_map/ppermute | solution.py:442

commit v2 on v1

v2 whole, which is shorter than its diff:
```python
import functools

import jax
import jax.numpy as jnp
from jax import lax
from jax.experimental import pallas as pl
from jax.experimental.pallas import tpu as pltpu
from jax.sharding import PartitionSpec as P

PASSES = 10
LANES = 128
SUB = 8
ROOM = pltpu.CompilerParams(vmem_limit_bytes=24 * 2**20)


def ceil_to(value, unit):
    return -(-value // unit) * unit


class Plan:
    def __init__(self, perturb, lat_coef, mem, lat):
        self.members, self.slots, self.vars, self.rows, self.nlon = perturb.shape
        self.mem, self.lat = mem, lat
        self.fields = self.slots * self.vars
        self.half = (self.fields + 2) // 2
        self.wide = ceil_to(self.nlon + 16, LANES)
        halo = -(-2 * PASSES // self.rows)
        self.group = max(
            g for g in range(1, lat + 1)
            if lat % g == 0 and self.members % g == 0 and (g == lat or g >= halo)
        )
        self.groups = lat // self.group
        self.halo = 0 if self.groups == 1 else halo
        self.share = self.members // self.group
        self.window = self.group + 2 * self.halo
        self.run = self.window * self.rows
        self.used = self.share * self.run
        self.lanes = ceil_to(self.used, LANES)
        self.tiles = self.lanes // LANES
        self.step = self.nlon // SUB
        self.unroll = max(u for u in range(1, 21) if self.step % u == 0)
        self.stride = max(u for u in range(1, 91) if self.step % u == 0)
        self.parts = max(
            q for q in (1, 2, 4) if mem % q == 0 and self.wide % (q * LANES) == 0
        )
        self.piece = self.wide // self.parts


def adjoint_kernel(p, second, *refs):
    if second:
        perturb, weight, mine, other, out, total, scal, prod = refs
    else:
        perturb, weight, value, out, prod = refs
    step = pl.program_id(0)

    @pl.when(step == 0)
    def _():
        if second:
            core = lax.axis_index("mem") % 2
            acc = jnp.zeros((p.rows, p.nlon), jnp.float32)
            for half, at in ((mine, core * p.half), (other, (1 - core) * p.half)):
                for k in range(p.half):
                    t = half[k, :, : p.nlon]
                    wt = weight[jnp.minimum(at + k, p.fields - 1)] * t
                    prod[at + k] = wt
                    total[at + k] = t
                    acc = acc + wt * t
            rr = mine[0, :1, p.nlon : p.nlon + 1]
            scal[0] = jnp.broadcast_to(rr, (p.rows, LANES))
            scal[1] = jnp.full((p.rows, LANES), jnp.sum(acc))
        else:
            for k in range(p.fields):
                prod[k] = weight[k] * value[k]

    acc = [0.0] * p.share
    for k in range(p.fields):
        row = prod[k]
        for m in range(p.share):
            acc[m] = acc[m] + perturb[m, k].astype(jnp.float32) * row
    tail = jnp.zeros((p.rows, p.wide - p.nlon), jnp.float32)
    if second:
        tail = jnp.broadcast_to(scal[1][:1, :1], tail.shape)
    for m in range(p.share):
        out[0, m, :, : p.nlon] = acc[m]
        out[0, m, :, p.nlon :] = tail


def adjoint(p, perturb, weight, *rest, second):
    whole = lambda *shape: pl.BlockSpec(shape, lambda i: (0,) * len(shape))
    rows, nlon = p.rows, p.nlon
    field = whole(p.fields, rows, nlon)
    more = [whole(p.half, rows, p.wide)] * 2 if second else [field]
    out_shape = [jax.ShapeDtypeStruct((p.group, p.share, rows, p.wide), jnp.float32)]
    out_specs = [pl.BlockSpec((1, p.share, rows, p.wide), lambda i: (i, 0, 0, 0))]
    if second:
        out_shape += [
            jax.ShapeDtypeStruct((2 * p.half, rows, nlon), jnp.float32),
            jax.ShapeDtypeStruct((2, rows, LANES), jnp.float32),
        ]
        out_specs += [whole(2 * p.half, rows, nlon), whole(2, rows, LANES)]
    return pl.pallas_call(
        functools.partial(adjoint_kernel, p, second),
        grid=(p.group,),
        in_specs=[
            pl.BlockSpec((p.share, p.fields, rows, nlon), lambda i: (i, 0, 0, 0)),
            field,
            *more,
        ],
        out_specs=out_specs,
        out_shape=out_shape,
        scratch_shapes=[pltpu.VMEM((2 * p.half, rows, nlon), jnp.float32)],
        cost_estimate=cost(p, 2),
        compiler_params=ROOM,
        name="adjoint_second" if second else "adjoint_first",
    )(perturb, weight, *rest)


def cost(p, size):
    cells = p.members * p.fields * p.rows * p.nlon
    return pl.CostEstimate(flops=2 * cells, bytes_accessed=size * cells, transcendentals=0)


def forward_kernel(p, perturb, field, keep, send, scr):
    step = pl.program_id(0)

    @pl.when(step == 0)
    def _():
        for k in range(2 * p.half):
            scr[k, :, p.nlon :] = jnp.zeros((p.rows, p.wide - p.nlon), jnp.float32)
        for k in range(p.fields, 2 * p.half):
            scr[k, :, : p.nlon] = jnp.zeros((p.rows, p.nlon), jnp.float32)

    split = p.nlon // (2 * LANES) * LANES
    for cols in (slice(0, split), slice(split, p.nlon)):
        acc = [0.0] * p.vars
        for m in range(p.members):
            f = field[m, :, cols]
            for v in range(p.vars):
                acc[v] = acc[v] + perturb[m, 0, v, :, cols].astype(jnp.float32) * f
        for v in range(p.vars):
            scr[step * p.vars + v, :, cols] = acc[v]

    @pl.when(step == p.slots - 1)
    def _():
        core = lax.axis_index("mem") % 2
        one = jnp.zeros((1, 1), jnp.float32)
        two = jnp.zeros((1, 1), jnp.float32)
        for k in range(p.group):
            one = one + field[k * p.share, :1, p.nlon : p.nlon + 1]
            two = two + field[k * p.share, :1, p.nlon + SUB : p.nlon + SUB + 1]
        for k in (0, p.half):
            scr[k, :, p.nlon : p.nlon + SUB] = jnp.broadcast_to(one, (p.rows, SUB))
            scr[k, :, p.nlon + SUB : p.nlon + 2 * SUB] = jnp.broadcast_to(two, (p.rows, SUB))
        for k in range(p.half):
            keep[k] = scr[core * p.half + k]
            send[k] = scr[(1 - core) * p.half + k]


def forward(p, perturb, field):
    rows, nlon = p.rows, p.nlon
    shape = (p.half, rows, p.wide)
    spec = pl.BlockSpec(shape, lambda i: (0, 0, 0))
    return pl.pallas_call(
        functools.partial(forward_kernel, p),
        grid=(p.slots,),
        in_specs=[
            pl.BlockSpec((p.members, 1, p.vars, rows, nlon), lambda i: (0, i, 0, 0, 0)),
            pl.BlockSpec((p.members, rows, p.wide), lambda i: (0, 0, 0)),
        ],
        out_specs=[spec, spec],
        out_shape=[jax.ShapeDtypeStruct(shape, jnp.float32)] * 2,
        scratch_shapes=[pltpu.VMEM((2 * p.half, rows, p.wide), jnp.float32)],
        cost_estimate=cost(p, 2),
        compiler_params=ROOM,
        name="forward",
    )(perturb, field)


def roll(x, shift, axis):
    return pltpu.roll(x, shift % x.shape[axis], axis)


def flip(p, pick, sheet):
    for j in range(p.wide // LANES):
        cols = slice(j * LANES, (j + 1) * LANES)
        tiles = [pick(c, m, cols) for m in range(p.share) for c in range(p.window)]
        if p.used < p.lanes:
            tiles.append(jnp.zeros((p.lanes - p.used, LANES), jnp.float32))
        block = jnp.concatenate(tiles, axis=0)
        for t in range(p.tiles):
            sheet[t, cols, :] = block[t * LANES : (t + 1) * LANES].T


def unflip(p, sheet, out, stop):
    for j in range(-(-stop // LANES)):
        low, high = j * LANES, min((j + 1) * LANES, stop)
        block = [sheet[t, low : low + LANES, :].T for t in range(p.tiles)]
        for m in range(p.share):
            for c in range(p.group):
                at = m * p.run + (p.halo + c) * p.rows
                piece = block[at // LANES][at % LANES : at % LANES + p.rows]
                out[c, m, :, low:high] = piece[:, : high - low]


def lane_row(p):
    lane = lax.broadcasted_iota(jnp.int32, (SUB, p.lanes), 1)
    return lane % p.run, lane


def wrap(p, buf):
    buf[0] = roll(buf[p.step], 1, 0)
    buf[p.step + 1] = roll(buf[1], -1, 0)


def tile(t):
    return slice(t * LANES, (t + 1) * LANES)


def sheet_to(p, sheet, buf):
    def one(i, none):
        for t in range(p.tiles):
            buf[i + 1, :, tile(t)] = sheet[t, pl.ds(i, SUB, stride=p.step), :]
        return none
    lax.fori_loop(0, p.step, one, 0, unroll=p.unroll)


def to_sheet(p, buf, sheet):
    def one(i, none):
        for t in range(p.tiles):
            sheet[t, pl.ds(i, SUB, stride=p.step), :] = buf[i + 1, :, tile(t)]
        return none
    lax.fori_loop(0, p.step, one, 0, unroll=p.unroll)


def one_pass(p, src, dst, east, north, south, diag):
    def body(c, carry):
        f, fw, west = carry
        for k in range(p.stride):
            i = 1 + c * p.stride + k
            fe, here = src[i + 1], east[i]
            across = north[i] * roll(f, -1, 1) + south[i] * roll(f, 1, 1)
            dst[i] = (diag[i] * f + across) + (here * fe + west * fw)
            f, fw, west = fe, f, here
        return f, fw, west
    lax.fori_loop(0, p.step // p.stride, body, (src[1], src[0], east[0]))
    wrap(p, dst)


def ten(p, a, b, *coefs):
    def two(_, none):
        one_pass(p, a, b, *coefs)
        one_pass(p, b, a, *coefs)
        return none
    lax.fori_loop(0, PASSES // 2, two, 0)
    if PASSES % 2:
        one_pass(p, a, b, *coefs)
        a[...] = b[...]


def total_of(p, own, term):
    def one(i, acc):
        return acc + term(i + 1)
    acc = lax.fori_loop(0, p.step, one, jnp.zeros((SUB, p.lanes), jnp.float32), unroll=p.unroll)
    return jnp.sum(jnp.where(own, acc, 0.0))


def own_lanes(p):
    row, lane = lane_row(p)
    first = p.halo * p.rows
    return (row >= first) & (row < first + p.group * p.rows) & (lane < p.used)


def first_kernel(p, got, near, far, out, right, east, north, south, diag, sheet, a, b, coef):
    row, lane = lane_row(p)
    low = 0
    high = p.run - 1
    if p.groups > 1:
        here = lax.axis_index("lat") // p.group * p.group - p.halo
        low = jnp.maximum(-here, 0) * p.rows
        high = jnp.minimum(p.lat - here, p.window) * p.rows - 1
    mine = lax.axis_index("mem") % p.parts
    for k in range(max(p.parts // 2, 1)):
        coef[mine ^ k] = near[k]
    for k in range(p.parts // 2):
        coef[mine ^ (p.parts // 2) ^ k] = far[k]
    per = p.piece // LANES

    def pick(which):
        def of(c, m, cols):
            j = cols.start // LANES
            return coef[j // per, c, which, :, tile(j % per)]
        return of
    flip(p, pick(1), sheet)
    sheet_to(p, sheet, south)
    flip(p, pick(0), sheet)
    sheet_to(p, sheet, east)
    wrap(p, east)
    inside = (row >= low) & (row <= high) & (lane < p.used)

    def coefs(i, none):
        lower = jnp.where(inside, south[i + 1], 0.0)
        upper = jnp.where(inside & (row < high), roll(lower, -1, 1), 0.0)
        west = east[i]
        diag[i + 1] = (1.0 - (lower + upper)) - (east[i + 1] + west)
        north[i + 1] = upper
        south[i + 1] = jnp.where(row > low, lower, 0.0)
        return none
    lax.fori_loop(0, p.step, coefs, 0, unroll=p.unroll)
    flip(p, lambda c, m, cols: got[c, m, :, cols], sheet)
    sheet_to(p, sheet, a)
    wrap(p, a)
    ten(p, a, b, east, north, south, diag)

    def keep(i, none):
        right[i + 1] = a[i + 1]
        return none
    lax.fori_loop(0, p.step, keep, 0, unroll=p.unroll)
    rr = total_of(p, own_lanes(p), lambda i: a[i] * a[i])
    ten(p, a, b, east, north, south, diag)
    to_sheet(p, a, sheet)
    sheet[:, p.nlon :, :] = jnp.full((p.tiles, p.wide - p.nlon, LANES), rr)
    unflip(p, sheet, out, p.wide)


def second_kernel(p, got, right, east, north, south, diag, scal, out, resid, ahead, sheet, a, b):
    row, lane = lane_row(p)
    flip(p, lambda c, m, cols: got[c, m, :, cols], sheet)
    if p.groups == 1:
        q = 0.0
        for t in range(p.tiles):
            first = (row[:1, tile(t)] % p.rows == 0) & (lane[:1, tile(t)] < p.run)
            q = q + jnp.sum(jnp.where(first, sheet[t, p.nlon : p.nlon + 1, :], 0.0))
        q = jnp.full((SUB, LANES), q)
    else:
        q = scal[1][:SUB]
    rr = scal[0][:SUB]
    alpha = rr / (rr + q)
    ahead[...] = alpha
    sheet_to(p, sheet, a)
    wrap(p, a)
    ten(p, a, b, east, north, south, diag)
    alpha = jnp.broadcast_to(alpha[:, :1], (SUB, p.lanes))

    def cut(i, sums):
        r0 = right[i + 1]
        r = r0 - alpha * (r0 + a[i + 1])
        a[i + 1] = r
        resid[i + 1] = r
        return sums[0] + r * r, sums[1] + r * r0
    zero = jnp.zeros((SUB, p.lanes), jnp.float32)
    rr1, rb = lax.fori_loop(0, p.step, cut, (zero, zero), unroll=p.unroll)
    wrap(p, a)
    own = own_lanes(p)
    rr1 = jnp.sum(jnp.where(own, rr1, 0.0))
    rb = jnp.sum(jnp.where(own, rb, 0.0))
    ten(p, a, b, east, north, south, diag)
    to_sheet(p, a, sheet)
    sheet[:, p.nlon :, :] = jnp.zeros((p.tiles, p.wide - p.nlon, LANES), jnp.float32)
    sheet[:, p.nlon : p.nlon + SUB, :] = jnp.full((p.tiles, SUB, LANES), rr1)
    sheet[:, p.nlon + SUB : p.nlon + 2 * SUB, :] = jnp.full((p.tiles, SUB, LANES), rb)
    unflip(p, sheet, out, p.wide)


def back_kernel(p, field, out, sheet):
    to_sheet(p, field, sheet)
    sheet[:, p.nlon :, :] = jnp.zeros((p.tiles, p.wide - p.nlon, LANES), jnp.float32)
    unflip(p, sheet, out, p.nlon)


def buffers(p):
    buf = (p.step + 2, SUB, p.lanes)
    return [pltpu.VMEM((p.tiles, p.wide, LANES), jnp.float32)] + [pltpu.VMEM(buf, jnp.float32)] * 2


def vmem(n):
    return [pl.BlockSpec(memory_space=pltpu.VMEM)] * n


def first_half(p, got, near, far):
    buf = jax.ShapeDtypeStruct((p.step + 2, SUB, p.lanes), jnp.float32)
    back = jax.ShapeDtypeStruct((p.group, p.share, p.rows, p.wide), jnp.float32)
    coef = pltpu.VMEM((p.parts, p.window, 2, p.rows, p.piece), jnp.float32)
    return pl.pallas_call(
        functools.partial(first_kernel, p),
        in_specs=vmem(3),
        out_specs=vmem(6),
        out_shape=[back] + [buf] * 5,
        scratch_shapes=buffers(p) + [coef],
        compiler_params=ROOM,
        name="smooth_first",
    )(got, near, far)


def second_half(p, got, right, east, north, south, diag, scal):
    buf = jax.ShapeDtypeStruct((p.step + 2, SUB, p.lanes), jnp.float32)
    back = jax.ShapeDtypeStruct((p.group, p.share, p.rows, p.wide), jnp.float32)
    return pl.pallas_call(
        functools.partial(second_kernel, p),
        in_specs=vmem(7),
        out_specs=vmem(3),
        out_shape=[back, buf, jax.ShapeDtypeStruct((SUB, LANES), jnp.float32)],
        scratch_shapes=buffers(p),
        compiler_params=ROOM,
        name="smooth_second",
    )(got, right, east, north, south, diag, scal)


def to_rows(p, field):
    return pl.pallas_call(
        functools.partial(back_kernel, p),
        in_specs=vmem(1),
        out_specs=vmem(1)[0],
        out_shape=jax.ShapeDtypeStruct((p.group, p.share, p.rows, p.nlon), jnp.float32),
        scratch_shapes=buffers(p)[:1],
        cost_estimate=pl.CostEstimate(flops=0, bytes_accessed=2**22, transcendentals=0),
        compiler_params=ROOM,
        name="to_rows",
    )(field)


def scalars(p, mine, scal):
    rr1 = mine[0, :1, p.nlon : p.nlon + 1]
    rb = mine[0, :1, p.nlon + SUB : p.nlon + SUB + 1]
    rr = scal[0][:1, :1]
    beta = rr1 / rr
    return rr1, beta, rr1 + beta * (2.0 * rb + beta * rr)


def test_kernel(p, weight, total, mine, scal, part):
    at = lax.axis_index("mem") % 2 * p.half
    beta = scalars(p, mine, scal)[1]
    acc = jnp.zeros((p.rows, p.nlon), jnp.float32)
    for k in range(p.half):
        t = mine[k, :, : p.nlon] + beta * total[at + k]
        acc = acc + weight[jnp.minimum(at + k, p.fields - 1)] * t * t
    acc = jnp.broadcast_to(jnp.sum(acc, axis=(0, 1), keepdims=True), part.shape[1:])
    for k in range(part.shape[0]):
        part[k] = acc


def test(p, weight, total, mine, scal):
    copies = 1 if p.groups > 1 else p.mem * p.lat
    return pl.pallas_call(
        functools.partial(test_kernel, p),
        in_specs=vmem(4),
        out_specs=vmem(1)[0],
        out_shape=jax.ShapeDtypeStruct((copies, SUB, LANES), jnp.float32),
        compiler_params=ROOM,
        name="last_sums",
    )(weight, total, mine, scal)


def last_kernel(p, total, mine, other, scal, ahead, q, right, resid, grown, control):
    core = lax.axis_index("mem") % 2
    rr1, beta, length = scalars(p, mine, scal)
    every = q[0]
    for k in range(1, q.shape[0]):
        every = every + q[k]
    every = every[:1, :1] * (2.0 / p.mem)
    step1 = ahead[:1, :1]
    step2 = rr1 / (length + every)
    near = step1 + step2 * beta
    for half, at in ((mine, core * p.half), (other, (1 - core) * p.half)):
        for k in range(p.half):
            @pl.when(at + k < p.fields)
            def _():
                grown[at + k] = near * total[at + k] + step2 * half[k, :, : p.nlon]
    for m in range(p.members):
        control[m] = near * right[m] + step2 * resid[m]


def last(p, total, mine, other, scal, ahead, q, right, resid):
    return pl.pallas_call(
        functools.partial(last_kernel, p),
        in_specs=vmem(8),
        out_specs=vmem(2),
        out_shape=[
            jax.ShapeDtypeStruct((p.fields, p.rows, p.nlon), jnp.float32),
            jax.ShapeDtypeStruct((p.members, p.rows, p.nlon), jnp.float32),
        ],
        compiler_params=ROOM,
        name="last_update",
    )(total, mine, other, scal, ahead, q, right, resid)


def swap(p, x, axis, bit, count):
    return lax.ppermute(x, axis, [(i, i ^ bit) for i in range(count)])


def turn(p, x):
    if p.groups == 1:
        return lax.all_to_all(x, "lat", 0, 0)
    sets = [[g * p.group + i for i in range(p.group)] for g in range(p.groups)]
    return lax.all_to_all(x, "lat", 0, 0, axis_index_groups=sets)


def widen(p, x):
    if p.groups == 1:
        return x
    gap = p.group
    up = [(i, i + gap) for i in range(p.lat - gap)]
    down = [(i + gap, i) for i in range(p.lat - gap)]
    before = lax.ppermute(x[-p.halo :], "lat", up)
    after = lax.ppermute(x[: p.halo], "lat", down)
    return jnp.concatenate([before, x, after], axis=0)


def member_sum(p, keep, send):
    mine = keep + swap(p, send, "mem", 1, p.mem)
    bit = 2
    while bit < p.mem:
        mine = mine + swap(p, mine, "mem", bit, p.mem)
        bit *= 2
    if p.groups > 1:
        tail = lax.psum(mine[:1, :, p.nlon :], "lat") / p.group
        mine = lax.dynamic_update_slice(mine, tail, (0, 0, p.nlon))
    return mine


def coefficients(p, lon_coef, lat_coef):
    both = jnp.pad(jnp.stack([lon_coef, lat_coef]), ((0, 0), (0, 0), (0, p.wide - p.nlon)))
    part = lax.axis_index("mem") % p.parts
    both = lax.dynamic_slice_in_dim(both, part * p.piece, p.piece, axis=2)
    both = jnp.broadcast_to(both[None], (p.group, 2, p.rows, p.piece))
    near = widen(p, turn(p, both))[None]
    if p.parts == 1:
        return near, near
    if p.parts == 4:
        near = jnp.concatenate([near, swap(p, near, "mem", 1, p.mem)])
    return near, swap(p, near, "mem", p.parts // 2, p.mem)


def per_device(perturb, innovation, obs_weight, lon_coef, lat_coef):
    p = Plan(perturb, lat_coef, lax.axis_size("mem"), lax.axis_size("lat"))
    flat = lambda x: x.reshape(p.fields, p.rows, p.nlon)
    by_rank = lambda x: x.reshape((p.members,) + x.shape[2:])
    weight = flat(obs_weight)
    by_member = perturb.reshape(p.members, p.fields, p.rows, p.nlon)

    near, far = coefficients(p, lon_coef, lat_coef)
    (sent,) = adjoint(p, by_member, weight, flat(innovation), second=False)
    back, right, *coefs = first_half(p, widen(p, turn(p, sent)), near, far)
    field, rows_right = lax.optimization_barrier((turn(p, back), to_rows(p, right)))
    rows_right = by_rank(turn(p, rows_right))
    mine = member_sum(p, *forward(p, perturb, by_rank(field)))
    other = swap(p, mine, "mem", 1, p.mem)
    sent, total, scal = adjoint(p, by_member, weight, mine, other, second=True)
    sent, rows_right = lax.optimization_barrier((sent, rows_right))
    if p.groups > 1:
        scal = jnp.concatenate([scal[:1], lax.psum(scal[1:], "lat")], axis=0)
    back, resid, ahead = second_half(p, widen(p, turn(p, sent)), right, *coefs, scal)
    field, rows_resid = lax.optimization_barrier((turn(p, back), to_rows(p, resid)))
    rows_resid = by_rank(turn(p, rows_resid))
    mine = member_sum(p, *forward(p, perturb, by_rank(field)))
    mine, rows_resid = lax.optimization_barrier((mine, rows_resid))
    other = swap(p, mine, "mem", 1, p.mem)
    q = test(p, weight, total, mine, scal)
    q = lax.all_to_all(q, ("mem", "lat"), 0, 0) if p.groups == 1 else lax.psum(q, ("mem", "lat"))
    grown, control = last(p, total, mine, other, scal, ahead, q, rows_right, rows_resid)
    return control, grown.reshape(p.slots, p.vars, p.rows, p.nlon)


def solution(mesh):
    return jax.shard_map(
        per_device,
        mesh=mesh,
        in_specs=(
            P("mem", None, None, "lat", None),
            P(None, None, "lat", None),
            P(None, None, "lat", None),
            P("lat", None),
            P("lat", None),
        ),
        out_specs=(P("mem", "lat", None), P(None, None, "lat", None)),
        check_vma=False,
    )
```

time: 287 us -> 220 us (0.77)
  blocking collectives: 138 us -> 37.5 us
  Pallas kernels: 99.6 us -> 41.8 us
  waiting for transfers between devices: 34.9 us -> 82 us
  starting transfers between devices: 6.9 us -> 32.5 us
  local copies, waits for them, and re-layouts: 2.38 us -> 23.8 us
    all_to_all x5 -> x1, blocking collectives: 138 us -> 26.2 us  [turn(): return lax.all_to_all(x, 'lat', 0, 0)]
    all_to_all x0 -> x6, waiting for transfers between devices: none -> 46.4 us  [turn(): return lax.all_to_all(x, 'lat', 0, 0)]
    pallas_call x4 -> x6, Pallas kernels: 74.7 us -> 33.3 us  [the longest x1 14.9 us: first_half(): pl.pallas_call(functools.partial(first_kernel, p), in_specs=vmem(3), out_...]
    all_to_all x0 -> x6, starting transfers between devices: none -> 27.6 us  [turn(): return lax.all_to_all(x, 'lat', 0, 0)]
    unnamed x9 -> x38, local copies, waits for them, and re-layouts: 2.38 us -> 23.1 us
    all_to_all x0 -> x1, blocking collectives: none -> 11.3 us  [per_device(): lax.all_to_all(q, ('mem', 'lat'), 0, 0)]
    pallas_call x2, Pallas kernels: 14.8 us -> 4.95 us  [adjoint(): pl.pallas_call(functools.partial(adjoint_kernel, p, second), grid=(p.grou...]
    pallas_call x2, Pallas kernels: 10.1 us -> 3.55 us  [forward(): pl.pallas_call(functools.partial(forward_kernel, p), grid=(p.slots,), in_...]
  transfers between devices with their start and end apart: 9 -> 14, of which waited for: 9 -> 11; matrix products, arithmetic and copies ran while one was open for 0% -> 0% of each run, Pallas kernels for 0% -> 5%
where the time goes in v2:
time: 220 us; the launch traced here: 219 us
  waiting for transfers between devices  82 us (37%)
  Pallas kernels  41.8 us (19%)
  blocking collectives  37.5 us (17%)
  starting transfers between devices  32.5 us (15%)
  local copies, waits for them, and re-layouts  23.8 us (11%)
    all_to_all x6, waiting for transfers between devices, turn(): return lax.all_to_all(x, 'lat', 0, 0)  46.4 us
    ppermute x8, waiting for transfers between devices, swap(): return lax.ppermute(x, axis, [(i, i ^ bit) for i in range(count)])  35.6 us
    all_to_all x6, starting transfers between devices, turn(): return lax.all_to_all(x, 'lat', 0, 0)  27.6 us
    all_to_all x1, blocking collectives, turn(): return lax.all_to_all(x, 'lat', 0, 0)  26.2 us
    unnamed x38, local copies, waits for them, and re-layouts  23.1 us
    pallas_call x1, Pallas kernels, first_half(): pl.pallas_call(functools.partial(first_kernel, p), in_specs=vmem(3), out_...  14.9 us
    pallas_call x1, Pallas kernels, second_half(): pl.pallas_call(functools.partial(second_kernel, p), in_specs=vmem(7), out...  12.5 us
    all_to_all x1, blocking collectives, per_device(): lax.all_to_all(q, ('mem', 'lat'), 0, 0)  11.3 us
  transfers between devices with their start and end apart: 14, of which 11 were waited for; matrix products, arithmetic and copies ran while one was open for 0% of the time, Pallas kernels for 5%

profile of v2, /device:TPU:0, one launch (start us, length us, event | category | flops | bytes accessed | tf_op | source)
XLA Modules:
  0.0 219.2 jit_solution(6437358813223133708)
XLA Ops:
  2.1 7.3 %all-to-all-start.1 = ((f32[8,2,8,384]{3,2,1,0:T(8,128)}), f32[8,2,8,384]{3,2,1,0:T(8,128)S(1)}, u32[]{:S(2)}, u32[]{:S(2)}) async-start(f32[8,2,8,384]{3,2,1,0:T(8,128)} %broadcast_in_dim.4), calls=%async_computation.1 | async-start | bytes 393216 | tf_op jit(solution)/shard_map/all_to_all | solution.py:492
  9.4 2.7 %copy-done = bf16[16,3,5,8,1440]{4,3,2,1,0:T(8,128)(2,1)S(1)} copy-done((bf16[16,3,5,8,1440]{4,3,2,1,0:T(8,128)(2,1)S(1)}, bf16[16,3,5,8,1440]{4,3,2,1,0:T(8,128)(2,1)}, u32[]{:S(2)}) %copy-start) | copy-done | bytes 5529624
  12.1 1.1 copy-done.3
  13.2 1.1 copy-done.18
  14.3 3.4 %adjoint_first.1 = f32[8,2,8,1536]{3,2,1,0:T(8,128)} custom-call(bf16[16,15,8,1440]{3,2,1,0:T(8,128)(2,1)S(1)} %bitcast.11, f32[15,8,1440]{2,1,0:T(8,128)S(1)} %bitcast.13, f32[15,8,1440]{2,1,0:T(8,128)S(1)} %bitcast.20), custom_call_target="tpu_custom_call" | custom-call | flops 5529600 | bytes 5529600 | tf_op jit(solution)/shard_map/adjoint_first/pallas_call | solution.py:101
  17.7 6.0 %all-to-all-start = ((f32[8,2,8,1536]{3,2,1,0:T(8,128)}), f32[8,2,8,1536]{3,2,1,0:T(8,128)S(1)}, u32[]{:S(2)}, u32[]{:S(2)}) async-start(f32[8,2,8,1536]{3,2,1,0:T(8,128)} %adjoint_first.1), calls=%async_computation | async-start | bytes 1572864 | tf_op jit(solution)/shard_map/all_to_all | solution.py:492
  23.7 1.4 collective-permute-done
  25.2 1.6 collective-permute-start.1
  26.7 9.7 %collective-permute-done.1.far = f32[2,8,2,8,384]{4,3,2,1,0:T(8,128)S(1)} collective-permute-done((f32[2,8,2,8,384]{4,3,2,1,0:T(8,128)S(1)}, f32[2,8,2,8,384]{4,3,2,1,0:T(8,128)S(1)}, u32[]{:S(2)}, u32[]{:S(2)}) %collective-permute-start.1) | collective-permute-done | bytes 393248 | tf_op jit(solution)/shard_map/ppermute | solution.py:487
  36.4 7.0 %all-to-all-done.got = f32[8,2,8,1536]{3,2,1,0:T(8,128)S(1)} async-done(((f32[8,2,8,1536]{3,2,1,0:T(8,128)}), f32[8,2,8,1536]{3,2,1,0:T(8,128)S(1)}, u32[]{:S(2)}, u32[]{:S(2)}) %all-to-all-start) | async-done | bytes 786464 | tf_op jit(solution)/shard_map/all_to_all | solution.py:492
  43.4 14.9 %smooth_first.1 = (f32[8,2,8,1536]{3,2,1,0:T(8,128)}, f32[182,8,128]{2,1,0:T(8,128)S(1)}, f32[182,8,128]{2,1,0:T(8,128)S(1)}, f32[182,8,128]{2,1,0:T(8,128)S(1)}...) custom-call(f32[8,2,8,1536]{3,2,1,0:T(8,128)S(1)} %all-to-all-done.got, ...), custom_call_target="tpu_custom_call" | custom-call | tf_op jit(solution)/shard_map/smooth_first/pallas_call | solution.py:383
  58.3 0.9 copy-done.10
  59.1 0.9 copy-done.12
  60.0 0.9 copy-done.14
  61.8 3.5 %all-to-all-start.2 = ((f32[8,2,8,1536]{3,2,1,0:T(8,128)}), f32[8,2,8,1536]{3,2,1,0:T(8,128)S(1)}, u32[]{:S(2)}, u32[]{:S(2)}) async-start(f32[8,2,8,1536]{3,2,1,0:T(8,128)} %get-tuple-element.28), calls=%async_computation.2 | async-start | bytes 1572864 | tf_op jit(solution)/shard_map/all_to_all | solution.py:492
  65.3 1.3 to_rows.2
  66.6 19.0 %all-to-all-done.2 = f32[8,2,8,1536]{3,2,1,0:T(8,128)S(1)} async-done(((f32[8,2,8,1536]{3,2,1,0:T(8,128)}), f32[8,2,8,1536]{3,2,1,0:T(8,128)S(1)}, u32[]{:S(2)}, u32[]{:S(2)}) %all-to-all-start.2) | async-done | bytes 786464 | tf_op jit(solution)/shard_map/all_to_all | solution.py:492
  85.6 3.5 %all-to-all-start.3 = ((f32[8,2,8,1440]{3,2,1,0:T(8,128)}), f32[8,2,8,1440]{3,2,1,0:T(8,128)S(1)}, u32[]{:S(2)}, u32[]{:S(2)}) async-start(f32[8,2,8,1440]{3,2,1,0:T(8,128)} %to_rows.2), calls=%async_computation.3 | async-start | bytes 1572864 | tf_op jit(solution)/shard_map/all_to_all | solution.py:492
  89.2 2.7 %copy-done.1 = bf16[16,3,5,8,1440]{4,3,2,1,0:T(8,128)(2,1)S(1)} copy-done((bf16[16,3,5,8,1440]{4,3,2,1,0:T(8,128)(2,1)S(1)}, bf16[16,3,5,8,1440]{4,3,2,1,0:T(8,128)(2,1)}, u32[]{:S(2)}) %copy-start.1) | copy-done | bytes 5529624
  91.9 1.9 forward.2
  93.8 1.7 collective-permute-done.2
  95.6 1.6 collective-permute-start.3
  97.1 9.7 %collective-permute-done.3 = f32[8,8,1536]{2,1,0:T(8,128)S(1)} collective-permute-done((f32[8,8,1536]{2,1,0:T(8,128)S(1)}, f32[8,8,1536]{2,1,0:T(8,128)S(1)}, u32[]{:S(2)}, u32[]{:S(2)}) %collective-permute-start.3) | collective-permute-done | bytes 393248 | tf_op jit(solution)/shard_map/ppermute | solution.py:487
  106.9 1.7 collective-permute-done.4.refs_3_
  108.6 1.5 adjoint_second.1
  110.2 0.9 copy-done.5
  111.1 26.2 %all_to_all.40.got = f32[8,2,8,1536]{3,2,1,0:T(8,128)S(1)} all-to-all(f32[8,2,8,1536]{3,2,1,0:T(8,128)S(1)} %get-tuple-element.36), channel_id=1, replica_groups=mesh['mem'=4,'lat'=8] {'lat'}, dimensions={0} | all-to-all | bytes 1572864 | tf_op jit(solution)/shard_map/all_to_all | solution.py:492
  137.3 1.1 copy-done.11
  138.4 1.1 copy-done.13
  139.5 1.1 copy-done.15
  140.6 1.1 copy-done.17
  141.7 12.5 %smooth_second.1 = (f32[8,2,8,1536]{3,2,1,0:T(8,128)S(1)}, f32[182,8,128]{2,1,0:T(8,128)S(1)}, f32[8,128]{1,0:T(8,128)S(1)}) custom-call(f32[8,2,8,1536]{3,2,1,0:T(8,128)S(1)} %all_to_all.40.got, f32[182,8,128]{2,1,0:T(8,128)S(1)} %get-tuple-element.29.field.right, f32[182,8,128]{2,1,0:T(8,128)S(1)} %copy-done.11, f32[182,8,128]{2,1,0:T(8,128)S(1)} %copy-done.13, ...), custom_call_target="tpu_custom_call" | custom-call | tf_op jit(solution)/shard_map/smooth_second/pallas_call | solution.py:397
  154.2 0.9 copy-done.7
  155.1 0.9 copy-done.8
  156.0 3.6 %all-to-all-start.5 = ((f32[8,2,8,1536]{3,2,1,0:T(8,128)}), f32[8,2,8,1536]{3,2,1,0:T(8,128)S(1)}, u32[]{:S(2)}, u32[]{:S(2)}) async-start(f32[8,2,8,1536]{3,2,1,0:T(8,128)} %copy-done.7), calls=%async_computation.5 | async-start | bytes 1572864 | tf_op jit(solution)/shard_map/all_to_all | solution.py:492
  159.6 1.1 copy-done.9
  160.8 1.2 to_rows.3
  162.0 17.5 %all-to-all-done.5 = f32[8,2,8,1536]{3,2,1,0:T(8,128)S(1)} async-done(((f32[8,2,8,1536]{3,2,1,0:T(8,128)}), f32[8,2,8,1536]{3,2,1,0:T(8,128)S(1)}, u32[]{:S(2)}, u32[]{:S(2)}) %all-to-all-start.5) | async-done | bytes 786464 | tf_op jit(solution)/shard_map/all_to_all | solution.py:492
  179.5 3.5 %all-to-all-start.6 = ((f32[8,2,8,1440]{3,2,1,0:T(8,128)}), f32[8,2,8,1440]{3,2,1,0:T(8,128)S(1)}, u32[]{:S(2)}, u32[]{:S(2)}) async-start(f32[8,2,8,1440]{3,2,1,0:T(8,128)} %to_rows.3), calls=%async_computation.6 | async-start | bytes 1572864 | tf_op jit(solution)/shard_map/all_to_all | solution.py:492
  183.1 2.7 %copy-done.2 = bf16[16,3,5,8,1440]{4,3,2,1,0:T(8,128)(2,1)S(1)} copy-done((bf16[16,3,5,8,1440]{4,3,2,1,0:T(8,128)(2,1)S(1)}, bf16[16,3,5,8,1440]{4,3,2,1,0:T(8,128)(2,1)}, u32[]{:S(2)}) %copy-start.2) | copy-done | bytes 5529624
  185.8 1.7 forward.3
  187.5 1.7 collective-permute-done.5
  189.3 1.6 collective-permute-start.6
  190.9 9.7 %collective-permute-done.6 = f32[8,8,1536]{2,1,0:T(8,128)S(1)} collective-permute-done((f32[8,8,1536]{2,1,0:T(8,128)S(1)}, f32[8,8,1536]{2,1,0:T(8,128)S(1)}, u32[]{:S(2)}, u32[]{:S(2)}) %collective-permute-start.6) | collective-permute-done | bytes 393248 | tf_op jit(solution)/shard_map/ppermute | solution.py:487
  200.6 2.8 %all-to-all-done.6 = f32[8,2,8,1440]{3,2,1,0:T(8,128)S(1)} async-done(((f32[8,2,8,1440]{3,2,1,0:T(8,128)}), f32[8,2,8,1440]{3,2,1,0:T(8,128)S(1)}, u32[]{:S(2)}, u32[]{:S(2)}) %all-to-all-start.6) | async-done | bytes 737312 | tf_op jit(solution)/shard_map/all_to_all | solution.py:492
  203.4 1.1 copy-done.6
  204.9 11.3 %all_to_all.41.q = f32[32,8,128]{2,1,0:T(8,128)S(1)} all-to-all(f32[32,8,128]{2,1,0:T(8,128)S(1)} %last_sums.1), channel_id=1, replica_groups=mesh['mem'=4,'lat'=8] {'mem','lat'}, dimensions={0} | all-to-all | bytes 262144 | tf_op jit(solution)/shard_map/all_to_all | solution.py:558
  216.2 3.0 %last_update.1 = (f32[15,8,1440]{2,1,0:T(8,128)}, f32[16,8,1440]{2,1,0:T(8,128)}) custom-call(f32[16,8,1440]{2,1,0:T(8,128)S(1)} %copy-done.6, f32[8,8,1536]{2,1,0:T(8,128)S(1)} %add.26.mine, f32[8,8,1536]{2,1,0:T(8,128)S(1)} %collective-permute-done.7.other, f32[2,8,128]{2,1,0:T(8,128)S(1)} %get-tuple-element.41.scal, ...), custom_call_target="tpu_custom_call" | custom-call | tf_op jit(solution)/shard_map/last_update/pallas_call | solution.py:473
  (37 shorter events, 3.2 us)
Async XLA Ops:
  2.1 15.6 %all-to-all-start.1 = ((f32[8,2,8,384]{3,2,1,0:T(8,128)}), f32[8,2,8,384]{3,2,1,0:T(8,128)S(1)}, u32[]{:S(2)}, u32[]{:S(2)}) async-start(f32[8,2,8,384]{3,2,1,0:T(8,128)} %broadcast_in_dim.4), calls=%async_computation.1 | async-start | bytes 393216 | tf_op jit(solution)/shard_map/all_to_all | solution.py:492
  9.4 2.7 %copy-start = (bf16[16,3,5,8,1440]{4,3,2,1,0:T(8,128)(2,1)S(1)}, bf16[16,3,5,8,1440]{4,3,2,1,0:T(8,128)(2,1)}, u32[]{:S(2)}) copy-start(bf16[16,3,5,8,1440]{4,3,2,1,0:T(8,128)(2,1)} %perturb.3) | copy-start | bytes 16588804
  12.1 1.1 copy-start.3
  13.2 1.1 copy-start.18
  17.7 25.7 %all-to-all-start = ((f32[8,2,8,1536]{3,2,1,0:T(8,128)}), f32[8,2,8,1536]{3,2,1,0:T(8,128)S(1)}, u32[]{:S(2)}, u32[]{:S(2)}) async-start(f32[8,2,8,1536]{3,2,1,0:T(8,128)} %adjoint_first.1), calls=%async_computation | async-start | bytes 1572864 | tf_op jit(solution)/shard_map/all_to_all | solution.py:492
  23.7 1.4 collective-permute-start
  25.2 11.2 %collective-permute-start.1 = (f32[2,8,2,8,384]{4,3,2,1,0:T(8,128)S(1)}, f32[2,8,2,8,384]{4,3,2,1,0:T(8,128)S(1)}, u32[]{:S(2)}, u32[]{:S(2)}) collective-permute-start(f32[2,8,2,8,384]{4,3,2,1,0:T(8,128)S(1)} %pad_maximum_fusion.near), channel_id=1, source_target_pairs={{0,16},{8,24},{16,0},{24,8},{1,17},{9,25},{17,1},{25,9},{2,18},{10... | collective-permute-start | bytes 1179656 | tf_op jit(solution)/shard_map/ppermute | solution.py:487
  58.3 0.9 copy-start.10
  59.1 0.9 copy-start.12
  60.0 0.9 copy-start.14
  60.9 0.9 copy-start.16
  61.8 23.9 %all-to-all-start.2 = ((f32[8,2,8,1536]{3,2,1,0:T(8,128)}), f32[8,2,8,1536]{3,2,1,0:T(8,128)S(1)}, u32[]{:S(2)}, u32[]{:S(2)}) async-start(f32[8,2,8,1536]{3,2,1,0:T(8,128)} %get-tuple-element.28), calls=%async_computation.2 | async-start | bytes 1572864 | tf_op jit(solution)/shard_map/all_to_all | solution.py:492
  65.3 43.3 %copy-start.4 = (f32[3,5,8,1440]{3,2,1,0:T(8,128)S(1)}, f32[3,5,8,1440]{3,2,1,0:T(8,128)}, u32[]{:S(2)}) copy-start(f32[3,5,8,1440]{3,2,1,0:T(8,128)} %param.7) | copy-start | bytes 2073604
  85.6 25.4 %all-to-all-start.3 = ((f32[8,2,8,1440]{3,2,1,0:T(8,128)}), f32[8,2,8,1440]{3,2,1,0:T(8,128)S(1)}, u32[]{:S(2)}, u32[]{:S(2)}) async-start(f32[8,2,8,1440]{3,2,1,0:T(8,128)} %to_rows.2), calls=%async_computation.3 | async-start | bytes 1572864 | tf_op jit(solution)/shard_map/all_to_all | solution.py:492
  89.2 2.7 %copy-start.1 = (bf16[16,3,5,8,1440]{4,3,2,1,0:T(8,128)(2,1)S(1)}, bf16[16,3,5,8,1440]{4,3,2,1,0:T(8,128)(2,1)}, u32[]{:S(2)}) copy-start(bf16[16,3,5,8,1440]{4,3,2,1,0:T(8,128)(2,1)} %perturb.3) | copy-start | bytes 16588804
  93.7 1.8 collective-permute-start.2
  95.6 11.2 %collective-permute-start.3 = (f32[8,8,1536]{2,1,0:T(8,128)S(1)}, f32[8,8,1536]{2,1,0:T(8,128)S(1)}, u32[]{:S(2)}, u32[]{:S(2)}) collective-permute-start(f32[8,8,1536]{2,1,0:T(8,128)S(1)} %add.23), channel_id=1, source_target_pairs={{0,16},{8,24},{16,0},{24,8},{1,17},{9,25},{17,1},{25,9},{2,18},{10... | collective-permute-start | bytes 1179656 | tf_op jit(solution)/shard_map/ppermute | solution.py:487
  106.8 1.8 collective-permute-start.4
  110.2 0.9 copy-start.5
  137.3 1.1 copy-start.11
  138.4 1.1 copy-start.13
  139.5 1.1 copy-start.15
  140.6 1.1 copy-start.17
  154.2 0.9 copy-start.7
  155.1 0.9 copy-start.8
  156.0 23.5 %all-to-all-start.5 = ((f32[8,2,8,1536]{3,2,1,0:T(8,128)}), f32[8,2,8,1536]{3,2,1,0:T(8,128)S(1)}, u32[]{:S(2)}, u32[]{:S(2)}) async-start(f32[8,2,8,1536]{3,2,1,0:T(8,128)} %copy-done.7), calls=%async_computation.5 | async-start | bytes 1572864 | tf_op jit(solution)/shard_map/all_to_all | solution.py:492
  159.6 1.1 copy-start.9
  179.5 23.9 %all-to-all-start.6 = ((f32[8,2,8,1440]{3,2,1,0:T(8,128)}), f32[8,2,8,1440]{3,2,1,0:T(8,128)S(1)}, u32[]{:S(2)}, u32[]{:S(2)}) async-start(f32[8,2,8,1440]{3,2,1,0:T(8,128)} %to_rows.3), calls=%async_computation.6 | async-start | bytes 1572864 | tf_op jit(solution)/shard_map/all_to_all | solution.py:492
  183.1 2.7 %copy-start.2 = (bf16[16,3,5,8,1440]{4,3,2,1,0:T(8,128)(2,1)S(1)}, bf16[16,3,5,8,1440]{4,3,2,1,0:T(8,128)(2,1)}, u32[]{:S(2)}) copy-start(bf16[16,3,5,8,1440]{4,3,2,1,0:T(8,128)(2,1)} %perturb.3) | copy-start | bytes 16588804
  187.5 1.8 collective-permute-start.5
  189.3 11.2 %collective-permute-start.6 = (f32[8,8,1536]{2,1,0:T(8,128)S(1)}, f32[8,8,1536]{2,1,0:T(8,128)S(1)}, u32[]{:S(2)}, u32[]{:S(2)}) collective-permute-start(f32[8,8,1536]{2,1,0:T(8,128)S(1)} %add.25), channel_id=1, source_target_pairs={{0,16},{8,24},{16,0},{24,8},{1,17},{9,25},{17,1},{25,9},{2,18},{10... | collective-permute-start | bytes 1179656 | tf_op jit(solution)/shard_map/ppermute | solution.py:487
  203.4 12.8 %collective-permute-start.7 = (f32[8,8,1536]{2,1,0:T(8,128)S(1)}, f32[8,8,1536]{2,1,0:T(8,128)S(1)}, u32[]{:S(2)}, u32[]{:S(2)}) collective-permute-start(f32[8,8,1536]{2,1,0:T(8,128)S(1)} %add.26.mine), channel_id=1, source_target_pairs={{0,8},{8,0},{16,24},{24,16},{1,9},{9,1},{17,25},{25,17},{2,10},{10... | collective-permute-start | bytes 1179656 | tf_op jit(solution)/shard_map/ppermute | solution.py:487
  203.4 1.1 copy-start.6

commit v3 on v2

--- a/solution.py
+++ b/solution.py
@@ -39,7 +39,7 @@
         self.tiles = self.lanes // LANES
         self.step = self.nlon // SUB
         self.unroll = max(u for u in range(1, 21) if self.step % u == 0)
-        self.stride = max(u for u in range(1, 91) if self.step % u == 0)
+        self.stride = max(u for u in range(1, 181) if self.step % u == 0)
         self.parts = max(
             q for q in (1, 2, 4) if mem % q == 0 and self.wide % (q * LANES) == 0
         )
@@ -270,14 +270,32 @@
     return (row >= first) & (row < first + p.group * p.rows) & (lane < p.used)
 
 
-def first_kernel(p, got, near, far, out, right, east, north, south, diag, sheet, a, b, coef):
+def ends(p):
+    if p.groups == 1:
+        return 0, p.run - 1
+    here = lax.axis_index("lat") // p.group * p.group - p.halo
+    return jnp.maximum(-here, 0) * p.rows, jnp.minimum(p.lat - here, p.window) * p.rows - 1
+
+
+def spread(p, low, high, lower, east, north, south, diag):
     row, lane = lane_row(p)
-    low = 0
-    high = p.run - 1
-    if p.groups > 1:
-        here = lax.axis_index("lat") // p.group * p.group - p.halo
-        low = jnp.maximum(-here, 0) * p.rows
-        high = jnp.minimum(p.lat - here, p.window) * p.rows - 1
+
+    def coefs(i, none):
+        below = lower[i + 1]
+        above = jnp.where(row < high, roll(below, -1, 1), 0.0)
+        diag[i + 1] = (1.0 - (below + above)) - (east[i + 1] + east[i])
+        north[i + 1] = above
+        south[i + 1] = jnp.where(row > low, below, 0.0)
+        return none
+    lax.fori_loop(0, p.step, coefs, 0, unroll=p.unroll)
+
+
+def first_kernel(p, got, near, far, out, *refs):
+    stores, sheet, a, b, north, south, diag, right, east, lower, rows_right, coef, sem = (
+        refs[:4], *refs[4:]
+    )
+    row, lane = lane_row(p)
+    low, high = ends(p)
     mine = lax.axis_index("mem") % p.parts
     for k in range(max(p.parts // 2, 1)):
         coef[mine ^ k] = near[k]
@@ -291,21 +309,17 @@
             return coef[j // per, c, which, :, tile(j % per)]
         return of
     flip(p, pick(1), sheet)
-    sheet_to(p, sheet, south)
+    sheet_to(p, sheet, lower)
     flip(p, pick(0), sheet)
     sheet_to(p, sheet, east)
     wrap(p, east)
     inside = (row >= low) & (row <= high) & (lane < p.used)
 
-    def coefs(i, none):
-        lower = jnp.where(inside, south[i + 1], 0.0)
-        upper = jnp.where(inside & (row < high), roll(lower, -1, 1), 0.0)
-        west = east[i]
-        diag[i + 1] = (1.0 - (lower + upper)) - (east[i + 1] + west)
-        north[i + 1] = upper
-        south[i + 1] = jnp.where(row > low, lower, 0.0)
+    def clean(i, none):
+        lower[i + 1] = jnp.where(inside, lower[i + 1], 0.0)
         return none
-    lax.fori_loop(0, p.step, coefs, 0, unroll=p.unroll)
+    lax.fori_loop(0, p.step, clean, 0, unroll=p.unroll)
+    spread(p, low, high, lower, east, north, south, diag)
     flip(p, lambda c, m, cols: got[c, m, :, cols], sheet)
     sheet_to(p, sheet, a)
     wrap(p, a)
@@ -316,14 +330,33 @@
         return none
     lax.fori_loop(0, p.step, keep, 0, unroll=p.unroll)
     rr = total_of(p, own_lanes(p), lambda i: a[i] * a[i])
+    to_sheet(p, a, sheet)
+    unflip(p, sheet, rows_right, p.nlon)
+    moves = [
+        pltpu.make_async_copy(src, dst, sem.at[k])
+        for k, (src, dst) in enumerate(zip((rows_right, right, east, lower), stores))
+    ]
+    for move in moves:
+        move.start()
     ten(p, a, b, east, north, south, diag)
     to_sheet(p, a, sheet)
     sheet[:, p.nlon :, :] = jnp.full((p.tiles, p.wide - p.nlon, LANES), rr)
     unflip(p, sheet, out, p.wide)
-
-
-def second_kernel(p, got, right, east, north, south, diag, scal, out, resid, ahead, sheet, a, b):
+    for move in moves:
+        move.wait()
+
+
+def second_kernel(p, got, scal, *refs):
+    loads, out, store, ahead, sheet, a, b, north, south, diag, right, east, lower, rows_resid, sem = (
+        refs[:3], *refs[3:]
+    )
     row, lane = lane_row(p)
+    moves = [
+        pltpu.make_async_copy(src, dst, sem.at[k])
+        for k, (src, dst) in enumerate(zip(loads, (east, lower, right)))
+    ]
+    for move in moves:
+        move.start()
     flip(p, lambda c, m, cols: got[c, m, :, cols], sheet)
     if p.groups == 1:
         q = 0.0
@@ -338,14 +371,17 @@
     ahead[...] = alpha
     sheet_to(p, sheet, a)
     wrap(p, a)
+    moves[0].wait()
+    moves[1].wait()
+    spread(p, *ends(p), lower, east, north, south, diag)
     ten(p, a, b, east, north, south, diag)
+    moves[2].wait()
     alpha = jnp.broadcast_to(alpha[:, :1], (SUB, p.lanes))
 
     def cut(i, sums):
         r0 = right[i + 1]
         r = r0 - alpha * (r0 + a[i + 1])
         a[i + 1] = r
-        resid[i + 1] = r
         return sums[0] + r * r, sums[1] + r * r0
     zero = jnp.zeros((SUB, p.lanes), jnp.float32)
     rr1, rb = lax.fori_loop(0, p.step, cut, (zero, zero), unroll=p.unroll)
@@ -353,69 +389,66 @@
     own = own_lanes(p)
     rr1 = jnp.sum(jnp.where(own, rr1, 0.0))
     rb = jnp.sum(jnp.where(own, rb, 0.0))
+    to_sheet(p, a, sheet)
+    unflip(p, sheet, rows_resid, p.nlon)
+    leave = pltpu.make_async_copy(rows_resid, store, sem.at[3])
+    leave.start()
     ten(p, a, b, east, north, south, diag)
     to_sheet(p, a, sheet)
     sheet[:, p.nlon :, :] = jnp.zeros((p.tiles, p.wide - p.nlon, LANES), jnp.float32)
     sheet[:, p.nlon : p.nlon + SUB, :] = jnp.full((p.tiles, SUB, LANES), rr1)
     sheet[:, p.nlon + SUB : p.nlon + 2 * SUB, :] = jnp.full((p.tiles, SUB, LANES), rb)
     unflip(p, sheet, out, p.wide)
-
-
-def back_kernel(p, field, out, sheet):
-    to_sheet(p, field, sheet)
-    sheet[:, p.nlon :, :] = jnp.zeros((p.tiles, p.wide - p.nlon, LANES), jnp.float32)
-    unflip(p, sheet, out, p.nlon)
-
-
-def buffers(p):
-    buf = (p.step + 2, SUB, p.lanes)
-    return [pltpu.VMEM((p.tiles, p.wide, LANES), jnp.float32)] + [pltpu.VMEM(buf, jnp.float32)] * 2
+    leave.wait()
 
 
 def vmem(n):
     return [pl.BlockSpec(memory_space=pltpu.VMEM)] * n
 
 
+def hbm(n):
+    return [pl.BlockSpec(memory_space=pltpu.HBM)] * n
+
+
+def half_shapes(p):
+    buf = (p.step + 2, SUB, p.lanes)
+    rows = (p.group, p.share, p.rows, p.nlon)
+    back = (p.group, p.share, p.rows, p.wide)
+    scratch = [pltpu.VMEM((p.tiles, p.wide, LANES), jnp.float32)]
+    scratch += [pltpu.VMEM(buf, jnp.float32)] * 8
+    scratch += [pltpu.VMEM(rows, jnp.float32)]
+    return *(jax.ShapeDtypeStruct(x, jnp.float32) for x in (buf, rows, back)), scratch
+
+
 def first_half(p, got, near, far):
-    buf = jax.ShapeDtypeStruct((p.step + 2, SUB, p.lanes), jnp.float32)
-    back = jax.ShapeDtypeStruct((p.group, p.share, p.rows, p.wide), jnp.float32)
+    buf, rows, back, scratch = half_shapes(p)
     coef = pltpu.VMEM((p.parts, p.window, 2, p.rows, p.piece), jnp.float32)
     return pl.pallas_call(
         functools.partial(first_kernel, p),
         in_specs=vmem(3),
-        out_specs=vmem(6),
-        out_shape=[back] + [buf] * 5,
-        scratch_shapes=buffers(p) + [coef],
+        out_specs=vmem(1) + hbm(4),
+        out_shape=[back] + [pltpu.HBM(x.shape, x.dtype) for x in (rows, buf, buf, buf)],
+        scratch_shapes=scratch + [coef, pltpu.SemaphoreType.DMA((4,))],
         compiler_params=ROOM,
         name="smooth_first",
     )(got, near, far)
 
 
-def second_half(p, got, right, east, north, south, diag, scal):
-    buf = jax.ShapeDtypeStruct((p.step + 2, SUB, p.lanes), jnp.float32)
-    back = jax.ShapeDtypeStruct((p.group, p.share, p.rows, p.wide), jnp.float32)
+def second_half(p, got, scal, right, east, lower):
+    buf, rows, back, scratch = half_shapes(p)
     return pl.pallas_call(
         functools.partial(second_kernel, p),
-        in_specs=vmem(7),
-        out_specs=vmem(3),
-        out_shape=[back, buf, jax.ShapeDtypeStruct((SUB, LANES), jnp.float32)],
-        scratch_shapes=buffers(p),
+        in_specs=vmem(2) + hbm(3),
+        out_specs=vmem(1) + hbm(1) + vmem(1),
+        out_shape=[
+            back,
+            pltpu.HBM(rows.shape, rows.dtype),
+            jax.ShapeDtypeStruct((SUB, LANES), jnp.float32),
+        ],
+        scratch_shapes=scratch + [pltpu.SemaphoreType.DMA((4,))],
         compiler_params=ROOM,
         name="smooth_second",
-    )(got, right, east, north, south, diag, scal)
-
-
-def to_rows(p, field):
-    return pl.pallas_call(
-        functools.partial(back_kernel, p),
-        in_specs=vmem(1),
-        out_specs=vmem(1)[0],
-        out_shape=jax.ShapeDtypeStruct((p.group, p.share, p.rows, p.nlon), jnp.float32),
-        scratch_shapes=buffers(p)[:1],
-        cost_estimate=pl.CostEstimate(flops=0, bytes_accessed=2**22, transcendentals=0),
-        compiler_params=ROOM,
-        name="to_rows",
-    )(field)
+    )(got, scal, *(pltpu.with_memory_space_constraint(x, pltpu.HBM) for x in (east, lower, right)))
 
 
 def scalars(p, mine, scal):
@@ -521,8 +554,11 @@
     both = jnp.pad(jnp.stack([lon_coef, lat_coef]), ((0, 0), (0, 0), (0, p.wide - p.nlon)))
     part = lax.axis_index("mem") % p.parts
     both = lax.dynamic_slice_in_dim(both, part * p.piece, p.piece, axis=2)
-    both = jnp.broadcast_to(both[None], (p.group, 2, p.rows, p.piece))
-    near = widen(p, turn(p, both))[None]
+    return turn(p, jnp.broadcast_to(both[None], (p.group, 2, p.rows, p.piece)))
+
+
+def share_out(p, pieces):
+    near = widen(p, pieces)[None]
     if p.parts == 1:
         return near, near
     if p.parts == 4:
@@ -537,21 +573,28 @@
     weight = flat(obs_weight)
     by_member = perturb.reshape(p.members, p.fields, p.rows, p.nlon)
 
-    near, far = coefficients(p, lon_coef, lat_coef)
-    (sent,) = adjoint(p, by_member, weight, flat(innovation), second=False)
-    back, right, *coefs = first_half(p, widen(p, turn(p, sent)), near, far)
-    field, rows_right = lax.optimization_barrier((turn(p, back), to_rows(p, right)))
-    rows_right = by_rank(turn(p, rows_right))
-    mine = member_sum(p, *forward(p, perturb, by_rank(field)))
+    pieces, value = lax.optimization_barrier((coefficients(p, lon_coef, lat_coef), flat(innovation)))
+    (sent,) = adjoint(p, by_member, weight, value, second=False)
+    near, far = share_out(p, pieces)
+    back, rows_right, *kept = first_half(p, widen(p, turn(p, sent)), near, far)
+    field, rows_right = lax.optimization_barrier((turn(p, back), rows_right))
+    with jax.named_scope("return_first"):
+        rows_right = by_rank(turn(p, rows_right))
+    with jax.named_scope("map_first"):
+        keep, send = forward(p, perturb, by_rank(field))
+    mine = member_sum(p, keep, send)
     other = swap(p, mine, "mem", 1, p.mem)
     sent, total, scal = adjoint(p, by_member, weight, mine, other, second=True)
     sent, rows_right = lax.optimization_barrier((sent, rows_right))
     if p.groups > 1:
         scal = jnp.concatenate([scal[:1], lax.psum(scal[1:], "lat")], axis=0)
-    back, resid, ahead = second_half(p, widen(p, turn(p, sent)), right, *coefs, scal)
-    field, rows_resid = lax.optimization_barrier((turn(p, back), to_rows(p, resid)))
-    rows_resid = by_rank(turn(p, rows_resid))
-    mine = member_sum(p, *forward(p, perturb, by_rank(field)))
+    back, rows_resid, ahead = second_half(p, widen(p, turn(p, sent)), scal, *kept)
+    field, rows_resid = lax.optimization_barrier((turn(p, back), rows_resid))
+    with jax.named_scope("return_second"):
+        rows_resid = by_rank(turn(p, rows_resid))
+    with jax.named_scope("map_second"):
+        keep, send = forward(p, perturb, by_rank(field))
+    mine = member_sum(p, keep, send)
     mine, rows_resid = lax.optimization_barrier((mine, rows_resid))
     other = swap(p, mine, "mem", 1, p.mem)
     q = test(p, weight, total, mine, scal)

time: 220 us -> 210 us (0.955)
  blocking collectives: 37.5 us -> 99.8 us
  waiting for transfers between devices: 82 us -> 44.6 us
  starting transfers between devices: 32.5 us -> 15.7 us
  local copies, waits for them, and re-layouts: 23.8 us -> 12.3 us
  Pallas kernels: 41.8 us -> 35 us
    all_to_all x1 -> x4, blocking collectives: 26.2 us -> 88.2 us  [turn(): return lax.all_to_all(x, 'lat', 0, 0)]
    all_to_all x6 -> x3, waiting for transfers between devices: 46.4 us -> 9.03 us  [turn(): return lax.all_to_all(x, 'lat', 0, 0)]
    all_to_all x6 -> x3, starting transfers between devices: 27.6 us -> 10.8 us  [turn(): return lax.all_to_all(x, 'lat', 0, 0)]
    unnamed x38 -> x16, local copies, waits for them, and re-layouts: 23.1 us -> 12.3 us
    pallas_call x1, Pallas kernels: 14.9 us -> 11.5 us  [first_half(): pl.pallas_call(functools.partial(first_kernel, p), in_specs=vmem(3), out_...]
    pallas_call x3 -> x1, Pallas kernels: 15 us -> 11.7 us  [second_half(): pl.pallas_call(functools.partial(second_kernel, p), in_specs=vmem(2) + hb...]
  transfers between devices with their start and end apart: 14 -> 11, of which waited for: 11 -> 9; matrix products, arithmetic and copies ran while one was open for 0% -> 0% of each run, Pallas kernels for 5% -> 3%
where the time goes in v3:
time: 210 us; the launch traced here: 209 us
  blocking collectives  99.8 us (48%)
  waiting for transfers between devices  44.6 us (21%)
  Pallas kernels  35 us (17%)
  starting transfers between devices  15.7 us (7%)
  local copies, waits for them, and re-layouts  12.3 us (6%)
    all_to_all x4, blocking collectives, turn(): return lax.all_to_all(x, 'lat', 0, 0)  88.2 us
    ppermute x8, waiting for transfers between devices, swap(): return lax.ppermute(x, axis, [(i, i ^ bit) for i in range(count)])  35.6 us
    unnamed x16, local copies, waits for them, and re-layouts  12.3 us
    pallas_call x1, Pallas kernels, second_half(): pl.pallas_call(functools.partial(second_kernel, p), in_specs=vmem(2) + hb...  11.7 us
    all_to_all x1, blocking collectives, per_device(): lax.all_to_all(q, ('mem', 'lat'), 0, 0)  11.6 us
    pallas_call x1, Pallas kernels, first_half(): pl.pallas_call(functools.partial(first_kernel, p), in_specs=vmem(3), out_...  11.5 us
    all_to_all x3, starting transfers between devices, turn(): return lax.all_to_all(x, 'lat', 0, 0)  10.8 us
    all_to_all x3, waiting for transfers between devices, turn(): return lax.all_to_all(x, 'lat', 0, 0)  9.03 us
  transfers between devices with their start and end apart: 11, of which 9 were waited for; matrix products, arithmetic and copies ran while one was open for 0% of the time, Pallas kernels for 3%

profile of v3, /device:TPU:0, one launch (start us, length us, event | category | flops | bytes accessed | tf_op | source)
XLA Modules:
  0.0 209.2 jit_solution(2789435022505928489)
XLA Ops:
  0.6 0.7 fusion.1
  1.4 15.1 %all_to_all.40 = f32[8,2,8,384]{3,2,1,0:T(8,128)S(1)} all-to-all(f32[8,2,8,384]{3,2,1,0:T(8,128)S(1)} %broadcast_in_dim.4), channel_id=1, replica_groups=mesh['mem'=4,'lat'=8] {'lat'}, dimensions={0} | all-to-all | bytes 393216 | tf_op jit(solution)/shard_map/all_to_all | solution.py:525
  16.5 2.7 %copy-done = bf16[16,3,5,8,1440]{4,3,2,1,0:T(8,128)(2,1)S(1)} copy-done((bf16[16,3,5,8,1440]{4,3,2,1,0:T(8,128)(2,1)S(1)}, bf16[16,3,5,8,1440]{4,3,2,1,0:T(8,128)(2,1)}, u32[]{:S(2)}) %copy-start) | copy-done | bytes 5529624
  19.1 1.1 copy-done.3
  20.3 1.1 copy-done.7
  21.4 3.4 %adjoint_first.1 = f32[8,2,8,1536]{3,2,1,0:T(8,128)} custom-call(bf16[16,15,8,1440]{3,2,1,0:T(8,128)(2,1)S(1)} %bitcast.11, f32[15,8,1440]{2,1,0:T(8,128)S(1)} %bitcast.13, f32[15,8,1440]{2,1,0:T(8,128)S(1)} %bitcast.20), custom_call_target="tpu_custom_call" | custom-call | flops 5529600 | bytes 5529600 | tf_op jit(solution)/shard_map/adjoint_first/pallas_call | solution.py:101
  24.8 3.5 %all-to-all-start.1 = ((f32[8,2,8,1536]{3,2,1,0:T(8,128)}), f32[8,2,8,1536]{3,2,1,0:T(8,128)S(1)}, u32[]{:S(2)}, u32[]{:S(2)}) async-start(f32[8,2,8,1536]{3,2,1,0:T(8,128)} %adjoint_first.1), calls=%async_computation.1 | async-start | bytes 1572864 | tf_op jit(solution)/shard_map/all_to_all | solution.py:525
  28.3 0.1 collective-permute-start
  28.4 1.4 collective-permute-done
  29.9 1.6 collective-permute-start.1
  31.4 9.7 %collective-permute-done.1.far = f32[2,8,2,8,384]{4,3,2,1,0:T(8,128)S(1)} collective-permute-done((f32[2,8,2,8,384]{4,3,2,1,0:T(8,128)S(1)}, f32[2,8,2,8,384]{4,3,2,1,0:T(8,128)S(1)}, u32[]{:S(2)}, u32[]{:S(2)}) %collective-permute-start.1) | collective-permute-done | bytes 393248 | tf_op jit(solution)/shard_map/ppermute | solution.py:520
  41.1 6.8 %all-to-all-done.1.got = f32[8,2,8,1536]{3,2,1,0:T(8,128)S(1)} async-done(((f32[8,2,8,1536]{3,2,1,0:T(8,128)}), f32[8,2,8,1536]{3,2,1,0:T(8,128)S(1)}, u32[]{:S(2)}, u32[]{:S(2)}) %all-to-all-start.1) | async-done | bytes 786464 | tf_op jit(solution)/shard_map/all_to_all | solution.py:525
  47.9 11.5 %smooth_first.1 = (f32[8,2,8,1536]{3,2,1,0:T(8,128)S(1)}, f32[8,2,8,1440]{3,2,1,0:T(8,128)}, f32[182,8,128]{2,1,0:T(8,128)}, f32[182,8,128]{2,1,0:T(8,128)}, f32[182,8,128]{2,1,0:T(8,128)}) custom-call(f32[8,2,8,1536]{3,2,1,0:T(8,128)S(1)} %all-to-all-done.1.got, f32[2,8,2,8,384]{4,3,2,1,0:T(8,128)S(1)} %pad_maximum_fusion.near, ...), custom_call_target="tpu_custom_call" | custom-call | tf_op jit(solution)/shard_map/smooth_first/pallas_call | solution.py:426
  59.4 0.0 copy-start.4
  59.4 23.7 %all_to_all.41 = f32[8,2,8,1536]{3,2,1,0:T(8,128)S(1)} all-to-all(f32[8,2,8,1536]{3,2,1,0:T(8,128)S(1)} %get-tuple-element.31), channel_id=1, replica_groups=mesh['mem'=4,'lat'=8] {'lat'}, dimensions={0} | all-to-all | bytes 1572864 | tf_op jit(solution)/shard_map/all_to_all | solution.py:525
  83.1 3.6 %all-to-all-start.3 = ((f32[8,2,8,1440]{3,2,1,0:T(8,128)}), f32[8,2,8,1440]{3,2,1,0:T(8,128)S(1)}, u32[]{:S(2)}, u32[]{:S(2)}) async-start(f32[8,2,8,1440]{3,2,1,0:T(8,128)} %get-tuple-element.38), calls=%async_computation.3 | async-start | bytes 1572864 | tf_op jit(solution)/shard_map/return_first/all_to_all | solution.py:525
  86.8 2.7 %copy-done.1 = bf16[16,3,5,8,1440]{4,3,2,1,0:T(8,128)(2,1)S(1)} copy-done((bf16[16,3,5,8,1440]{4,3,2,1,0:T(8,128)(2,1)S(1)}, bf16[16,3,5,8,1440]{4,3,2,1,0:T(8,128)(2,1)}, u32[]{:S(2)}) %copy-start.1) | copy-done | bytes 5529624
  89.4 1.7 forward.2
  91.1 0.1 collective-permute-start.2
  91.2 1.7 collective-permute-done.2
  92.9 0.1 add.23
  93.0 1.6 collective-permute-start.3
  94.5 9.7 %collective-permute-done.3 = f32[8,8,1536]{2,1,0:T(8,128)S(1)} collective-permute-done((f32[8,8,1536]{2,1,0:T(8,128)S(1)}, f32[8,8,1536]{2,1,0:T(8,128)S(1)}, u32[]{:S(2)}, u32[]{:S(2)}) %collective-permute-start.3) | collective-permute-done | bytes 393248 | tf_op jit(solution)/shard_map/ppermute | solution.py:520
  104.3 0.1 collective-permute-start.4
  104.3 1.7 collective-permute-done.4.refs_3_
  106.0 0.0 copy-done.4
  106.0 1.5 adjoint_second.1
  107.6 0.0 copy-start.5
  107.6 0.9 copy-done.5
  108.5 0.0 all-to-all-done.3
  108.5 26.2 %all_to_all.42.got = f32[8,2,8,1536]{3,2,1,0:T(8,128)S(1)} all-to-all(f32[8,2,8,1536]{3,2,1,0:T(8,128)S(1)} %get-tuple-element.39), channel_id=1, replica_groups=mesh['mem'=4,'lat'=8] {'lat'}, dimensions={0} | all-to-all | bytes 1572864 | tf_op jit(solution)/shard_map/all_to_all | solution.py:525
  134.7 11.7 %smooth_second.1 = (f32[8,2,8,1536]{3,2,1,0:T(8,128)S(1)}, f32[8,2,8,1440]{3,2,1,0:T(8,128)}, f32[8,128]{1,0:T(8,128)S(1)}) custom-call(f32[8,2,8,1536]{3,2,1,0:T(8,128)S(1)} %all_to_all.42.got, f32[2,8,128]{2,1,0:T(8,128)S(1)} %get-tuple-element.40.scal, f32[182,8,128]{2,1,0:T(8,128)} %get-tuple-element.41.refs_0_, ...), custom_call_target="tpu_custom_call" | custom-call | tf_op jit(solution)/shard_map/smooth_second/pallas_call | solution.py:439
  146.3 23.2 %all_to_all.43 = f32[8,2,8,1536]{3,2,1,0:T(8,128)S(1)} all-to-all(f32[8,2,8,1536]{3,2,1,0:T(8,128)S(1)} %get-tuple-element.44), channel_id=1, replica_groups=mesh['mem'=4,'lat'=8] {'lat'}, dimensions={0} | all-to-all | bytes 1572864 | tf_op jit(solution)/shard_map/all_to_all | solution.py:525
  169.6 3.6 %all-to-all-start.6 = ((f32[8,2,8,1440]{3,2,1,0:T(8,128)}), f32[8,2,8,1440]{3,2,1,0:T(8,128)S(1)}, u32[]{:S(2)}, u32[]{:S(2)}) async-start(f32[8,2,8,1440]{3,2,1,0:T(8,128)} %get-tuple-element.49), calls=%async_computation.6 | async-start | bytes 1572864 | tf_op jit(solution)/shard_map/return_second/all_to_all | solution.py:525
  173.2 2.7 %copy-done.2 = bf16[16,3,5,8,1440]{4,3,2,1,0:T(8,128)(2,1)S(1)} copy-done((bf16[16,3,5,8,1440]{4,3,2,1,0:T(8,128)(2,1)S(1)}, bf16[16,3,5,8,1440]{4,3,2,1,0:T(8,128)(2,1)}, u32[]{:S(2)}) %copy-start.2) | copy-done | bytes 5529624
  175.8 1.8 forward.3
  177.7 0.1 collective-permute-start.5
  177.7 1.7 collective-permute-done.5
  179.5 0.1 add.25
  179.5 1.6 collective-permute-start.6
  181.1 9.7 %collective-permute-done.6 = f32[8,8,1536]{2,1,0:T(8,128)S(1)} collective-permute-done((f32[8,8,1536]{2,1,0:T(8,128)S(1)}, f32[8,8,1536]{2,1,0:T(8,128)S(1)}, u32[]{:S(2)}, u32[]{:S(2)}) %collective-permute-start.6) | collective-permute-done | bytes 393248 | tf_op jit(solution)/shard_map/ppermute | solution.py:520
  190.8 2.2 %all-to-all-done.6 = f32[8,2,8,1440]{3,2,1,0:T(8,128)S(1)} async-done(((f32[8,2,8,1440]{3,2,1,0:T(8,128)}), f32[8,2,8,1440]{3,2,1,0:T(8,128)S(1)}, u32[]{:S(2)}, u32[]{:S(2)}) %all-to-all-start.6) | async-done | bytes 737312 | tf_op jit(solution)/shard_map/return_second/all_to_all | solution.py:525
  193.0 0.0 collective-permute-start.7
  193.0 1.1 copy-done.6
  194.1 0.4 last_sums.1
  194.5 11.6 %all_to_all.44.q = f32[32,8,128]{2,1,0:T(8,128)S(1)} all-to-all(f32[32,8,128]{2,1,0:T(8,128)S(1)} %last_sums.1), channel_id=1, replica_groups=mesh['mem'=4,'lat'=8] {'mem','lat'}, dimensions={0} | all-to-all | bytes 262144 | tf_op jit(solution)/shard_map/all_to_all | solution.py:601
  206.1 0.0 collective-permute-done.7.other
  206.1 3.0 %last_update.1 = (f32[15,8,1440]{2,1,0:T(8,128)}, f32[16,8,1440]{2,1,0:T(8,128)}) custom-call(f32[16,8,1440]{2,1,0:T(8,128)S(1)} %copy-done.6, f32[8,8,1536]{2,1,0:T(8,128)S(1)} %add.26.mine, f32[8,8,1536]{2,1,0:T(8,128)S(1)} %collective-permute-done.7.other, f32[2,8,128]{2,1,0:T(8,128)S(1)} %get-tuple-element.40.scal, ...), custom_call_target="tpu_custom_call" | custom-call | tf_op jit(solution)/shard_map/last_update/pallas_call | solution.py:506
  (10 shorter events, 0.1 us)
Async XLA Ops:
  16.5 2.7 %copy-start = (bf16[16,3,5,8,1440]{4,3,2,1,0:T(8,128)(2,1)S(1)}, bf16[16,3,5,8,1440]{4,3,2,1,0:T(8,128)(2,1)}, u32[]{:S(2)}) copy-start(bf16[16,3,5,8,1440]{4,3,2,1,0:T(8,128)(2,1)} %perturb.3) | copy-start | bytes 16588804
  19.1 1.1 copy-start.3
  20.3 1.1 copy-start.7
  24.8 23.1 %all-to-all-start.1 = ((f32[8,2,8,1536]{3,2,1,0:T(8,128)}), f32[8,2,8,1536]{3,2,1,0:T(8,128)S(1)}, u32[]{:S(2)}, u32[]{:S(2)}) async-start(f32[8,2,8,1536]{3,2,1,0:T(8,128)} %adjoint_first.1), calls=%async_computation.1 | async-start | bytes 1572864 | tf_op jit(solution)/shard_map/all_to_all | solution.py:525
  28.3 1.5 collective-permute-start
  29.9 11.2 %collective-permute-start.1 = (f32[2,8,2,8,384]{4,3,2,1,0:T(8,128)S(1)}, f32[2,8,2,8,384]{4,3,2,1,0:T(8,128)S(1)}, u32[]{:S(2)}, u32[]{:S(2)}) collective-permute-start(f32[2,8,2,8,384]{4,3,2,1,0:T(8,128)S(1)} %pad_maximum_fusion.near), channel_id=1, source_target_pairs={{0,16},{8,24},{16,0},{24,8},{1,17},{9,25},{17,1},{25,9},{2,18},{10... | collective-permute-start | bytes 1179656 | tf_op jit(solution)/shard_map/ppermute | solution.py:520
  59.4 46.6 %copy-start.4 = (f32[3,5,8,1440]{3,2,1,0:T(8,128)S(1)}, f32[3,5,8,1440]{3,2,1,0:T(8,128)}, u32[]{:S(2)}) copy-start(f32[3,5,8,1440]{3,2,1,0:T(8,128)} %param.7) | copy-start | bytes 2073604
  83.1 25.4 %all-to-all-start.3 = ((f32[8,2,8,1440]{3,2,1,0:T(8,128)}), f32[8,2,8,1440]{3,2,1,0:T(8,128)S(1)}, u32[]{:S(2)}, u32[]{:S(2)}) async-start(f32[8,2,8,1440]{3,2,1,0:T(8,128)} %get-tuple-element.38), calls=%async_computation.3 | async-start | bytes 1572864 | tf_op jit(solution)/shard_map/return_first/all_to_all | solution.py:525
  86.8 2.7 %copy-start.1 = (bf16[16,3,5,8,1440]{4,3,2,1,0:T(8,128)(2,1)S(1)}, bf16[16,3,5,8,1440]{4,3,2,1,0:T(8,128)(2,1)}, u32[]{:S(2)}) copy-start(bf16[16,3,5,8,1440]{4,3,2,1,0:T(8,128)(2,1)} %perturb.3) | copy-start | bytes 16588804
  91.1 1.8 collective-permute-start.2
  93.0 11.2 %collective-permute-start.3 = (f32[8,8,1536]{2,1,0:T(8,128)S(1)}, f32[8,8,1536]{2,1,0:T(8,128)S(1)}, u32[]{:S(2)}, u32[]{:S(2)}) collective-permute-start(f32[8,8,1536]{2,1,0:T(8,128)S(1)} %add.23), channel_id=1, source_target_pairs={{0,16},{8,24},{16,0},{24,8},{1,17},{9,25},{17,1},{25,9},{2,18},{10... | collective-permute-start | bytes 1179656 | tf_op jit(solution)/shard_map/ppermute | solution.py:520
  104.3 1.8 collective-permute-start.4
  107.6 0.9 copy-start.5
  169.6 23.4 %all-to-all-start.6 = ((f32[8,2,8,1440]{3,2,1,0:T(8,128)}), f32[8,2,8,1440]{3,2,1,0:T(8,128)S(1)}, u32[]{:S(2)}, u32[]{:S(2)}) async-start(f32[8,2,8,1440]{3,2,1,0:T(8,128)} %get-tuple-element.49), calls=%async_computation.6 | async-start | bytes 1572864 | tf_op jit(solution)/shard_map/return_second/all_to_all | solution.py:525
  173.2 2.7 %copy-start.2 = (bf16[16,3,5,8,1440]{4,3,2,1,0:T(8,128)(2,1)S(1)}, bf16[16,3,5,8,1440]{4,3,2,1,0:T(8,128)(2,1)}, u32[]{:S(2)}) copy-start(bf16[16,3,5,8,1440]{4,3,2,1,0:T(8,128)(2,1)} %perturb.3) | copy-start | bytes 16588804
  177.7 1.8 collective-permute-start.5
  179.5 11.2 %collective-permute-start.6 = (f32[8,8,1536]{2,1,0:T(8,128)S(1)}, f32[8,8,1536]{2,1,0:T(8,128)S(1)}, u32[]{:S(2)}, u32[]{:S(2)}) collective-permute-start(f32[8,8,1536]{2,1,0:T(8,128)S(1)} %add.25), channel_id=1, source_target_pairs={{0,16},{8,24},{16,0},{24,8},{1,17},{9,25},{17,1},{25,9},{2,18},{10... | collective-permute-start | bytes 1179656 | tf_op jit(solution)/shard_map/ppermute | solution.py:520
  193.0 13.1 %collective-permute-start.7 = (f32[8,8,1536]{2,1,0:T(8,128)S(1)}, f32[8,8,1536]{2,1,0:T(8,128)S(1)}, u32[]{:S(2)}, u32[]{:S(2)}) collective-permute-start(f32[8,8,1536]{2,1,0:T(8,128)S(1)} %add.26.mine), channel_id=1, source_target_pairs={{0,8},{8,0},{16,24},{24,16},{1,9},{9,1},{17,25},{25,17},{2,10},{10... | collective-permute-start | bytes 1179656 | tf_op jit(solution)/shard_map/ppermute | solution.py:520
  193.0 1.1 copy-start.6

commit v4 on v3

--- a/solution.py
+++ b/solution.py
@@ -46,73 +46,124 @@
         self.piece = self.wide // self.parts
 
 
-def adjoint_kernel(p, second, *refs):
-    if second:
-        perturb, weight, mine, other, out, total, scal, prod = refs
-    else:
-        perturb, weight, value, out, prod = refs
-    step = pl.program_id(0)
-
-    @pl.when(step == 0)
-    def _():
-        if second:
-            core = lax.axis_index("mem") % 2
-            acc = jnp.zeros((p.rows, p.nlon), jnp.float32)
-            for half, at in ((mine, core * p.half), (other, (1 - core) * p.half)):
-                for k in range(p.half):
-                    t = half[k, :, : p.nlon]
-                    wt = weight[jnp.minimum(at + k, p.fields - 1)] * t
-                    prod[at + k] = wt
-                    total[at + k] = t
-                    acc = acc + wt * t
-            rr = mine[0, :1, p.nlon : p.nlon + 1]
-            scal[0] = jnp.broadcast_to(rr, (p.rows, LANES))
-            scal[1] = jnp.full((p.rows, LANES), jnp.sum(acc))
-        else:
-            for k in range(p.fields):
-                prod[k] = weight[k] * value[k]
-
+def mapped(p, perturb, first, prod):
     acc = [0.0] * p.share
     for k in range(p.fields):
         row = prod[k]
         for m in range(p.share):
-            acc[m] = acc[m] + perturb[m, k].astype(jnp.float32) * row
-    tail = jnp.zeros((p.rows, p.wide - p.nlon), jnp.float32)
-    if second:
-        tail = jnp.broadcast_to(scal[1][:1, :1], tail.shape)
+            acc[m] = acc[m] + perturb[first + m, k].astype(jnp.float32) * row
+    return acc
+
+
+def adjoint_first_kernel(p, perturb, weight, value, out, pbuf, wbuf, vbuf, obuf, prod, sem):
+    def part(k):
+        rows = pl.ds(k * p.share, p.share)
+        return pltpu.make_async_copy(perturb.at[rows], pbuf.at[rows], sem.at[k])
+
+    def leave(k):
+        return pltpu.make_async_copy(obuf.at[k], out.at[k], sem.at[p.group + k])
+
+    heads = [
+        pltpu.make_async_copy(weight, wbuf, sem.at[2 * p.group]),
+        pltpu.make_async_copy(value, vbuf, sem.at[2 * p.group + 1]),
+    ]
+    for head in heads:
+        head.start()
+    for k in range(p.group):
+        part(k).start()
+    for head in heads:
+        head.wait()
+    for k in range(p.fields):
+        prod[k] = wbuf[k] * vbuf[k]
+
+    def one(k, none):
+        part(k).wait()
+        acc = mapped(p, pbuf, k * p.share, prod)
+        for m in range(p.share):
+            obuf[k, m, :, : p.nlon] = acc[m]
+            obuf[k, m, :, p.nlon :] = jnp.zeros((p.rows, p.wide - p.nlon), jnp.float32)
+        leave(k).start()
+        return none
+    lax.fori_loop(0, p.group, one, 0)
+    for k in range(p.group):
+        leave(k).wait()
+
+
+def adjoint_first(p, perturb, weight, value):
+    shape = (p.group, p.share, p.rows, p.wide)
+    field = pltpu.VMEM((p.fields, p.rows, p.nlon), jnp.float32)
+    held = [pltpu.with_memory_space_constraint(x, pltpu.HBM) for x in (perturb, weight, value)]
+    return pl.pallas_call(
+        functools.partial(adjoint_first_kernel, p),
+        in_specs=hbm(3),
+        out_specs=hbm(1)[0],
+        out_shape=pltpu.HBM(shape, jnp.float32),
+        scratch_shapes=[
+            pltpu.VMEM(perturb.shape, perturb.dtype),
+            field,
+            field,
+            pltpu.VMEM(shape, jnp.float32),
+            field,
+            pltpu.SemaphoreType.DMA((2 * p.group + 2,)),
+        ],
+        compiler_params=ROOM,
+        cost_estimate=cost(p, 2),
+        name="adjoint_first",
+    )(*held)
+
+
+def adjoint_kernel(p, perturb, weight, mine, other, out, total, scal, prod):
+    step = pl.program_id(0)
+
+    @pl.when(step == 0)
+    def _():
+        core = lax.axis_index("mem") % 2
+        acc = jnp.zeros((p.rows, p.nlon), jnp.float32)
+        for half, at in ((mine, core * p.half), (other, (1 - core) * p.half)):
+            for k in range(p.half):
+                t = half[k, :, : p.nlon]
+                wt = weight[jnp.minimum(at + k, p.fields - 1)] * t
+                prod[at + k] = wt
+                total[at + k] = t
+                acc = acc + wt * t
+        rr = mine[0, :1, p.nlon : p.nlon + 1]
+        scal[0] = jnp.broadcast_to(rr, (p.rows, LANES))
+        scal[1] = jnp.full((p.rows, LANES), jnp.sum(acc))
+
+    acc = mapped(p, perturb, 0, prod)
+    tail = jnp.broadcast_to(scal[1][:1, :1], (p.rows, p.wide - p.nlon))
     for m in range(p.share):
         out[0, m, :, : p.nlon] = acc[m]
         out[0, m, :, p.nlon :] = tail
 
 
-def adjoint(p, perturb, weight, *rest, second):
+def adjoint(p, perturb, weight, mine, other):
     whole = lambda *shape: pl.BlockSpec(shape, lambda i: (0,) * len(shape))
     rows, nlon = p.rows, p.nlon
-    field = whole(p.fields, rows, nlon)
-    more = [whole(p.half, rows, p.wide)] * 2 if second else [field]
-    out_shape = [jax.ShapeDtypeStruct((p.group, p.share, rows, p.wide), jnp.float32)]
-    out_specs = [pl.BlockSpec((1, p.share, rows, p.wide), lambda i: (i, 0, 0, 0))]
-    if second:
-        out_shape += [
-            jax.ShapeDtypeStruct((2 * p.half, rows, nlon), jnp.float32),
-            jax.ShapeDtypeStruct((2, rows, LANES), jnp.float32),
-        ]
-        out_specs += [whole(2 * p.half, rows, nlon), whole(2, rows, LANES)]
     return pl.pallas_call(
-        functools.partial(adjoint_kernel, p, second),
+        functools.partial(adjoint_kernel, p),
         grid=(p.group,),
         in_specs=[
             pl.BlockSpec((p.share, p.fields, rows, nlon), lambda i: (i, 0, 0, 0)),
-            field,
-            *more,
+            whole(p.fields, rows, nlon),
+            whole(p.half, rows, p.wide),
+            whole(p.half, rows, p.wide),
         ],
-        out_specs=out_specs,
-        out_shape=out_shape,
+        out_specs=[
+            pl.BlockSpec((1, p.share, rows, p.wide), lambda i: (i, 0, 0, 0)),
+            whole(2 * p.half, rows, nlon),
+            whole(2, rows, LANES),
+        ],
+        out_shape=[
+            jax.ShapeDtypeStruct((p.group, p.share, rows, p.wide), jnp.float32),
+            jax.ShapeDtypeStruct((2 * p.half, rows, nlon), jnp.float32),
+            jax.ShapeDtypeStruct((2, rows, LANES), jnp.float32),
+        ],
         scratch_shapes=[pltpu.VMEM((2 * p.half, rows, nlon), jnp.float32)],
+        compiler_params=ROOM,
         cost_estimate=cost(p, 2),
-        compiler_params=ROOM,
-        name="adjoint_second" if second else "adjoint_first",
-    )(perturb, weight, *rest)
+        name="adjoint_second",
+    )(perturb, weight, mine, other)
 
 
 def cost(p, size):
@@ -120,60 +171,68 @@
     return pl.CostEstimate(flops=2 * cells, bytes_accessed=size * cells, transcendentals=0)
 
 
-def forward_kernel(p, perturb, field, keep, send, scr):
-    step = pl.program_id(0)
-
-    @pl.when(step == 0)
-    def _():
-        for k in range(2 * p.half):
-            scr[k, :, p.nlon :] = jnp.zeros((p.rows, p.wide - p.nlon), jnp.float32)
-        for k in range(p.fields, 2 * p.half):
-            scr[k, :, : p.nlon] = jnp.zeros((p.rows, p.nlon), jnp.float32)
+def forward_kernel(p, perturb, field, keep, send, held, scr, sem):
+    cut = -(-p.vars // 2)
+    parts = [(t, 0, p.vars) for t in range(p.slots - 1)]
+    parts += [(p.slots - 1, 0, cut), (p.slots - 1, cut, p.vars)]
+    moves = []
+    for n, (t, low, high) in enumerate(parts):
+        at = (slice(None), t, pl.ds(low, high - low))
+        moves.append(pltpu.make_async_copy(perturb.at[at], held.at[at], sem.at[n]))
+        moves[-1].start()
+
+    one = jnp.zeros((1, 1), jnp.float32)
+    two = jnp.zeros((1, 1), jnp.float32)
+    for k in range(p.group):
+        one = one + field[k * p.share, :1, p.nlon : p.nlon + 1]
+        two = two + field[k * p.share, :1, p.nlon + SUB : p.nlon + SUB + 1]
+    for k in range(2 * p.half):
+        scr[k, :, p.nlon :] = jnp.zeros((p.rows, p.wide - p.nlon), jnp.float32)
+    for k in (0, p.half):
+        scr[k, :, p.nlon : p.nlon + SUB] = jnp.broadcast_to(one, (p.rows, SUB))
+        scr[k, :, p.nlon + SUB : p.nlon + 2 * SUB] = jnp.broadcast_to(two, (p.rows, SUB))
+    for k in range(p.fields, 2 * p.half):
+        scr[k, :, : p.nlon] = jnp.zeros((p.rows, p.nlon), jnp.float32)
 
     split = p.nlon // (2 * LANES) * LANES
-    for cols in (slice(0, split), slice(split, p.nlon)):
-        acc = [0.0] * p.vars
-        for m in range(p.members):
-            f = field[m, :, cols]
-            for v in range(p.vars):
-                acc[v] = acc[v] + perturb[m, 0, v, :, cols].astype(jnp.float32) * f
-        for v in range(p.vars):
-            scr[step * p.vars + v, :, cols] = acc[v]
-
-    @pl.when(step == p.slots - 1)
-    def _():
-        core = lax.axis_index("mem") % 2
-        one = jnp.zeros((1, 1), jnp.float32)
-        two = jnp.zeros((1, 1), jnp.float32)
-        for k in range(p.group):
-            one = one + field[k * p.share, :1, p.nlon : p.nlon + 1]
-            two = two + field[k * p.share, :1, p.nlon + SUB : p.nlon + SUB + 1]
-        for k in (0, p.half):
-            scr[k, :, p.nlon : p.nlon + SUB] = jnp.broadcast_to(one, (p.rows, SUB))
-            scr[k, :, p.nlon + SUB : p.nlon + 2 * SUB] = jnp.broadcast_to(two, (p.rows, SUB))
-        for k in range(p.half):
-            keep[k] = scr[core * p.half + k]
-            send[k] = scr[(1 - core) * p.half + k]
-
-
-def forward(p, perturb, field):
-    rows, nlon = p.rows, p.nlon
-    shape = (p.half, rows, p.wide)
-    spec = pl.BlockSpec(shape, lambda i: (0, 0, 0))
+    for move, (t, low, high) in zip(moves, parts):
+        move.wait()
+        for cols in (slice(0, split), slice(split, p.nlon)):
+            acc = [0.0] * (high - low)
+            for m in range(p.members):
+                f = field[m, :, cols]
+                for v in range(low, high):
+                    acc[v - low] += held[m, t, v, :, cols].astype(jnp.float32) * f
+            for v in range(low, high):
+                scr[t * p.vars + v, :, cols] = acc[v - low]
+
+    core = lax.axis_index("mem") % 2
+    for k in range(p.half):
+        keep[k] = scr[core * p.half + k]
+        send[k] = scr[(1 - core) * p.half + k]
+
+
+def forward(p, perturb, field, hold):
+    shape = (p.half, p.rows, p.wide)
+    scratch = [
+        pltpu.VMEM((2 * p.half, p.rows, p.wide), jnp.float32),
+        pltpu.SemaphoreType.DMA((p.slots + 1,)),
+    ]
+    outs = [jax.ShapeDtypeStruct(shape, jnp.float32)] * 2
+    if hold:
+        outs = outs + [jax.ShapeDtypeStruct(perturb.shape, perturb.dtype)]
+    else:
+        scratch = [pltpu.VMEM(perturb.shape, perturb.dtype)] + scratch
     return pl.pallas_call(
         functools.partial(forward_kernel, p),
-        grid=(p.slots,),
-        in_specs=[
-            pl.BlockSpec((p.members, 1, p.vars, rows, nlon), lambda i: (0, i, 0, 0, 0)),
-            pl.BlockSpec((p.members, rows, p.wide), lambda i: (0, 0, 0)),
-        ],
-        out_specs=[spec, spec],
-        out_shape=[jax.ShapeDtypeStruct(shape, jnp.float32)] * 2,
-        scratch_shapes=[pltpu.VMEM((2 * p.half, rows, p.wide), jnp.float32)],
+        in_specs=hbm(1) + vmem(1),
+        out_specs=vmem(len(outs)),
+        out_shape=outs,
+        scratch_shapes=scratch,
+        compiler_params=ROOM,
         cost_estimate=cost(p, 2),
-        compiler_params=ROOM,
         name="forward",
-    )(perturb, field)
+    )(pltpu.with_memory_space_constraint(perturb, pltpu.HBM), field)
 
 
 def roll(x, shift, axis):
@@ -573,18 +632,18 @@
     weight = flat(obs_weight)
     by_member = perturb.reshape(p.members, p.fields, p.rows, p.nlon)
 
-    pieces, value = lax.optimization_barrier((coefficients(p, lon_coef, lat_coef), flat(innovation)))
-    (sent,) = adjoint(p, by_member, weight, value, second=False)
+    pieces = coefficients(p, lon_coef, lat_coef)
+    sent = adjoint_first(p, by_member, weight, flat(innovation))
     near, far = share_out(p, pieces)
     back, rows_right, *kept = first_half(p, widen(p, turn(p, sent)), near, far)
     field, rows_right = lax.optimization_barrier((turn(p, back), rows_right))
     with jax.named_scope("return_first"):
         rows_right = by_rank(turn(p, rows_right))
     with jax.named_scope("map_first"):
-        keep, send = forward(p, perturb, by_rank(field))
+        keep, send, held = forward(p, perturb, by_rank(field), True)
     mine = member_sum(p, keep, send)
     other = swap(p, mine, "mem", 1, p.mem)
-    sent, total, scal = adjoint(p, by_member, weight, mine, other, second=True)
+    sent, total, scal = adjoint(p, held.reshape(by_member.shape), weight, mine, other)
     sent, rows_right = lax.optimization_barrier((sent, rows_right))
     if p.groups > 1:
         scal = jnp.concatenate([scal[:1], lax.psum(scal[1:], "lat")], axis=0)
@@ -593,7 +652,7 @@
     with jax.named_scope("return_second"):
         rows_resid = by_rank(turn(p, rows_resid))
     with jax.named_scope("map_second"):
-        keep, send = forward(p, perturb, by_rank(field))
+        keep, send = forward(p, perturb, by_rank(field), False)
     mine = member_sum(p, keep, send)
     mine, rows_resid = lax.optimization_barrier((mine, rows_resid))
     other = swap(p, mine, "mem", 1, p.mem)

time: 210 us -> 201 us (0.957)
  blocking collectives: 99.8 us -> 84.4 us
  local copies, waits for them, and re-layouts: 12.3 us -> 2.7 us
  starting transfers between devices: 15.7 us -> 23 us
  waiting for transfers between devices: 44.6 us -> 49.7 us
  Pallas kernels: 35 us -> 38.3 us
    all_to_all x4 -> x3, blocking collectives: 88.2 us -> 73.1 us  [turn(): return lax.all_to_all(x, 'lat', 0, 0)]
    unnamed x16 -> x6, local copies, waits for them, and re-layouts: 12.3 us -> 2.01 us
    all_to_all x3 -> x4, starting transfers between devices: 10.8 us -> 18.1 us  [turn(): return lax.all_to_all(x, 'lat', 0, 0)]
    all_to_all x3 -> x4, waiting for transfers between devices: 9.03 us -> 14.2 us  [turn(): return lax.all_to_all(x, 'lat', 0, 0)]
    pallas_call x4, Pallas kernels: 8.46 us -> 11.8 us  [the longest x2 6.12 us: forward(): pl.pallas_call(functools.partial(forward_kernel, p), in_specs=hbm(1) + vm...]
  transfers between devices with their start and end apart: 11 -> 12, of which waited for: 9 -> 10; matrix products, arithmetic and copies ran while one was open for 0% -> 0% of each run, Pallas kernels for 3% -> 6%
where the time goes in v4:
time: 201 us; the launch traced here: 200 us
  blocking collectives  84.4 us (42%)
  waiting for transfers between devices  49.7 us (25%)
  Pallas kernels  38.3 us (19%)
  starting transfers between devices  23 us (11%)
  local copies, waits for them, and re-layouts  2.7 us (1%)
    all_to_all x3, blocking collectives, turn(): return lax.all_to_all(x, 'lat', 0, 0)  73.1 us
    ppermute x8, waiting for transfers between devices, swap(): return lax.ppermute(x, axis, [(i, i ^ bit) for i in range(count)])  35.6 us
    all_to_all x4, starting transfers between devices, turn(): return lax.all_to_all(x, 'lat', 0, 0)  18.1 us
    all_to_all x4, waiting for transfers between devices, turn(): return lax.all_to_all(x, 'lat', 0, 0)  14.2 us
    pallas_call x1, Pallas kernels, second_half(): pl.pallas_call(functools.partial(second_kernel, p), in_specs=vmem(2) + hb...  11.7 us
    pallas_call x1, Pallas kernels, first_half(): pl.pallas_call(functools.partial(first_kernel, p), in_specs=vmem(3), out_...  11.5 us
    all_to_all x1, blocking collectives, per_device(): lax.all_to_all(q, ('mem', 'lat'), 0, 0)  11.2 us
    pallas_call x2, Pallas kernels, forward(): pl.pallas_call(functools.partial(forward_kernel, p), in_specs=hbm(1) + vm...  6.12 us
  transfers between devices with their start and end apart: 12, of which 10 were waited for; matrix products, arithmetic and copies ran while one was open for 0% of the time, Pallas kernels for 6%

profile of v4, /device:TPU:0, one launch (start us, length us, event | category | flops | bytes accessed | tf_op | source)
XLA Modules:
  0.0 200.0 jit_solution(7600436113002256155)
XLA Ops:
  0.6 0.7 fusion.1
  1.4 0.7 broadcast_in_dim.4
  2.1 7.3 %all-to-all-start.1 = ((f32[8,2,8,384]{3,2,1,0:T(8,128)}), f32[8,2,8,384]{3,2,1,0:T(8,128)S(1)}, u32[]{:S(2)}, u32[]{:S(2)}) async-start(f32[8,2,8,384]{3,2,1,0:T(8,128)} %broadcast_in_dim.4), calls=%async_computation.1 | async-start | bytes 393216 | tf_op jit(solution)/shard_map/all_to_all | solution.py:584
  9.4 4.2 %adjoint_first.1 = f32[8,2,8,1536]{3,2,1,0:T(8,128)} custom-call(bf16[16,15,8,1440]{3,2,1,0:T(8,128)(2,1)} %bitcast.20, f32[15,8,1440]{2,1,0:T(8,128)} %bitcast.12, f32[15,8,1440]{2,1,0:T(8,128)} %bitcast.23), custom_call_target="tpu_custom_call" | custom-call | flops 5529600 | bytes 5529600 | tf_op jit(solution)/shard_map/adjoint_first/pallas_call | solution.py:96
  13.6 3.8 %all-to-all-done.1 = f32[8,2,8,384]{3,2,1,0:T(8,128)S(1)} async-done(((f32[8,2,8,384]{3,2,1,0:T(8,128)}), f32[8,2,8,384]{3,2,1,0:T(8,128)S(1)}, u32[]{:S(2)}, u32[]{:S(2)}) %all-to-all-start.1) | async-done | bytes 196640 | tf_op jit(solution)/shard_map/all_to_all | solution.py:584
  17.3 3.5 %all-to-all-start = ((f32[8,2,8,1536]{3,2,1,0:T(8,128)}), f32[8,2,8,1536]{3,2,1,0:T(8,128)S(1)}, u32[]{:S(2)}, u32[]{:S(2)}) async-start(f32[8,2,8,1536]{3,2,1,0:T(8,128)} %adjoint_first.1), calls=%async_computation | async-start | bytes 1572864 | tf_op jit(solution)/shard_map/all_to_all | solution.py:584
  20.9 0.1 collective-permute-start
  21.0 1.4 collective-permute-done
  22.4 1.6 collective-permute-start.1
  24.0 9.7 %collective-permute-done.1.far = f32[2,8,2,8,384]{4,3,2,1,0:T(8,128)S(1)} collective-permute-done((f32[2,8,2,8,384]{4,3,2,1,0:T(8,128)S(1)}, f32[2,8,2,8,384]{4,3,2,1,0:T(8,128)S(1)}, u32[]{:S(2)}, u32[]{:S(2)}) %collective-permute-start.1) | collective-permute-done | bytes 393248 | tf_op jit(solution)/shard_map/ppermute | solution.py:579
  33.7 6.8 %all-to-all-done.got = f32[8,2,8,1536]{3,2,1,0:T(8,128)S(1)} async-done(((f32[8,2,8,1536]{3,2,1,0:T(8,128)}), f32[8,2,8,1536]{3,2,1,0:T(8,128)S(1)}, u32[]{:S(2)}, u32[]{:S(2)}) %all-to-all-start) | async-done | bytes 786464 | tf_op jit(solution)/shard_map/all_to_all | solution.py:584
  40.5 11.5 %smooth_first.1 = (f32[8,2,8,1536]{3,2,1,0:T(8,128)S(1)}, f32[8,2,8,1440]{3,2,1,0:T(8,128)}, f32[182,8,128]{2,1,0:T(8,128)}, f32[182,8,128]{2,1,0:T(8,128)}, f32[182,8,128]{2,1,0:T(8,128)}) custom-call(f32[8,2,8,1536]{3,2,1,0:T(8,128)S(1)} %all-to-all-done.got, f32[2,8,2,8,384]{4,3,2,1,0:T(8,128)S(1)} %pad_maximum_fusion.near, ...), custom_call_target="tpu_custom_call" | custom-call | tf_op jit(solution)/shard_map/smooth_first/pallas_call | solution.py:485
  52.0 0.0 copy-start
  52.0 23.7 %all_to_all.40 = f32[8,2,8,1536]{3,2,1,0:T(8,128)S(1)} all-to-all(f32[8,2,8,1536]{3,2,1,0:T(8,128)S(1)} %get-tuple-element.28), channel_id=1, replica_groups=mesh['mem'=4,'lat'=8] {'lat'}, dimensions={0} | all-to-all | bytes 1572864 | tf_op jit(solution)/shard_map/all_to_all | solution.py:584
  75.7 3.6 %all-to-all-start.3 = ((f32[8,2,8,1440]{3,2,1,0:T(8,128)}), f32[8,2,8,1440]{3,2,1,0:T(8,128)S(1)}, u32[]{:S(2)}, u32[]{:S(2)}) async-start(f32[8,2,8,1440]{3,2,1,0:T(8,128)} %get-tuple-element.36), calls=%async_computation.3 | async-start | bytes 1572864 | tf_op jit(solution)/shard_map/return_first/all_to_all | solution.py:584
  79.3 3.0 %forward.2 = (f32[8,8,1536]{2,1,0:T(8,128)S(1)}, f32[8,8,1536]{2,1,0:T(8,128)S(1)}, bf16[16,3,5,8,1440]{4,3,2,1,0:T(8,128)(2,1)S(1)}) custom-call(bf16[16,3,5,8,1440]{4,3,2,1,0:T(8,128)(2,1)} %perturb.3, f32[16,8,1536]{2,1,0:T(8,128)S(1)} %bitcast.16), custom_call_target="tpu_custom_call" | custom-call | flops 5529600 | bytes 5529600 | tf_op jit(solution)/shard_map/map_first/forward/pallas_call | solution.py:226
  82.3 0.1 collective-permute-start.2
  82.4 1.7 collective-permute-done.2
  84.1 0.1 add.23
  84.2 1.6 collective-permute-start.3
  85.7 9.7 %collective-permute-done.3 = f32[8,8,1536]{2,1,0:T(8,128)S(1)} collective-permute-done((f32[8,8,1536]{2,1,0:T(8,128)S(1)}, f32[8,8,1536]{2,1,0:T(8,128)S(1)}, u32[]{:S(2)}, u32[]{:S(2)}) %collective-permute-start.3) | collective-permute-done | bytes 393248 | tf_op jit(solution)/shard_map/ppermute | solution.py:579
  95.4 0.1 collective-permute-start.4
  95.5 1.7 collective-permute-done.4.other
  97.2 0.0 copy-done
  97.2 1.5 adjoint_second.1
  98.8 0.0 copy-start.1
  98.8 0.9 copy-done.1
  99.7 0.0 all-to-all-done.3
  99.7 26.2 %all_to_all.41.got = f32[8,2,8,1536]{3,2,1,0:T(8,128)S(1)} all-to-all(f32[8,2,8,1536]{3,2,1,0:T(8,128)S(1)} %get-tuple-element.37), channel_id=1, replica_groups=mesh['mem'=4,'lat'=8] {'lat'}, dimensions={0} | all-to-all | bytes 1572864 | tf_op jit(solution)/shard_map/all_to_all | solution.py:584
  125.9 11.7 %smooth_second.1 = (f32[8,2,8,1536]{3,2,1,0:T(8,128)S(1)}, f32[8,2,8,1440]{3,2,1,0:T(8,128)}, f32[8,128]{1,0:T(8,128)S(1)}) custom-call(f32[8,2,8,1536]{3,2,1,0:T(8,128)S(1)} %all_to_all.41.got, f32[2,8,128]{2,1,0:T(8,128)S(1)} %get-tuple-element.38.scal, f32[182,8,128]{2,1,0:T(8,128)} %get-tuple-element.39.refs_0_, ...), custom_call_target="tpu_custom_call" | custom-call | tf_op jit(solution)/shard_map/smooth_second/pallas_call | solution.py:498
  137.5 23.2 %all_to_all.42 = f32[8,2,8,1536]{3,2,1,0:T(8,128)S(1)} all-to-all(f32[8,2,8,1536]{3,2,1,0:T(8,128)S(1)} %get-tuple-element.42), channel_id=1, replica_groups=mesh['mem'=4,'lat'=8] {'lat'}, dimensions={0} | all-to-all | bytes 1572864 | tf_op jit(solution)/shard_map/all_to_all | solution.py:584
  160.8 3.6 %all-to-all-start.6 = ((f32[8,2,8,1440]{3,2,1,0:T(8,128)}), f32[8,2,8,1440]{3,2,1,0:T(8,128)S(1)}, u32[]{:S(2)}, u32[]{:S(2)}) async-start(f32[8,2,8,1440]{3,2,1,0:T(8,128)} %get-tuple-element.47), calls=%async_computation.6 | async-start | bytes 1572864 | tf_op jit(solution)/shard_map/return_second/all_to_all | solution.py:584
  164.3 3.1 %forward.3 = (f32[8,8,1536]{2,1,0:T(8,128)S(1)}, f32[8,8,1536]{2,1,0:T(8,128)S(1)}) custom-call(bf16[16,3,5,8,1440]{4,3,2,1,0:T(8,128)(2,1)} %perturb.3, f32[16,8,1536]{2,1,0:T(8,128)S(1)} %bitcast.17), custom_call_target="tpu_custom_call" | custom-call | flops 5529600 | bytes 5529600 | tf_op jit(solution)/shard_map/map_second/forward/pallas_call | solution.py:226
  167.5 0.1 collective-permute-start.5
  167.6 1.7 collective-permute-done.5
  169.3 0.1 add.25
  169.3 1.6 collective-permute-start.6
  170.9 9.7 %collective-permute-done.6 = f32[8,8,1536]{2,1,0:T(8,128)S(1)} collective-permute-done((f32[8,8,1536]{2,1,0:T(8,128)S(1)}, f32[8,8,1536]{2,1,0:T(8,128)S(1)}, u32[]{:S(2)}, u32[]{:S(2)}) %collective-permute-start.6) | collective-permute-done | bytes 393248 | tf_op jit(solution)/shard_map/ppermute | solution.py:579
  180.6 3.6 %all-to-all-done.6 = f32[8,2,8,1440]{3,2,1,0:T(8,128)S(1)} async-done(((f32[8,2,8,1440]{3,2,1,0:T(8,128)}), f32[8,2,8,1440]{3,2,1,0:T(8,128)S(1)}, u32[]{:S(2)}, u32[]{:S(2)}) %all-to-all-start.6) | async-done | bytes 737312 | tf_op jit(solution)/shard_map/return_second/all_to_all | solution.py:584
  184.2 0.0 collective-permute-start.7
  184.2 0.0 copy-start.2
  184.2 1.1 copy-done.2
  185.3 0.4 last_sums.1
  185.7 11.2 %all_to_all.43.q = f32[32,8,128]{2,1,0:T(8,128)S(1)} all-to-all(f32[32,8,128]{2,1,0:T(8,128)S(1)} %last_sums.1), channel_id=1, replica_groups=mesh['mem'=4,'lat'=8] {'mem','lat'}, dimensions={0} | all-to-all | bytes 262144 | tf_op jit(solution)/shard_map/all_to_all | solution.py:660
  196.9 0.0 collective-permute-done.7.other
  196.9 3.0 %last_update.1 = (f32[15,8,1440]{2,1,0:T(8,128)}, f32[16,8,1440]{2,1,0:T(8,128)}) custom-call(f32[16,8,1440]{2,1,0:T(8,128)S(1)} %copy-done.2, f32[8,8,1536]{2,1,0:T(8,128)S(1)} %add.26.mine, f32[8,8,1536]{2,1,0:T(8,128)S(1)} %collective-permute-done.7.other, f32[2,8,128]{2,1,0:T(8,128)S(1)} %get-tuple-element.38.scal, ...), custom_call_target="tpu_custom_call" | custom-call | tf_op jit(solution)/shard_map/last_update/pallas_call | solution.py:565
  (3 shorter events, 0.1 us)
Async XLA Ops:
  2.1 15.3 %all-to-all-start.1 = ((f32[8,2,8,384]{3,2,1,0:T(8,128)}), f32[8,2,8,384]{3,2,1,0:T(8,128)S(1)}, u32[]{:S(2)}, u32[]{:S(2)}) async-start(f32[8,2,8,384]{3,2,1,0:T(8,128)} %broadcast_in_dim.4), calls=%async_computation.1 | async-start | bytes 393216 | tf_op jit(solution)/shard_map/all_to_all | solution.py:584
  17.3 23.1 %all-to-all-start = ((f32[8,2,8,1536]{3,2,1,0:T(8,128)}), f32[8,2,8,1536]{3,2,1,0:T(8,128)S(1)}, u32[]{:S(2)}, u32[]{:S(2)}) async-start(f32[8,2,8,1536]{3,2,1,0:T(8,128)} %adjoint_first.1), calls=%async_computation | async-start | bytes 1572864 | tf_op jit(solution)/shard_map/all_to_all | solution.py:584
  20.9 1.5 collective-permute-start
  22.4 11.2 %collective-permute-start.1 = (f32[2,8,2,8,384]{4,3,2,1,0:T(8,128)S(1)}, f32[2,8,2,8,384]{4,3,2,1,0:T(8,128)S(1)}, u32[]{:S(2)}, u32[]{:S(2)}) collective-permute-start(f32[2,8,2,8,384]{4,3,2,1,0:T(8,128)S(1)} %pad_maximum_fusion.near), channel_id=1, source_target_pairs={{0,16},{8,24},{16,0},{24,8},{1,17},{9,25},{17,1},{25,9},{2,18},{10... | collective-permute-start | bytes 1179656 | tf_op jit(solution)/shard_map/ppermute | solution.py:579
  52.0 45.3 %copy-start = (f32[3,5,8,1440]{3,2,1,0:T(8,128)S(1)}, f32[3,5,8,1440]{3,2,1,0:T(8,128)}, u32[]{:S(2)}) copy-start(f32[3,5,8,1440]{3,2,1,0:T(8,128)} %param.7) | copy-start | bytes 2073604
  75.7 24.0 %all-to-all-start.3 = ((f32[8,2,8,1440]{3,2,1,0:T(8,128)}), f32[8,2,8,1440]{3,2,1,0:T(8,128)S(1)}, u32[]{:S(2)}, u32[]{:S(2)}) async-start(f32[8,2,8,1440]{3,2,1,0:T(8,128)} %get-tuple-element.36), calls=%async_computation.3 | async-start | bytes 1572864 | tf_op jit(solution)/shard_map/return_first/all_to_all | solution.py:584
  82.3 1.8 collective-permute-start.2
  84.2 11.2 %collective-permute-start.3 = (f32[8,8,1536]{2,1,0:T(8,128)S(1)}, f32[8,8,1536]{2,1,0:T(8,128)S(1)}, u32[]{:S(2)}, u32[]{:S(2)}) collective-permute-start(f32[8,8,1536]{2,1,0:T(8,128)S(1)} %add.23), channel_id=1, source_target_pairs={{0,16},{8,24},{16,0},{24,8},{1,17},{9,25},{17,1},{25,9},{2,18},{10... | collective-permute-start | bytes 1179656 | tf_op jit(solution)/shard_map/ppermute | solution.py:579
  95.4 1.8 collective-permute-start.4
  98.8 0.9 copy-start.1
  160.8 23.4 %all-to-all-start.6 = ((f32[8,2,8,1440]{3,2,1,0:T(8,128)}), f32[8,2,8,1440]{3,2,1,0:T(8,128)S(1)}, u32[]{:S(2)}, u32[]{:S(2)}) async-start(f32[8,2,8,1440]{3,2,1,0:T(8,128)} %get-tuple-element.47), calls=%async_computation.6 | async-start | bytes 1572864 | tf_op jit(solution)/shard_map/return_second/all_to_all | solution.py:584
  167.5 1.8 collective-permute-start.5
  169.3 11.2 %collective-permute-start.6 = (f32[8,8,1536]{2,1,0:T(8,128)S(1)}, f32[8,8,1536]{2,1,0:T(8,128)S(1)}, u32[]{:S(2)}, u32[]{:S(2)}) collective-permute-start(f32[8,8,1536]{2,1,0:T(8,128)S(1)} %add.25), channel_id=1, source_target_pairs={{0,16},{8,24},{16,0},{24,8},{1,17},{9,25},{17,1},{25,9},{2,18},{10... | collective-permute-start | bytes 1179656 | tf_op jit(solution)/shard_map/ppermute | solution.py:579
  184.2 12.8 %collective-permute-start.7 = (f32[8,8,1536]{2,1,0:T(8,128)S(1)}, f32[8,8,1536]{2,1,0:T(8,128)S(1)}, u32[]{:S(2)}, u32[]{:S(2)}) collective-permute-start(f32[8,8,1536]{2,1,0:T(8,128)S(1)} %add.26.mine), channel_id=1, source_target_pairs={{0,8},{8,0},{16,24},{24,16},{1,9},{9,1},{17,25},{25,17},{2,10},{10... | collective-permute-start | bytes 1179656 | tf_op jit(solution)/shard_map/ppermute | solution.py:579
  184.2 1.1 copy-start.2

commit v5 on v4

--- a/solution.py
+++ b/solution.py
@@ -7,6 +7,7 @@
 from jax.experimental.pallas import tpu as pltpu
 from jax.sharding import PartitionSpec as P
 
+
 PASSES = 10
 LANES = 128
 SUB = 8
@@ -18,7 +19,7 @@
 
 
 class Plan:
-    def __init__(self, perturb, lat_coef, mem, lat):
+    def __init__(self, perturb, mem, lat):
         self.members, self.slots, self.vars, self.rows, self.nlon = perturb.shape
         self.mem, self.lat = mem, lat
         self.fields = self.slots * self.vars
@@ -44,6 +45,7 @@
             q for q in (1, 2, 4) if mem % q == 0 and self.wide % (q * LANES) == 0
         )
         self.piece = self.wide // self.parts
+        self.doubling = self.groups == 1 and lat > 1 and lat & (lat - 1) == 0
 
 
 def mapped(p, perturb, first, prod):
@@ -337,7 +339,7 @@
 
 
 def spread(p, low, high, lower, east, north, south, diag):
-    row, lane = lane_row(p)
+    row, _ = lane_row(p)
 
     def coefs(i, none):
         below = lower[i + 1]
@@ -356,10 +358,12 @@
     row, lane = lane_row(p)
     low, high = ends(p)
     mine = lax.axis_index("mem") % p.parts
-    for k in range(max(p.parts // 2, 1)):
-        coef[mine ^ k] = near[k]
-    for k in range(p.parts // 2):
-        coef[mine ^ (p.parts // 2) ^ k] = far[k]
+    here = lax.axis_index("lat") if p.doubling else 0
+    for c in range(p.window):
+        for k in range(max(p.parts // 2, 1)):
+            coef[mine ^ k, here ^ c] = near[k, c]
+        for k in range(p.parts // 2):
+            coef[mine ^ (p.parts // 2) ^ k, here ^ c] = far[k, c]
     per = p.piece // LANES
 
     def pick(which):
@@ -494,7 +498,7 @@
 
 
 def second_half(p, got, scal, right, east, lower):
-    buf, rows, back, scratch = half_shapes(p)
+    _, rows, back, scratch = half_shapes(p)
     return pl.pallas_call(
         functools.partial(second_kernel, p),
         in_specs=vmem(2) + hbm(3),
@@ -575,7 +579,7 @@
     )(total, mine, other, scal, ahead, q, right, resid)
 
 
-def swap(p, x, axis, bit, count):
+def swap(x, axis, bit, count):
     return lax.ppermute(x, axis, [(i, i ^ bit) for i in range(count)])
 
 
@@ -598,10 +602,10 @@
 
 
 def member_sum(p, keep, send):
-    mine = keep + swap(p, send, "mem", 1, p.mem)
+    mine = keep + swap(send, "mem", 1, p.mem)
     bit = 2
     while bit < p.mem:
-        mine = mine + swap(p, mine, "mem", bit, p.mem)
+        mine = mine + swap(mine, "mem", bit, p.mem)
         bit *= 2
     if p.groups > 1:
         tail = lax.psum(mine[:1, :, p.nlon :], "lat") / p.group
@@ -612,21 +616,31 @@
 def coefficients(p, lon_coef, lat_coef):
     both = jnp.pad(jnp.stack([lon_coef, lat_coef]), ((0, 0), (0, 0), (0, p.wide - p.nlon)))
     part = lax.axis_index("mem") % p.parts
-    both = lax.dynamic_slice_in_dim(both, part * p.piece, p.piece, axis=2)
-    return turn(p, jnp.broadcast_to(both[None], (p.group, 2, p.rows, p.piece)))
+    both = lax.dynamic_slice_in_dim(both, part * p.piece, p.piece, axis=2)[None]
+    if not p.doubling:
+        return turn(p, jnp.broadcast_to(both, (p.group, 2, p.rows, p.piece)))
+    return jnp.concatenate([both, swap(both, "lat", 1, p.lat)])
+
+
+def gather_on(p, pieces):
+    bit = 2
+    while p.doubling and bit < p.lat:
+        pieces = jnp.concatenate([pieces, swap(pieces, "lat", bit, p.lat)])
+        bit *= 2
+    return pieces
 
 
 def share_out(p, pieces):
-    near = widen(p, pieces)[None]
+    near = widen(p, gather_on(p, pieces))[None]
     if p.parts == 1:
         return near, near
     if p.parts == 4:
-        near = jnp.concatenate([near, swap(p, near, "mem", 1, p.mem)])
-    return near, swap(p, near, "mem", p.parts // 2, p.mem)
+        near = jnp.concatenate([near, swap(near, "mem", 1, p.mem)])
+    return near, swap(near, "mem", p.parts // 2, p.mem)
 
 
 def per_device(perturb, innovation, obs_weight, lon_coef, lat_coef):
-    p = Plan(perturb, lat_coef, lax.axis_size("mem"), lax.axis_size("lat"))
+    p = Plan(perturb, lax.axis_size("mem"), lax.axis_size("lat"))
     flat = lambda x: x.reshape(p.fields, p.rows, p.nlon)
     by_rank = lambda x: x.reshape((p.members,) + x.shape[2:])
     weight = flat(obs_weight)
@@ -634,28 +648,27 @@
 
     pieces = coefficients(p, lon_coef, lat_coef)
     sent = adjoint_first(p, by_member, weight, flat(innovation))
+    if p.doubling:
+        sent, pieces = lax.optimization_barrier((sent, pieces))
+    got = turn(p, sent)
     near, far = share_out(p, pieces)
-    back, rows_right, *kept = first_half(p, widen(p, turn(p, sent)), near, far)
+    back, rows_right, *kept = first_half(p, widen(p, got), near, far)
     field, rows_right = lax.optimization_barrier((turn(p, back), rows_right))
-    with jax.named_scope("return_first"):
-        rows_right = by_rank(turn(p, rows_right))
-    with jax.named_scope("map_first"):
-        keep, send, held = forward(p, perturb, by_rank(field), True)
+    rows_right = by_rank(turn(p, rows_right))
+    keep, send, held = forward(p, perturb, by_rank(field), True)
     mine = member_sum(p, keep, send)
-    other = swap(p, mine, "mem", 1, p.mem)
+    other = swap(mine, "mem", 1, p.mem)
     sent, total, scal = adjoint(p, held.reshape(by_member.shape), weight, mine, other)
     sent, rows_right = lax.optimization_barrier((sent, rows_right))
     if p.groups > 1:
         scal = jnp.concatenate([scal[:1], lax.psum(scal[1:], "lat")], axis=0)
     back, rows_resid, ahead = second_half(p, widen(p, turn(p, sent)), scal, *kept)
     field, rows_resid = lax.optimization_barrier((turn(p, back), rows_resid))
-    with jax.named_scope("return_second"):
-        rows_resid = by_rank(turn(p, rows_resid))
-    with jax.named_scope("map_second"):
-        keep, send = forward(p, perturb, by_rank(field), False)
+    rows_resid = by_rank(turn(p, rows_resid))
+    keep, send = forward(p, perturb, by_rank(field), False)
     mine = member_sum(p, keep, send)
     mine, rows_resid = lax.optimization_barrier((mine, rows_resid))
-    other = swap(p, mine, "mem", 1, p.mem)
+    other = swap(mine, "mem", 1, p.mem)
     q = test(p, weight, total, mine, scal)
     q = lax.all_to_all(q, ("mem", "lat"), 0, 0) if p.groups == 1 else lax.psum(q, ("mem", "lat"))
     grown, control = last(p, total, mine, other, scal, ahead, q, rows_right, rows_resid)

time: 201 us -> 210 us (1.045)
  waiting for transfers between devices: 49.7 us -> 56.4 us
  starting transfers between devices: 23 us -> 26.9 us
    ppermute x8 -> x11, waiting for transfers between devices: 35.6 us -> 52.9 us  [swap(): return lax.ppermute(x, axis, [(i, i ^ bit) for i in range(count)])]
    all_to_all x4 -> x3, waiting for transfers between devices: 14.2 us -> 3.57 us  [turn(): return lax.all_to_all(x, 'lat', 0, 0)]
    ppermute x8 -> x11, starting transfers between devices: 4.96 us -> 14.9 us  [swap(): return lax.ppermute(x, axis, [(i, i ^ bit) for i in range(count)])]
    all_to_all x4 -> x3, starting transfers between devices: 18.1 us -> 12.1 us  [turn(): return lax.all_to_all(x, 'lat', 0, 0)]
  transfers between devices with their start and end apart: 12 -> 14, of which waited for: 10 -> 10; matrix products, arithmetic and copies ran while one was open for 0% -> 0% of each run, Pallas kernels for 6% -> 6%
where the time goes in v5:
time: 210 us; the launch traced here: 209 us
  blocking collectives  83.7 us (40%)
  waiting for transfers between devices  56.4 us (27%)
  Pallas kernels  38.3 us (18%)
  starting transfers between devices  26.9 us (13%)
    all_to_all x3, blocking collectives, turn(): return lax.all_to_all(x, 'lat', 0, 0)  72.5 us
    ppermute x11, waiting for transfers between devices, swap(): return lax.ppermute(x, axis, [(i, i ^ bit) for i in range(count)])  52.9 us
    ppermute x11, starting transfers between devices, swap(): return lax.ppermute(x, axis, [(i, i ^ bit) for i in range(count)])  14.9 us
    all_to_all x3, starting transfers between devices, turn(): return lax.all_to_all(x, 'lat', 0, 0)  12.1 us
    pallas_call x1, Pallas kernels, second_half(): pl.pallas_call(functools.partial(second_kernel, p), in_specs=vmem(2) + hb...  11.7 us
    pallas_call x1, Pallas kernels, first_half(): pl.pallas_call(functools.partial(first_kernel, p), in_specs=vmem(3), out_...  11.5 us
    all_to_all x1, blocking collectives, per_device(): lax.all_to_all(q, ('mem', 'lat'), 0, 0)  11.2 us
    pallas_call x2, Pallas kernels, forward(): pl.pallas_call(functools.partial(forward_kernel, p), in_specs=hbm(1) + vm...  6.12 us
  transfers between devices with their start and end apart: 14, of which 10 were waited for; matrix products, arithmetic and copies ran while one was open for 0% of the time, Pallas kernels for 6%

profile of v5, /device:TPU:0, one launch (start us, length us, event | category | flops | bytes accessed | tf_op | source)
XLA Modules:
  0.0 209.2 jit_solution(13790365130253082449)
XLA Ops:
  0.6 0.7 fusion.2
  1.4 3.1 %collective-permute-start = (f32[1,2,8,384]{3,2,1,0:T(8,128)S(1)}, f32[1,2,8,384]{3,2,1,0:T(8,128)S(1)}, u32[]{:S(2)}, u32[]{:S(2)}) collective-permute-start(f32[1,2,8,384]{3,2,1,0:T(8,128)S(1)} %fusion.2), channel_id=1, source_target_pairs={{0,1},{1,0},{2,3},{3,2},{4,5},{5,4},{6,7},{7,6},{8,9},{9,8},{10,11... | collective-permute-start | bytes 73736 | tf_op jit(solution)/shard_map/ppermute | solution.py:583
  4.5 4.2 %adjoint_first.1 = f32[8,2,8,1536]{3,2,1,0:T(8,128)} custom-call(bf16[16,15,8,1440]{3,2,1,0:T(8,128)(2,1)} %bitcast.23, f32[15,8,1440]{2,1,0:T(8,128)} %bitcast.15, f32[15,8,1440]{2,1,0:T(8,128)} %bitcast.24), custom_call_target="tpu_custom_call" | custom-call | flops 5529600 | bytes 5529600 | tf_op jit(solution)/shard_map/adjoint_first/pallas_call | solution.py:98
  8.6 0.0 collective-permute-done
  8.6 4.9 %all-to-all-start = ((f32[8,2,8,1536]{3,2,1,0:T(8,128)}), f32[8,2,8,1536]{3,2,1,0:T(8,128)S(1)}, u32[]{:S(2)}, u32[]{:S(2)}) async-start(f32[8,2,8,1536]{3,2,1,0:T(8,128)} %adjoint_first.1), calls=%async_computation | async-start | bytes 1572864 | tf_op jit(solution)/shard_map/all_to_all | solution.py:588
  13.5 2.0 collective-permute-start.1
  15.5 11.5 %collective-permute-done.1 = f32[2,2,8,384]{3,2,1,0:T(8,128)S(1)} collective-permute-done((f32[2,2,8,384]{3,2,1,0:T(8,128)S(1)}, f32[2,2,8,384]{3,2,1,0:T(8,128)S(1)}, u32[]{:S(2)}, u32[]{:S(2)}) %collective-permute-start.1) | collective-permute-done | bytes 49184 | tf_op jit(solution)/shard_map/ppermute | solution.py:583
  27.1 4.8 %collective-permute-start.2 = (f32[4,2,8,384]{3,2,1,0:T(8,128)S(1)}, f32[4,2,8,384]{3,2,1,0:T(8,128)S(1)}, u32[]{:S(2)}, u32[]{:S(2)}) collective-permute-start(f32[4,2,8,384]{3,2,1,0:T(8,128)S(1)} %pad_maximum_fusion.1), channel_id=1, source_target_pairs={{0,4},{1,5},{2,6},{3,7},{4,0},{5,1},{6,2},{7,3},{8,12},{9,13},{10,... | collective-permute-start | bytes 294920 | tf_op jit(solution)/shard_map/ppermute | solution.py:583
  31.9 5.8 %collective-permute-done.2 = f32[4,2,8,384]{3,2,1,0:T(8,128)S(1)} collective-permute-done((f32[4,2,8,384]{3,2,1,0:T(8,128)S(1)}, f32[4,2,8,384]{3,2,1,0:T(8,128)S(1)}, u32[]{:S(2)}, u32[]{:S(2)}) %collective-permute-start.2) | collective-permute-done | bytes 98336 | tf_op jit(solution)/shard_map/ppermute | solution.py:583
  37.7 0.1 collective-permute-start.3
  37.8 1.4 collective-permute-done.3
  39.3 1.6 collective-permute-start.4
  40.8 9.7 %collective-permute-done.4.far = f32[2,8,2,8,384]{4,3,2,1,0:T(8,128)S(1)} collective-permute-done((f32[2,8,2,8,384]{4,3,2,1,0:T(8,128)S(1)}, f32[2,8,2,8,384]{4,3,2,1,0:T(8,128)S(1)}, u32[]{:S(2)}, u32[]{:S(2)}) %collective-permute-start.4) | collective-permute-done | bytes 393248 | tf_op jit(solution)/shard_map/ppermute | solution.py:583
  50.5 0.0 all-to-all-done.got
  50.5 11.5 %smooth_first.1 = (f32[8,2,8,1536]{3,2,1,0:T(8,128)S(1)}, f32[8,2,8,1440]{3,2,1,0:T(8,128)}, f32[182,8,128]{2,1,0:T(8,128)}, f32[182,8,128]{2,1,0:T(8,128)}, f32[182,8,128]{2,1,0:T(8,128)}) custom-call(f32[8,2,8,1536]{3,2,1,0:T(8,128)S(1)} %all-to-all-done.got, f32[2,8,2,8,384]{4,3,2,1,0:T(8,128)S(1)} %pad_maximum_fusion.near, ...), custom_call_target="tpu_custom_call" | custom-call | tf_op jit(solution)/shard_map/smooth_first/pallas_call | solution.py:489
  62.0 0.0 copy-start
  62.0 23.0 %all_to_all.35 = f32[8,2,8,1536]{3,2,1,0:T(8,128)S(1)} all-to-all(f32[8,2,8,1536]{3,2,1,0:T(8,128)S(1)} %get-tuple-element.32), channel_id=1, replica_groups=mesh['mem'=4,'lat'=8] {'lat'}, dimensions={0} | all-to-all | bytes 1572864 | tf_op jit(solution)/shard_map/all_to_all | solution.py:588
  85.0 3.6 %all-to-all-start.2 = ((f32[8,2,8,1440]{3,2,1,0:T(8,128)}), f32[8,2,8,1440]{3,2,1,0:T(8,128)S(1)}, u32[]{:S(2)}, u32[]{:S(2)}) async-start(f32[8,2,8,1440]{3,2,1,0:T(8,128)} %get-tuple-element.40), calls=%async_computation.2 | async-start | bytes 1572864 | tf_op jit(solution)/shard_map/all_to_all | solution.py:588
  88.6 3.0 %forward.2 = (f32[8,8,1536]{2,1,0:T(8,128)S(1)}, f32[8,8,1536]{2,1,0:T(8,128)S(1)}, bf16[16,3,5,8,1440]{4,3,2,1,0:T(8,128)(2,1)S(1)}) custom-call(bf16[16,3,5,8,1440]{4,3,2,1,0:T(8,128)(2,1)} %perturb.3, f32[16,8,1536]{2,1,0:T(8,128)S(1)} %bitcast.19), custom_call_target="tpu_custom_call" | custom-call | flops 5529600 | bytes 5529600 | tf_op jit(solution)/shard_map/forward/pallas_call | solution.py:228
  91.6 0.1 collective-permute-start.5
  91.7 1.7 collective-permute-done.5
  93.4 0.1 add.23
  93.4 1.6 collective-permute-start.6
  95.0 9.7 %collective-permute-done.6 = f32[8,8,1536]{2,1,0:T(8,128)S(1)} collective-permute-done((f32[8,8,1536]{2,1,0:T(8,128)S(1)}, f32[8,8,1536]{2,1,0:T(8,128)S(1)}, u32[]{:S(2)}, u32[]{:S(2)}) %collective-permute-start.6) | collective-permute-done | bytes 393248 | tf_op jit(solution)/shard_map/ppermute | solution.py:583
  104.7 0.1 collective-permute-start.7
  104.8 1.7 collective-permute-done.7.other
  106.5 0.0 copy-done
  106.5 1.5 adjoint_second.1
  108.0 0.0 copy-start.1
  108.1 0.9 copy-done.1
  108.9 0.0 all-to-all-done.2
  108.9 26.2 %all_to_all.36.got = f32[8,2,8,1536]{3,2,1,0:T(8,128)S(1)} all-to-all(f32[8,2,8,1536]{3,2,1,0:T(8,128)S(1)} %get-tuple-element.41), channel_id=1, replica_groups=mesh['mem'=4,'lat'=8] {'lat'}, dimensions={0} | all-to-all | bytes 1572864 | tf_op jit(solution)/shard_map/all_to_all | solution.py:588
  135.1 11.7 %smooth_second.1 = (f32[8,2,8,1536]{3,2,1,0:T(8,128)S(1)}, f32[8,2,8,1440]{3,2,1,0:T(8,128)}, f32[8,128]{1,0:T(8,128)S(1)}) custom-call(f32[8,2,8,1536]{3,2,1,0:T(8,128)S(1)} %all_to_all.36.got, f32[2,8,128]{2,1,0:T(8,128)S(1)} %get-tuple-element.42.scal, f32[182,8,128]{2,1,0:T(8,128)} %get-tuple-element.43.refs_0_, ...), custom_call_target="tpu_custom_call" | custom-call | tf_op jit(solution)/shard_map/smooth_second/pallas_call | solution.py:502
  146.8 23.2 %all_to_all.37 = f32[8,2,8,1536]{3,2,1,0:T(8,128)S(1)} all-to-all(f32[8,2,8,1536]{3,2,1,0:T(8,128)S(1)} %get-tuple-element.46), channel_id=1, replica_groups=mesh['mem'=4,'lat'=8] {'lat'}, dimensions={0} | all-to-all | bytes 1572864 | tf_op jit(solution)/shard_map/all_to_all | solution.py:588
  170.0 3.6 %all-to-all-start.5 = ((f32[8,2,8,1440]{3,2,1,0:T(8,128)}), f32[8,2,8,1440]{3,2,1,0:T(8,128)S(1)}, u32[]{:S(2)}, u32[]{:S(2)}) async-start(f32[8,2,8,1440]{3,2,1,0:T(8,128)} %get-tuple-element.51), calls=%async_computation.5 | async-start | bytes 1572864 | tf_op jit(solution)/shard_map/all_to_all | solution.py:588
  173.6 3.1 %forward.3 = (f32[8,8,1536]{2,1,0:T(8,128)S(1)}, f32[8,8,1536]{2,1,0:T(8,128)S(1)}) custom-call(bf16[16,3,5,8,1440]{4,3,2,1,0:T(8,128)(2,1)} %perturb.3, f32[16,8,1536]{2,1,0:T(8,128)S(1)} %bitcast.20), custom_call_target="tpu_custom_call" | custom-call | flops 5529600 | bytes 5529600 | tf_op jit(solution)/shard_map/forward/pallas_call | solution.py:228
  176.7 0.1 collective-permute-start.8
  176.8 1.7 collective-permute-done.8
  178.5 0.1 add.25
  178.6 1.6 collective-permute-start.9
  180.1 9.7 %collective-permute-done.9 = f32[8,8,1536]{2,1,0:T(8,128)S(1)} collective-permute-done((f32[8,8,1536]{2,1,0:T(8,128)S(1)}, f32[8,8,1536]{2,1,0:T(8,128)S(1)}, u32[]{:S(2)}, u32[]{:S(2)}) %collective-permute-start.9) | collective-permute-done | bytes 393248 | tf_op jit(solution)/shard_map/ppermute | solution.py:583
  189.9 3.6 %all-to-all-done.5 = f32[8,2,8,1440]{3,2,1,0:T(8,128)S(1)} async-done(((f32[8,2,8,1440]{3,2,1,0:T(8,128)}), f32[8,2,8,1440]{3,2,1,0:T(8,128)S(1)}, u32[]{:S(2)}, u32[]{:S(2)}) %all-to-all-start.5) | async-done | bytes 737312 | tf_op jit(solution)/shard_map/all_to_all | solution.py:588
  193.4 0.0 collective-permute-start.10
  193.4 1.1 copy-done.2
  194.6 0.4 last_sums.1
  194.9 11.2 %all_to_all.38.q = f32[32,8,128]{2,1,0:T(8,128)S(1)} all-to-all(f32[32,8,128]{2,1,0:T(8,128)S(1)} %last_sums.1), channel_id=1, replica_groups=mesh['mem'=4,'lat'=8] {'mem','lat'}, dimensions={0} | all-to-all | bytes 262144 | tf_op jit(solution)/shard_map/all_to_all | solution.py:673
  206.2 0.0 collective-permute-done.10.other
  206.2 3.0 %last_update.1 = (f32[15,8,1440]{2,1,0:T(8,128)}, f32[16,8,1440]{2,1,0:T(8,128)}) custom-call(f32[16,8,1440]{2,1,0:T(8,128)S(1)} %copy-done.2, f32[8,8,1536]{2,1,0:T(8,128)S(1)} %add.26.mine, f32[8,8,1536]{2,1,0:T(8,128)S(1)} %collective-permute-done.10.other, f32[2,8,128]{2,1,0:T(8,128)S(1)} %get-tuple-element.42.scal, ...), custom_call_target="tpu_custom_call" | custom-call | tf_op jit(solution)/shard_map/last_update/pallas_call | solution.py:569
  (7 shorter events, 0.1 us)
Async XLA Ops:
  1.4 7.2 %collective-permute-start = (f32[1,2,8,384]{3,2,1,0:T(8,128)S(1)}, f32[1,2,8,384]{3,2,1,0:T(8,128)S(1)}, u32[]{:S(2)}, u32[]{:S(2)}) collective-permute-start(f32[1,2,8,384]{3,2,1,0:T(8,128)S(1)} %fusion.2), channel_id=1, source_target_pairs={{0,1},{1,0},{2,3},{3,2},{4,5},{5,4},{6,7},{7,6},{8,9},{9,8},{10,11... | collective-permute-start | bytes 73736 | tf_op jit(solution)/shard_map/ppermute | solution.py:583
  8.6 41.8 %all-to-all-start = ((f32[8,2,8,1536]{3,2,1,0:T(8,128)}), f32[8,2,8,1536]{3,2,1,0:T(8,128)S(1)}, u32[]{:S(2)}, u32[]{:S(2)}) async-start(f32[8,2,8,1536]{3,2,1,0:T(8,128)} %adjoint_first.1), calls=%async_computation | async-start | bytes 1572864 | tf_op jit(solution)/shard_map/all_to_all | solution.py:588
  13.5 13.6 %collective-permute-start.1 = (f32[2,2,8,384]{3,2,1,0:T(8,128)S(1)}, f32[2,2,8,384]{3,2,1,0:T(8,128)S(1)}, u32[]{:S(2)}, u32[]{:S(2)}) collective-permute-start(f32[2,2,8,384]{3,2,1,0:T(8,128)S(1)} %pad_maximum_fusion.2), channel_id=1, source_target_pairs={{0,2},{1,3},{2,0},{3,1},{4,6},{5,7},{6,4},{7,5},{8,10},{9,11},{10,... | collective-permute-start | bytes 147464 | tf_op jit(solution)/shard_map/ppermute | solution.py:583
  27.1 10.6 %collective-permute-start.2 = (f32[4,2,8,384]{3,2,1,0:T(8,128)S(1)}, f32[4,2,8,384]{3,2,1,0:T(8,128)S(1)}, u32[]{:S(2)}, u32[]{:S(2)}) collective-permute-start(f32[4,2,8,384]{3,2,1,0:T(8,128)S(1)} %pad_maximum_fusion.1), channel_id=1, source_target_pairs={{0,4},{1,5},{2,6},{3,7},{4,0},{5,1},{6,2},{7,3},{8,12},{9,13},{10,... | collective-permute-start | bytes 294920 | tf_op jit(solution)/shard_map/ppermute | solution.py:583
  37.7 1.5 collective-permute-start.3
  39.3 11.2 %collective-permute-start.4 = (f32[2,8,2,8,384]{4,3,2,1,0:T(8,128)S(1)}, f32[2,8,2,8,384]{4,3,2,1,0:T(8,128)S(1)}, u32[]{:S(2)}, u32[]{:S(2)}) collective-permute-start(f32[2,8,2,8,384]{4,3,2,1,0:T(8,128)S(1)} %pad_maximum_fusion.near), channel_id=1, source_target_pairs={{0,16},{8,24},{16,0},{24,8},{1,17},{9,25},{17,1},{25,9},{2,18},{10... | collective-permute-start | bytes 1179656 | tf_op jit(solution)/shard_map/ppermute | solution.py:583
  62.0 44.5 %copy-start = (f32[3,5,8,1440]{3,2,1,0:T(8,128)S(1)}, f32[3,5,8,1440]{3,2,1,0:T(8,128)}, u32[]{:S(2)}) copy-start(f32[3,5,8,1440]{3,2,1,0:T(8,128)} %param.7) | copy-start | bytes 2073604
  85.0 23.9 %all-to-all-start.2 = ((f32[8,2,8,1440]{3,2,1,0:T(8,128)}), f32[8,2,8,1440]{3,2,1,0:T(8,128)S(1)}, u32[]{:S(2)}, u32[]{:S(2)}) async-start(f32[8,2,8,1440]{3,2,1,0:T(8,128)} %get-tuple-element.40), calls=%async_computation.2 | async-start | bytes 1572864 | tf_op jit(solution)/shard_map/all_to_all | solution.py:588
  91.6 1.8 collective-permute-start.5
  93.4 11.2 %collective-permute-start.6 = (f32[8,8,1536]{2,1,0:T(8,128)S(1)}, f32[8,8,1536]{2,1,0:T(8,128)S(1)}, u32[]{:S(2)}, u32[]{:S(2)}) collective-permute-start(f32[8,8,1536]{2,1,0:T(8,128)S(1)} %add.23), channel_id=1, source_target_pairs={{0,16},{8,24},{16,0},{24,8},{1,17},{9,25},{17,1},{25,9},{2,18},{10... | collective-permute-start | bytes 1179656 | tf_op jit(solution)/shard_map/ppermute | solution.py:583
  104.7 1.8 collective-permute-start.7
  108.0 0.9 copy-start.1
  170.0 23.4 %all-to-all-start.5 = ((f32[8,2,8,1440]{3,2,1,0:T(8,128)}), f32[8,2,8,1440]{3,2,1,0:T(8,128)S(1)}, u32[]{:S(2)}, u32[]{:S(2)}) async-start(f32[8,2,8,1440]{3,2,1,0:T(8,128)} %get-tuple-element.51), calls=%async_computation.5 | async-start | bytes 1572864 | tf_op jit(solution)/shard_map/all_to_all | solution.py:588
  176.7 1.8 collective-permute-start.8
  178.6 11.2 %collective-permute-start.9 = (f32[8,8,1536]{2,1,0:T(8,128)S(1)}, f32[8,8,1536]{2,1,0:T(8,128)S(1)}, u32[]{:S(2)}, u32[]{:S(2)}) collective-permute-start(f32[8,8,1536]{2,1,0:T(8,128)S(1)} %add.25), channel_id=1, source_target_pairs={{0,16},{8,24},{16,0},{24,8},{1,17},{9,25},{17,1},{25,9},{2,18},{10... | collective-permute-start | bytes 1179656 | tf_op jit(solution)/shard_map/ppermute | solution.py:583
  193.4 12.8 %collective-permute-start.10 = (f32[8,8,1536]{2,1,0:T(8,128)S(1)}, f32[8,8,1536]{2,1,0:T(8,128)S(1)}, u32[]{:S(2)}, u32[]{:S(2)}) collective-permute-start(f32[8,8,1536]{2,1,0:T(8,128)S(1)} %add.26.mine), channel_id=1, source_target_pairs={{0,8},{8,0},{16,24},{24,16},{1,9},{9,1},{17,25},{25,17},{2,10},{10... | collective-permute-start | bytes 1179656 | tf_op jit(solution)/shard_map/ppermute | solution.py:583
  193.4 1.1 copy-start.2

commit v6 on v4

--- a/solution.py
+++ b/solution.py
@@ -38,8 +38,7 @@
         self.lanes = ceil_to(self.used, LANES)
         self.tiles = self.lanes // LANES
         self.step = self.nlon // SUB
-        self.unroll = max(u for u in range(1, 21) if self.step % u == 0)
-        self.stride = max(u for u in range(1, 181) if self.step % u == 0)
+        self.unroll = self.stride = max(u for u in range(1, 181) if self.step % u == 0)
         self.parts = max(
             q for q in (1, 2, 4) if mem % q == 0 and self.wide % (q * LANES) == 0
         )
@@ -112,8 +111,9 @@
     )(*held)
 
 
-def adjoint_kernel(p, perturb, weight, mine, other, out, total, scal, prod):
+def adjoint_kernel(p, perturb, weight, mine, other, out, store, scal, prod, total, sem):
     step = pl.program_id(0)
+    leave = pltpu.make_async_copy(total, store, sem)
 
     @pl.when(step == 0)
     def _():
@@ -129,12 +129,17 @@
         rr = mine[0, :1, p.nlon : p.nlon + 1]
         scal[0] = jnp.broadcast_to(rr, (p.rows, LANES))
         scal[1] = jnp.full((p.rows, LANES), jnp.sum(acc))
+        leave.start()
 
     acc = mapped(p, perturb, 0, prod)
     tail = jnp.broadcast_to(scal[1][:1, :1], (p.rows, p.wide - p.nlon))
     for m in range(p.share):
         out[0, m, :, : p.nlon] = acc[m]
         out[0, m, :, p.nlon :] = tail
+
+    @pl.when(step == p.group - 1)
+    def _():
+        leave.wait()
 
 
 def adjoint(p, perturb, weight, mine, other):
@@ -151,15 +156,19 @@
         ],
         out_specs=[
             pl.BlockSpec((1, p.share, rows, p.wide), lambda i: (i, 0, 0, 0)),
-            whole(2 * p.half, rows, nlon),
+            hbm(1)[0],
             whole(2, rows, LANES),
         ],
         out_shape=[
             jax.ShapeDtypeStruct((p.group, p.share, rows, p.wide), jnp.float32),
-            jax.ShapeDtypeStruct((2 * p.half, rows, nlon), jnp.float32),
+            pltpu.HBM((2 * p.half, rows, nlon), jnp.float32),
             jax.ShapeDtypeStruct((2, rows, LANES), jnp.float32),
         ],
-        scratch_shapes=[pltpu.VMEM((2 * p.half, rows, nlon), jnp.float32)],
+        scratch_shapes=[
+            pltpu.VMEM((2 * p.half, rows, nlon), jnp.float32),
+            pltpu.VMEM((2 * p.half, rows, nlon), jnp.float32),
+            pltpu.SemaphoreType.DMA(()),
+        ],
         compiler_params=ROOM,
         cost_estimate=cost(p, 2),
         name="adjoint_second",
@@ -316,11 +325,9 @@
         a[...] = b[...]
 
 
-def total_of(p, own, term):
-    def one(i, acc):
-        return acc + term(i + 1)
-    acc = lax.fori_loop(0, p.step, one, jnp.zeros((SUB, p.lanes), jnp.float32), unroll=p.unroll)
-    return jnp.sum(jnp.where(own, acc, 0.0))
+def put(p, sheet, i, value):
+    for t in range(p.tiles):
+        sheet[t, pl.ds(i, SUB, stride=p.step), :] = value[:, tile(t)]
 
 
 def own_lanes(p):
@@ -336,11 +343,14 @@
     return jnp.maximum(-here, 0) * p.rows, jnp.minimum(p.lat - here, p.window) * p.rows - 1
 
 
-def spread(p, low, high, lower, east, north, south, diag):
+def spread(p, low, high, inside, lower, east, north, south, diag):
     row, lane = lane_row(p)
 
     def coefs(i, none):
         below = lower[i + 1]
+        if inside is not None:
+            below = jnp.where(inside, below, 0.0)
+            lower[i + 1] = below
         above = jnp.where(row < high, roll(below, -1, 1), 0.0)
         diag[i + 1] = (1.0 - (below + above)) - (east[i + 1] + east[i])
         north[i + 1] = above
@@ -374,22 +384,19 @@
     wrap(p, east)
     inside = (row >= low) & (row <= high) & (lane < p.used)
 
-    def clean(i, none):
-        lower[i + 1] = jnp.where(inside, lower[i + 1], 0.0)
-        return none
-    lax.fori_loop(0, p.step, clean, 0, unroll=p.unroll)
-    spread(p, low, high, lower, east, north, south, diag)
+    spread(p, low, high, inside, lower, east, north, south, diag)
     flip(p, lambda c, m, cols: got[c, m, :, cols], sheet)
     sheet_to(p, sheet, a)
     wrap(p, a)
     ten(p, a, b, east, north, south, diag)
 
-    def keep(i, none):
-        right[i + 1] = a[i + 1]
-        return none
-    lax.fori_loop(0, p.step, keep, 0, unroll=p.unroll)
-    rr = total_of(p, own_lanes(p), lambda i: a[i] * a[i])
-    to_sheet(p, a, sheet)
+    def keep(i, acc):
+        b0 = a[i + 1]
+        right[i + 1] = b0
+        put(p, sheet, i, b0)
+        return acc + b0 * b0
+    rr = lax.fori_loop(0, p.step, keep, jnp.zeros((SUB, p.lanes), jnp.float32), unroll=p.unroll)
+    rr = jnp.sum(jnp.where(own_lanes(p), rr, 0.0))
     unflip(p, sheet, rows_right, p.nlon)
     moves = [
         pltpu.make_async_copy(src, dst, sem.at[k])
@@ -432,7 +439,7 @@
     wrap(p, a)
     moves[0].wait()
     moves[1].wait()
-    spread(p, *ends(p), lower, east, north, south, diag)
+    spread(p, *ends(p), None, lower, east, north, south, diag)
     ten(p, a, b, east, north, south, diag)
     moves[2].wait()
     alpha = jnp.broadcast_to(alpha[:, :1], (SUB, p.lanes))
@@ -441,6 +448,7 @@
         r0 = right[i + 1]
         r = r0 - alpha * (r0 + a[i + 1])
         a[i + 1] = r
+        put(p, sheet, i, r)
         return sums[0] + r * r, sums[1] + r * r0
     zero = jnp.zeros((SUB, p.lanes), jnp.float32)
     rr1, rb = lax.fori_loop(0, p.step, cut, (zero, zero), unroll=p.unroll)
@@ -448,7 +456,6 @@
     own = own_lanes(p)
     rr1 = jnp.sum(jnp.where(own, rr1, 0.0))
     rb = jnp.sum(jnp.where(own, rb, 0.0))
-    to_sheet(p, a, sheet)
     unflip(p, sheet, rows_resid, p.nlon)
     leave = pltpu.make_async_copy(rows_resid, store, sem.at[3])
     leave.start()
@@ -518,12 +525,15 @@
     return rr1, beta, rr1 + beta * (2.0 * rb + beta * rr)
 
 
-def test_kernel(p, weight, total, mine, scal, part):
+def test_kernel(p, weight, total, mine, scal, part, held, sem):
     at = lax.axis_index("mem") % 2 * p.half
+    load = pltpu.make_async_copy(total.at[pl.ds(at, p.half)], held, sem)
+    load.start()
     beta = scalars(p, mine, scal)[1]
     acc = jnp.zeros((p.rows, p.nlon), jnp.float32)
+    load.wait()
     for k in range(p.half):
-        t = mine[k, :, : p.nlon] + beta * total[at + k]
+        t = mine[k, :, : p.nlon] + beta * held[k]
         acc = acc + weight[jnp.minimum(at + k, p.fields - 1)] * t * t
     acc = jnp.broadcast_to(jnp.sum(acc, axis=(0, 1), keepdims=True), part.shape[1:])
     for k in range(part.shape[0]):
@@ -534,15 +544,22 @@
     copies = 1 if p.groups > 1 else p.mem * p.lat
     return pl.pallas_call(
         functools.partial(test_kernel, p),
-        in_specs=vmem(4),
+        in_specs=vmem(1) + hbm(1) + vmem(2),
         out_specs=vmem(1)[0],
         out_shape=jax.ShapeDtypeStruct((copies, SUB, LANES), jnp.float32),
+        scratch_shapes=[
+            pltpu.VMEM((p.half, p.rows, p.nlon), jnp.float32),
+            pltpu.SemaphoreType.DMA(()),
+        ],
         compiler_params=ROOM,
         name="last_sums",
-    )(weight, total, mine, scal)
-
-
-def last_kernel(p, total, mine, other, scal, ahead, q, right, resid, grown, control):
+    )(weight, pltpu.with_memory_space_constraint(total, pltpu.HBM), mine, scal)
+
+
+def last_kernel(p, total, mine, other, scal, ahead, q, right, resid, grown, control, *refs):
+    held, gbuf, cbuf, sem = refs
+    load = pltpu.make_async_copy(total, held, sem.at[0])
+    load.start()
     core = lax.axis_index("mem") % 2
     rr1, beta, length = scalars(p, mine, scal)
     every = q[0]
@@ -552,27 +569,46 @@
     step1 = ahead[:1, :1]
     step2 = rr1 / (length + every)
     near = step1 + step2 * beta
+    moves = []
+    cuts = (0, p.members // 2, p.members)
+    for n in range(2):
+        for m in range(cuts[n], cuts[n + 1]):
+            cbuf[m] = near * right[m] + step2 * resid[m]
+        rows = pl.ds(cuts[n], cuts[n + 1] - cuts[n])
+        moves.append(pltpu.make_async_copy(cbuf.at[rows], control.at[rows], sem.at[1 + n]))
+        moves[-1].start()
+    load.wait()
     for half, at in ((mine, core * p.half), (other, (1 - core) * p.half)):
         for k in range(p.half):
-            @pl.when(at + k < p.fields)
-            def _():
-                grown[at + k] = near * total[at + k] + step2 * half[k, :, : p.nlon]
-    for m in range(p.members):
-        control[m] = near * right[m] + step2 * resid[m]
+            gbuf[at + k] = near * held[at + k] + step2 * half[k, :, : p.nlon]
+    moves.append(pltpu.make_async_copy(gbuf.at[pl.ds(0, p.fields)], grown, sem.at[3]))
+    moves[-1].start()
+    for move in moves:
+        move.wait()
 
 
 def last(p, total, mine, other, scal, ahead, q, right, resid):
+    shape = (2 * p.half, p.rows, p.nlon)
     return pl.pallas_call(
         functools.partial(last_kernel, p),
-        in_specs=vmem(8),
-        out_specs=vmem(2),
+        in_specs=hbm(1) + vmem(7),
+        out_specs=hbm(2),
         out_shape=[
-            jax.ShapeDtypeStruct((p.fields, p.rows, p.nlon), jnp.float32),
-            jax.ShapeDtypeStruct((p.members, p.rows, p.nlon), jnp.float32),
+            pltpu.HBM((p.fields, p.rows, p.nlon), jnp.float32),
+            pltpu.HBM((p.members, p.rows, p.nlon), jnp.float32),
+        ],
+        scratch_shapes=[
+            pltpu.VMEM(shape, jnp.float32),
+            pltpu.VMEM(shape, jnp.float32),
+            pltpu.VMEM((p.members, p.rows, p.nlon), jnp.float32),
+            pltpu.SemaphoreType.DMA((4,)),
         ],
         compiler_params=ROOM,
         name="last_update",
-    )(total, mine, other, scal, ahead, q, right, resid)
+    )(
+        pltpu.with_memory_space_constraint(total, pltpu.HBM),
+        mine, other, scal, ahead, q, right, resid,
+    )
 
 
 def swap(p, x, axis, bit, count):

time: 201 us -> 197 us (0.980)
  Pallas kernels: 38.3 us -> 36.2 us
  transfers between devices with their start and end apart: 12 -> 12, of which waited for: 10 -> 11; matrix products, arithmetic and copies ran while one was open for 0% -> 0% of each run, Pallas kernels for 6% -> 7%
where the time goes in v6:
time: 197 us; the launch traced here: 196 us
  blocking collectives  84 us (43%)
  waiting for transfers between devices  50.2 us (25%)
  Pallas kernels  36.2 us (18%)
  starting transfers between devices  23 us (12%)
    all_to_all x3, blocking collectives, turn(): return lax.all_to_all(x, 'lat', 0, 0)  72.7 us
    ppermute x8, waiting for transfers between devices, swap(): return lax.ppermute(x, axis, [(i, i ^ bit) for i in range(count)])  35.6 us
    all_to_all x4, starting transfers between devices, turn(): return lax.all_to_all(x, 'lat', 0, 0)  18.1 us
    all_to_all x4, waiting for transfers between devices, turn(): return lax.all_to_all(x, 'lat', 0, 0)  14.6 us
    all_to_all x1, blocking collectives, per_device(): lax.all_to_all(q, ('mem', 'lat'), 0, 0)  11.2 us
    pallas_call x1, Pallas kernels, second_half(): pl.pallas_call(functools.partial(second_kernel, p), in_specs=vmem(2) + hb...  10.8 us
    pallas_call x1, Pallas kernels, first_half(): pl.pallas_call(functools.partial(first_kernel, p), in_specs=vmem(3), out_...  10.2 us
    pallas_call x2, Pallas kernels, forward(): pl.pallas_call(functools.partial(forward_kernel, p), in_specs=hbm(1) + vm...  6.12 us
  transfers between devices with their start and end apart: 12, of which 11 were waited for; matrix products, arithmetic and copies ran while one was open for 0% of the time, Pallas kernels for 7%

profile of v6, /device:TPU:0, one launch (start us, length us, event | category | flops | bytes accessed | tf_op | source)
XLA Modules:
  0.0 195.9 jit_solution(4717288107351968711)
XLA Ops:
  0.6 0.7 fusion.1
  1.4 0.7 broadcast_in_dim.4
  2.1 7.3 %all-to-all-start.1 = ((f32[8,2,8,384]{3,2,1,0:T(8,128)}), f32[8,2,8,384]{3,2,1,0:T(8,128)S(1)}, u32[]{:S(2)}, u32[]{:S(2)}) async-start(f32[8,2,8,384]{3,2,1,0:T(8,128)} %broadcast_in_dim.4), calls=%async_computation.1 | async-start | bytes 393216 | tf_op jit(solution)/shard_map/all_to_all | solution.py:620
  9.4 4.2 %adjoint_first.1 = f32[8,2,8,1536]{3,2,1,0:T(8,128)} custom-call(bf16[16,15,8,1440]{3,2,1,0:T(8,128)(2,1)} %bitcast.20, f32[15,8,1440]{2,1,0:T(8,128)} %bitcast.12, f32[15,8,1440]{2,1,0:T(8,128)} %bitcast.23), custom_call_target="tpu_custom_call" | custom-call | flops 5529600 | bytes 5529600 | tf_op jit(solution)/shard_map/adjoint_first/pallas_call | solution.py:95
  13.6 3.8 %all-to-all-done.1 = f32[8,2,8,384]{3,2,1,0:T(8,128)S(1)} async-done(((f32[8,2,8,384]{3,2,1,0:T(8,128)}), f32[8,2,8,384]{3,2,1,0:T(8,128)S(1)}, u32[]{:S(2)}, u32[]{:S(2)}) %all-to-all-start.1) | async-done | bytes 196640 | tf_op jit(solution)/shard_map/all_to_all | solution.py:620
  17.3 3.5 %all-to-all-start = ((f32[8,2,8,1536]{3,2,1,0:T(8,128)}), f32[8,2,8,1536]{3,2,1,0:T(8,128)S(1)}, u32[]{:S(2)}, u32[]{:S(2)}) async-start(f32[8,2,8,1536]{3,2,1,0:T(8,128)} %adjoint_first.1), calls=%async_computation | async-start | bytes 1572864 | tf_op jit(solution)/shard_map/all_to_all | solution.py:620
  20.9 0.1 collective-permute-start
  21.0 1.4 collective-permute-done
  22.4 1.6 collective-permute-start.1
  24.0 9.7 %collective-permute-done.1.far = f32[2,8,2,8,384]{4,3,2,1,0:T(8,128)S(1)} collective-permute-done((f32[2,8,2,8,384]{4,3,2,1,0:T(8,128)S(1)}, f32[2,8,2,8,384]{4,3,2,1,0:T(8,128)S(1)}, u32[]{:S(2)}, u32[]{:S(2)}) %collective-permute-start.1) | collective-permute-done | bytes 393248 | tf_op jit(solution)/shard_map/ppermute | solution.py:615
  33.7 6.8 %all-to-all-done.got = f32[8,2,8,1536]{3,2,1,0:T(8,128)S(1)} async-done(((f32[8,2,8,1536]{3,2,1,0:T(8,128)}), f32[8,2,8,1536]{3,2,1,0:T(8,128)S(1)}, u32[]{:S(2)}, u32[]{:S(2)}) %all-to-all-start) | async-done | bytes 786464 | tf_op jit(solution)/shard_map/all_to_all | solution.py:620
  40.5 10.2 %smooth_first.1 = (f32[8,2,8,1536]{3,2,1,0:T(8,128)S(1)}, f32[8,2,8,1440]{3,2,1,0:T(8,128)}, f32[182,8,128]{2,1,0:T(8,128)}, f32[182,8,128]{2,1,0:T(8,128)}, f32[182,8,128]{2,1,0:T(8,128)}) custom-call(f32[8,2,8,1536]{3,2,1,0:T(8,128)S(1)} %all-to-all-done.got, f32[2,8,2,8,384]{4,3,2,1,0:T(8,128)S(1)} %pad_maximum_fusion.near, ...), custom_call_target="tpu_custom_call" | custom-call | tf_op jit(solution)/shard_map/smooth_first/pallas_call | solution.py:492
  50.7 0.0 copy-start
  50.7 23.7 %all_to_all.40 = f32[8,2,8,1536]{3,2,1,0:T(8,128)S(1)} all-to-all(f32[8,2,8,1536]{3,2,1,0:T(8,128)S(1)} %get-tuple-element.28), channel_id=1, replica_groups=mesh['mem'=4,'lat'=8] {'lat'}, dimensions={0} | all-to-all | bytes 1572864 | tf_op jit(solution)/shard_map/all_to_all | solution.py:620
  74.4 3.6 %all-to-all-start.3 = ((f32[8,2,8,1440]{3,2,1,0:T(8,128)}), f32[8,2,8,1440]{3,2,1,0:T(8,128)S(1)}, u32[]{:S(2)}, u32[]{:S(2)}) async-start(f32[8,2,8,1440]{3,2,1,0:T(8,128)} %get-tuple-element.36), calls=%async_computation.3 | async-start | bytes 1572864 | tf_op jit(solution)/shard_map/return_first/all_to_all | solution.py:620
  78.0 3.0 %forward.2 = (f32[8,8,1536]{2,1,0:T(8,128)S(1)}, f32[8,8,1536]{2,1,0:T(8,128)S(1)}, bf16[16,3,5,8,1440]{4,3,2,1,0:T(8,128)(2,1)S(1)}) custom-call(bf16[16,3,5,8,1440]{4,3,2,1,0:T(8,128)(2,1)} %perturb.3, f32[16,8,1536]{2,1,0:T(8,128)S(1)} %bitcast.16), custom_call_target="tpu_custom_call" | custom-call | flops 5529600 | bytes 5529600 | tf_op jit(solution)/shard_map/map_first/forward/pallas_call | solution.py:235
  81.0 0.1 collective-permute-start.2
  81.1 1.7 collective-permute-done.2
  82.8 0.1 add.23
  82.9 1.6 collective-permute-start.3
  84.5 9.7 %collective-permute-done.3 = f32[8,8,1536]{2,1,0:T(8,128)S(1)} collective-permute-done((f32[8,8,1536]{2,1,0:T(8,128)S(1)}, f32[8,8,1536]{2,1,0:T(8,128)S(1)}, u32[]{:S(2)}, u32[]{:S(2)}) %collective-permute-start.3) | collective-permute-done | bytes 393248 | tf_op jit(solution)/shard_map/ppermute | solution.py:615
  94.2 0.1 collective-permute-start.4
  94.2 1.7 collective-permute-done.4.other
  96.0 0.0 copy-done
  96.0 1.6 adjoint_second.1
  97.5 0.4 all-to-all-done.3
  97.9 25.8 %all_to_all.41.got = f32[8,2,8,1536]{3,2,1,0:T(8,128)S(1)} all-to-all(f32[8,2,8,1536]{3,2,1,0:T(8,128)S(1)} %get-tuple-element.37), channel_id=1, replica_groups=mesh['mem'=4,'lat'=8] {'lat'}, dimensions={0} | all-to-all | bytes 1572864 | tf_op jit(solution)/shard_map/all_to_all | solution.py:620
  123.7 10.8 %smooth_second.1 = (f32[8,2,8,1536]{3,2,1,0:T(8,128)S(1)}, f32[8,2,8,1440]{3,2,1,0:T(8,128)}, f32[8,128]{1,0:T(8,128)S(1)}) custom-call(f32[8,2,8,1536]{3,2,1,0:T(8,128)S(1)} %all_to_all.41.got, f32[2,8,128]{2,1,0:T(8,128)S(1)} %get-tuple-element.38.scal, f32[182,8,128]{2,1,0:T(8,128)} %get-tuple-element.39.refs_0_, ...), custom_call_target="tpu_custom_call" | custom-call | tf_op jit(solution)/shard_map/smooth_second/pallas_call | solution.py:505
  134.5 23.2 %all_to_all.42 = f32[8,2,8,1536]{3,2,1,0:T(8,128)S(1)} all-to-all(f32[8,2,8,1536]{3,2,1,0:T(8,128)S(1)} %get-tuple-element.42), channel_id=1, replica_groups=mesh['mem'=4,'lat'=8] {'lat'}, dimensions={0} | all-to-all | bytes 1572864 | tf_op jit(solution)/shard_map/all_to_all | solution.py:620
  157.8 3.6 %all-to-all-start.6 = ((f32[8,2,8,1440]{3,2,1,0:T(8,128)}), f32[8,2,8,1440]{3,2,1,0:T(8,128)S(1)}, u32[]{:S(2)}, u32[]{:S(2)}) async-start(f32[8,2,8,1440]{3,2,1,0:T(8,128)} %get-tuple-element.47), calls=%async_computation.6 | async-start | bytes 1572864 | tf_op jit(solution)/shard_map/return_second/all_to_all | solution.py:620
  161.3 3.1 %forward.3 = (f32[8,8,1536]{2,1,0:T(8,128)S(1)}, f32[8,8,1536]{2,1,0:T(8,128)S(1)}) custom-call(bf16[16,3,5,8,1440]{4,3,2,1,0:T(8,128)(2,1)} %perturb.3, f32[16,8,1536]{2,1,0:T(8,128)S(1)} %bitcast.17), custom_call_target="tpu_custom_call" | custom-call | flops 5529600 | bytes 5529600 | tf_op jit(solution)/shard_map/map_second/forward/pallas_call | solution.py:235
  164.5 0.1 collective-permute-start.5
  164.6 1.7 collective-permute-done.5
  166.3 0.1 add.25
  166.3 1.6 collective-permute-start.6
  167.9 9.7 %collective-permute-done.6 = f32[8,8,1536]{2,1,0:T(8,128)S(1)} collective-permute-done((f32[8,8,1536]{2,1,0:T(8,128)S(1)}, f32[8,8,1536]{2,1,0:T(8,128)S(1)}, u32[]{:S(2)}, u32[]{:S(2)}) %collective-permute-start.6) | collective-permute-done | bytes 393248 | tf_op jit(solution)/shard_map/ppermute | solution.py:615
  177.6 3.6 %all-to-all-done.6 = f32[8,2,8,1440]{3,2,1,0:T(8,128)S(1)} async-done(((f32[8,2,8,1440]{3,2,1,0:T(8,128)}), f32[8,2,8,1440]{3,2,1,0:T(8,128)S(1)}, u32[]{:S(2)}, u32[]{:S(2)}) %all-to-all-start.6) | async-done | bytes 737312 | tf_op jit(solution)/shard_map/return_second/all_to_all | solution.py:620
  181.2 0.0 collective-permute-start.7
  181.2 1.3 last_sums.1
  182.5 11.2 %all_to_all.43.q = f32[32,8,128]{2,1,0:T(8,128)S(1)} all-to-all(f32[32,8,128]{2,1,0:T(8,128)S(1)} %last_sums.1), channel_id=1, replica_groups=mesh['mem'=4,'lat'=8] {'mem','lat'}, dimensions={0} | all-to-all | bytes 262144 | tf_op jit(solution)/shard_map/all_to_all | solution.py:696
  193.7 0.0 collective-permute-done.7.other
  193.7 2.1 %last_update.1 = (f32[15,8,1440]{2,1,0:T(8,128)}, f32[16,8,1440]{2,1,0:T(8,128)}) custom-call(f32[16,8,1440]{2,1,0:T(8,128)} %get-tuple-element.34.total, f32[8,8,1536]{2,1,0:T(8,128)S(1)} %add.26.mine, f32[8,8,1536]{2,1,0:T(8,128)S(1)} %collective-permute-done.7.other, f32[2,8,128]{2,1,0:T(8,128)S(1)} %get-tuple-element.38.scal, ...), custom_call_target="tpu_custom_call" | custom-call | tf_op jit(solution)/shard_map/last_update/pallas_call | solution.py:592
  (3 shorter events, 0.1 us)
Async XLA Ops:
  2.1 15.3 %all-to-all-start.1 = ((f32[8,2,8,384]{3,2,1,0:T(8,128)}), f32[8,2,8,384]{3,2,1,0:T(8,128)S(1)}, u32[]{:S(2)}, u32[]{:S(2)}) async-start(f32[8,2,8,384]{3,2,1,0:T(8,128)} %broadcast_in_dim.4), calls=%async_computation.1 | async-start | bytes 393216 | tf_op jit(solution)/shard_map/all_to_all | solution.py:620
  17.3 23.1 %all-to-all-start = ((f32[8,2,8,1536]{3,2,1,0:T(8,128)}), f32[8,2,8,1536]{3,2,1,0:T(8,128)S(1)}, u32[]{:S(2)}, u32[]{:S(2)}) async-start(f32[8,2,8,1536]{3,2,1,0:T(8,128)} %adjoint_first.1), calls=%async_computation | async-start | bytes 1572864 | tf_op jit(solution)/shard_map/all_to_all | solution.py:620
  20.9 1.5 collective-permute-start
  22.4 11.2 %collective-permute-start.1 = (f32[2,8,2,8,384]{4,3,2,1,0:T(8,128)S(1)}, f32[2,8,2,8,384]{4,3,2,1,0:T(8,128)S(1)}, u32[]{:S(2)}, u32[]{:S(2)}) collective-permute-start(f32[2,8,2,8,384]{4,3,2,1,0:T(8,128)S(1)} %pad_maximum_fusion.near), channel_id=1, source_target_pairs={{0,16},{8,24},{16,0},{24,8},{1,17},{9,25},{17,1},{25,9},{2,18},{10... | collective-permute-start | bytes 1179656 | tf_op jit(solution)/shard_map/ppermute | solution.py:615
  50.7 45.3 %copy-start = (f32[3,5,8,1440]{3,2,1,0:T(8,128)S(1)}, f32[3,5,8,1440]{3,2,1,0:T(8,128)}, u32[]{:S(2)}) copy-start(f32[3,5,8,1440]{3,2,1,0:T(8,128)} %param.7) | copy-start | bytes 2073604
  74.4 23.5 %all-to-all-start.3 = ((f32[8,2,8,1440]{3,2,1,0:T(8,128)}), f32[8,2,8,1440]{3,2,1,0:T(8,128)S(1)}, u32[]{:S(2)}, u32[]{:S(2)}) async-start(f32[8,2,8,1440]{3,2,1,0:T(8,128)} %get-tuple-element.36), calls=%async_computation.3 | async-start | bytes 1572864 | tf_op jit(solution)/shard_map/return_first/all_to_all | solution.py:620
  81.0 1.8 collective-permute-start.2
  82.9 11.2 %collective-permute-start.3 = (f32[8,8,1536]{2,1,0:T(8,128)S(1)}, f32[8,8,1536]{2,1,0:T(8,128)S(1)}, u32[]{:S(2)}, u32[]{:S(2)}) collective-permute-start(f32[8,8,1536]{2,1,0:T(8,128)S(1)} %add.23), channel_id=1, source_target_pairs={{0,16},{8,24},{16,0},{24,8},{1,17},{9,25},{17,1},{25,9},{2,18},{10... | collective-permute-start | bytes 1179656 | tf_op jit(solution)/shard_map/ppermute | solution.py:615
  94.2 1.8 collective-permute-start.4
  157.8 23.4 %all-to-all-start.6 = ((f32[8,2,8,1440]{3,2,1,0:T(8,128)}), f32[8,2,8,1440]{3,2,1,0:T(8,128)S(1)}, u32[]{:S(2)}, u32[]{:S(2)}) async-start(f32[8,2,8,1440]{3,2,1,0:T(8,128)} %get-tuple-element.47), calls=%async_computation.6 | async-start | bytes 1572864 | tf_op jit(solution)/shard_map/return_second/all_to_all | solution.py:620
  164.5 1.8 collective-permute-start.5
  166.3 11.2 %collective-permute-start.6 = (f32[8,8,1536]{2,1,0:T(8,128)S(1)}, f32[8,8,1536]{2,1,0:T(8,128)S(1)}, u32[]{:S(2)}, u32[]{:S(2)}) collective-permute-start(f32[8,8,1536]{2,1,0:T(8,128)S(1)} %add.25), channel_id=1, source_target_pairs={{0,16},{8,24},{16,0},{24,8},{1,17},{9,25},{17,1},{25,9},{2,18},{10... | collective-permute-start | bytes 1179656 | tf_op jit(solution)/shard_map/ppermute | solution.py:615
  181.2 12.6 %collective-permute-start.7 = (f32[8,8,1536]{2,1,0:T(8,128)S(1)}, f32[8,8,1536]{2,1,0:T(8,128)S(1)}, u32[]{:S(2)}, u32[]{:S(2)}) collective-permute-start(f32[8,8,1536]{2,1,0:T(8,128)S(1)} %add.26.mine), channel_id=1, source_target_pairs={{0,8},{8,0},{16,24},{24,16},{1,9},{9,1},{17,25},{25,17},{2,10},{10... | collective-permute-start | bytes 1179656 | tf_op jit(solution)/shard_map/ppermute | solution.py:615
